TPU v7x, 32 devices: a whole 2x2x4 slice. The times are simulated.
32 devices in a mesh: dp: 8 (over z, x), tensor: 4 (over y, core).
Axes of the slice: x: 2, y: 2, z: 4, core: 2. Of those that a mesh axis runs over, the one named last changes fastest.
Arguments:
- tokens: bfloat16 [8192, 2048], P(('dp', 'tensor')), may hold values from -6 to 6
- out_grad: bfloat16 [8192, 2048], P(('dp', 'tensor')), may hold values from -6 to 6
- segments: int32 [8, 1024], P('dp'), may hold values from 0 to 7, never falling along the last dimension, each value on 1 to 341 neighbouring positions
- ln_gain: float32 [2048], replicated, may hold values from 0.1 to 1.9
- ln_bias: float32 [2048], replicated, may hold values from -3 to 3
- qkv_weight: bfloat16 [2048, 3, 2048], P('dp', None, 'tensor'), may hold values from -0.125 to 0.125
- qkv_bias: float32 [3, 2048], P(None, 'tensor'), may hold values from -3 to 3
- dense_weight: bfloat16 [2048, 2048], P('dp', 'tensor'), may hold values from -0.75 to 0.75
- dense_bias: float32 [2048], replicated, may hold values from -2 to 2
- fc1_weight: bfloat16 [2048, 8192], P('dp', 'tensor'), may hold values from -0.125 to 0.125
- fc1_bias: float32 [8192], P('tensor'), may hold values from -3 to 3
- fc2_weight: bfloat16 [2048, 8192], P('dp', 'tensor'), may hold values from -0.0625 to 0.0625
- fc2_bias: float32 [2048], replicated, may hold values from -2 to 2
Outputs:
- output: bfloat16 [8192, 2048], P(('dp', 'tensor'))
- input_grad: bfloat16 [8192, 2048], P(('dp', 'tensor'))
- ln_gain_grad: float32 [2048], replicated
- ln_bias_grad: float32 [2048], replicated
- qkv_weight_grad: float32 [2048, 3, 2048], P('dp', None, 'tensor')
- qkv_bias_grad: float32 [3, 2048], P(None, 'tensor')
- dense_weight_grad: float32 [2048, 2048], P('dp', 'tensor')
- dense_bias_grad: float32 [2048], replicated
- fc1_weight_grad: float32 [2048, 8192], P('dp', 'tensor')
- fc1_bias_grad: float32 [8192], P('tensor')
- fc2_weight_grad: float32 [2048, 8192], P('dp', 'tensor')
- fc2_bias_grad: float32 [2048], replicated
Inputs may be any that keep to these rules, and one draw needn't show every extreme that they name: `segments`: segment numbers never fall along a sequence; a segment holds at most one third of 1024 tokens.
All inputs are finite; a program needn't handle non-finite values.
Results may differ from a plain program's by a relative error of at most 0.0099.
Values may be sent and summed in bfloat16 or wider, within the bound.
No kernel may reach another device: no remote copies, remote signals or barrier semaphores. Data moves between devices by JAX's collectives and lax.ppermute only.
A program may use at most 256 MiB of HBM per device.

v0:
```python
import math

import jax
import jax.numpy as jnp
from jax import lax
from jax.sharding import PartitionSpec as P

D = 2048
H = 32
FF = 8192
ROT = 32
LEN = 1024
QB = 512


EPSILON = 1e-05
GELU_SCALE = math.sqrt(2.0 / math.pi)
GELU_CUBIC = 0.044715
MASK_VALUE = -1e30
ROPE_BASE = 10000.0


def gelu_value(pre_gelu):
    tanh_arg = GELU_SCALE * (pre_gelu + GELU_CUBIC * pre_gelu * pre_gelu * pre_gelu)
    return 0.5 * pre_gelu * (1.0 + jnp.tanh(tanh_arg))


def gelu_slope(pre_gelu):
    tanh_arg = GELU_SCALE * (pre_gelu + GELU_CUBIC * pre_gelu * pre_gelu * pre_gelu)
    tangent = jnp.tanh(tanh_arg)
    return 0.5 * (1.0 + tangent) + 0.5 * pre_gelu * (1.0 - tangent * tangent) * GELU_SCALE * (
        1.0 + 3.0 * GELU_CUBIC * pre_gelu * pre_gelu
    )


def normalize_rows(token_rows):
    values = token_rows.astype(jnp.float32)
    centered = values - jnp.mean(values, axis=-1, keepdims=True)
    inv_std = lax.rsqrt(jnp.mean(centered * centered, axis=-1, keepdims=True) + EPSILON)
    return (centered * inv_std, inv_std)


def rotary_tables(row_total, period, rotated):
    half_rot = rotated // 2
    positions = (jnp.arange(row_total) % period).astype(jnp.float32)
    inverse = ROPE_BASE ** (-(2.0 * jnp.arange(half_rot).astype(jnp.float32)) / rotated)
    angles = positions[:, None] * inverse[None, :]
    return (jnp.cos(angles)[:, None, :], jnp.sin(angles)[:, None, :])


def rotate_heads(heads, cosine, sine, rotated):
    half_rot = rotated // 2
    former = heads[..., :half_rot]
    latter = heads[..., half_rot:rotated]
    return jnp.concatenate(
        [former * cosine - latter * sine, latter * cosine + former * sine, heads[..., rotated:]],
        axis=-1,
    )


def unrotate_heads(grads, cosine, sine, rotated):
    half_rot = rotated // 2
    former = grads[..., :half_rot]
    latter = grads[..., half_rot:rotated]
    return jnp.concatenate(
        [former * cosine + latter * sine, latter * cosine - former * sine, grads[..., rotated:]],
        axis=-1,
    )


def contract_last(left, right):
    return lax.dot_general(
        left, right, (((1,), (1,)), ((), ())), preferred_element_type=jnp.float32
    )


def contract_first(left, right):
    return lax.dot_general(
        left, right, (((0,), (0,)), ((), ())), preferred_element_type=jnp.float32
    )


def to_heads(flat, head_dim):
    rows_all = flat.shape[0]
    head_count = flat.shape[1] // head_dim
    return (
        flat.reshape(rows_all, head_count, head_dim)
        .transpose(1, 0, 2)
        .reshape(head_count, rows_all // LEN, LEN, head_dim)
    )


def from_heads(stacked):
    head_count, seqs_here, length, head_dim = stacked.shape
    return (
        stacked.reshape(head_count, seqs_here * length, head_dim)
        .transpose(1, 0, 2)
        .reshape(seqs_here * length, head_count * head_dim)
    )


def masked_scores(query_block, key_heads, segment_ids, block_start, block_rows, score_scale):
    scores = (
        jnp.einsum("sqd,skd->sqk", query_block, key_heads, preferred_element_type=jnp.float32)
        * score_scale
    )
    query_index = block_start + jnp.arange(block_rows)
    key_index = jnp.arange(key_heads.shape[1])
    same_doc = (
        segment_ids[:, block_start : block_start + block_rows, None] == segment_ids[:, None, :]
    )
    allowed = same_doc & (key_index[None, None, :] <= query_index[None, :, None])
    return jnp.where(allowed, scores, MASK_VALUE)


def attend_heads(query_heads, key_heads, value_heads, segment_ids, score_scale, block_rows):
    length = query_heads.shape[1]
    outputs = []
    log_totals = []
    for block_start in range(0, length, block_rows):
        query_block = query_heads[:, block_start : block_start + block_rows]
        scores = masked_scores(
            query_block, key_heads, segment_ids, block_start, block_rows, score_scale
        )
        row_max = jnp.max(scores, axis=-1, keepdims=True)
        log_total = row_max + jnp.log(jnp.sum(jnp.exp(scores - row_max), axis=-1, keepdims=True))
        probs_low = jnp.exp(scores - log_total).astype(jnp.bfloat16)
        outputs.append(
            jnp.einsum(
                "sqk,skd->sqd", probs_low, value_heads, preferred_element_type=jnp.float32
            ).astype(jnp.bfloat16)
        )
        log_totals.append(log_total[..., 0])
    return (jnp.concatenate(outputs, axis=1), jnp.concatenate(log_totals, axis=1))


def attend_heads_grad(
    query_heads,
    key_heads,
    value_heads,
    log_totals,
    grad_heads,
    segment_ids,
    score_scale,
    block_rows,
):
    length = query_heads.shape[1]
    query_grads = []
    key_grad = jnp.zeros(key_heads.shape, jnp.float32)
    value_grad = jnp.zeros(value_heads.shape, jnp.float32)
    for block_start in range(0, length, block_rows):
        query_block = query_heads[:, block_start : block_start + block_rows]
        grad_block = grad_heads[:, block_start : block_start + block_rows]
        total_block = log_totals[:, block_start : block_start + block_rows]
        scores = masked_scores(
            query_block, key_heads, segment_ids, block_start, block_rows, score_scale
        )
        probs_full = jnp.exp(scores - total_block[..., None])
        probs_low = probs_full.astype(jnp.bfloat16)
        value_grad = value_grad + jnp.einsum(
            "sqk,sqd->skd", probs_low, grad_block, preferred_element_type=jnp.float32
        )
        prob_grad = jnp.einsum(
            "sqd,skd->sqk", grad_block, value_heads, preferred_element_type=jnp.float32
        )
        row_dot = jnp.sum(probs_full * prob_grad, axis=-1, keepdims=True)
        score_grad = (probs_full * (prob_grad - row_dot) * score_scale).astype(jnp.bfloat16)
        query_grads.append(
            jnp.einsum("sqk,skd->sqd", score_grad, key_heads, preferred_element_type=jnp.float32)
        )
        key_grad = key_grad + jnp.einsum(
            "sqk,sqd->skd", score_grad, query_block, preferred_element_type=jnp.float32
        )
    return (jnp.concatenate(query_grads, axis=1), key_grad, value_grad)


def body(
    tokens,
    out_grad,
    segments,
    ln_gain,
    ln_bias,
    qkv_weight,
    qkv_bias,
    dense_weight,
    dense_bias,
    fc1_weight,
    fc1_bias,
    fc2_weight,
    fc2_bias,
):
    head_dim = D // H
    score_scale = 1.0 / math.sqrt(head_dim)
    x_hat, inv_std = normalize_rows(tokens)
    normed = (x_hat * ln_gain + ln_bias).astype(jnp.bfloat16)
    whole_normed = lax.all_gather(normed, "tensor", axis=0, tiled=True)
    qkv_full, dense_full, fc1_full, fc2_full = (
        lax.all_gather(qkv_weight, "dp", axis=0, tiled=True),
        lax.all_gather(dense_weight, "dp", axis=0, tiled=True),
        lax.all_gather(fc1_weight, "dp", axis=0, tiled=True),
        lax.all_gather(fc2_weight, "dp", axis=0, tiled=True),
    )
    rows_all = whole_normed.shape[0]
    local_width = qkv_full.shape[2]
    hidden_here = fc1_full.shape[1]
    heads_here = local_width // head_dim
    qkv_matrix = qkv_full.reshape(D, 3 * local_width)
    projected = (
        jnp.dot(whole_normed, qkv_matrix, preferred_element_type=jnp.float32).reshape(
            rows_all, 3, local_width
        )
        + qkv_bias[None]
    )
    cosine, sine = rotary_tables(rows_all, LEN, ROT)
    query_rows = (
        rotate_heads(projected[:, 0].reshape(rows_all, heads_here, head_dim), cosine, sine, ROT)
        .astype(jnp.bfloat16)
        .reshape(rows_all, local_width)
    )
    key_rows = (
        rotate_heads(projected[:, 1].reshape(rows_all, heads_here, head_dim), cosine, sine, ROT)
        .astype(jnp.bfloat16)
        .reshape(rows_all, local_width)
    )
    value_rows = projected[:, 2].astype(jnp.bfloat16)
    query_heads = to_heads(query_rows, head_dim)
    key_heads = to_heads(key_rows, head_dim)
    value_heads = to_heads(value_rows, head_dim)

    def head_forward(members):
        return attend_heads(members[0], members[1], members[2], segments, score_scale, QB)

    head_outputs, log_totals = lax.map(head_forward, (query_heads, key_heads, value_heads))
    attended = from_heads(head_outputs)
    pre_gelu = jnp.dot(whole_normed, fc1_full, preferred_element_type=jnp.float32) + fc1_bias
    activated = gelu_value(pre_gelu).astype(jnp.bfloat16)
    attended_part = lax.slice_in_dim(attended, 0, tokens.shape[0] * lax.axis_size("tensor"), axis=0)
    branch = lax.psum_scatter(
        contract_last(attended_part, dense_full) + contract_last(activated, fc2_full),
        "tensor",
        scatter_dimension=0,
        tiled=True,
    )
    output = (tokens.astype(jnp.float32) + branch + dense_bias + fc2_bias).astype(jnp.bfloat16)
    whole_grad = lax.all_gather(out_grad, "tensor", axis=0, tiled=True)
    pre_grad_full = jnp.dot(whole_grad, fc2_full, preferred_element_type=jnp.float32) * gelu_slope(
        pre_gelu
    )
    pre_grad = pre_grad_full.astype(jnp.bfloat16)
    attended_grad = jnp.dot(whole_grad, dense_full, preferred_element_type=jnp.float32).astype(
        jnp.bfloat16
    )
    weight_rows = qkv_weight.shape[0]

    def head_backward(members):
        return attend_heads_grad(
            members[0], members[1], members[2], members[3], members[4], segments, score_scale, QB
        )

    query_grads, key_grads, value_grads = lax.map(
        head_backward,
        (query_heads, key_heads, value_heads, log_totals, to_heads(attended_grad, head_dim)),
    )
    query_grad = unrotate_heads(
        from_heads(query_grads).reshape(rows_all, heads_here, head_dim), cosine, sine, ROT
    ).reshape(rows_all, local_width)
    key_grad = unrotate_heads(
        from_heads(key_grads).reshape(rows_all, heads_here, head_dim), cosine, sine, ROT
    ).reshape(rows_all, local_width)
    qkv_grad_full = jnp.stack([query_grad, key_grad, from_heads(value_grads)], axis=1)
    qkv_grad = qkv_grad_full.astype(jnp.bfloat16).reshape(rows_all, 3 * local_width)
    normed_grad = lax.psum_scatter(
        contract_last(qkv_grad, qkv_matrix) + contract_last(pre_grad, fc1_full),
        "tensor",
        scatter_dimension=0,
        tiled=True,
    )
    scaled = normed_grad * ln_gain
    token_grad = inv_std * (
        scaled
        - jnp.mean(scaled, axis=-1, keepdims=True)
        - x_hat * jnp.mean(scaled * x_hat, axis=-1, keepdims=True)
    )
    input_grad = (out_grad.astype(jnp.float32) + token_grad).astype(jnp.bfloat16)
    every_grad = lax.psum_scatter(
        jnp.concatenate(
            [
                contract_first(whole_normed, qkv_grad),
                contract_first(whole_grad, attended),
                contract_first(whole_normed, pre_grad),
                contract_first(whole_grad, activated),
            ],
            axis=1,
        ),
        "dp",
        scatter_dimension=0,
        tiled=True,
    )
    qkv_weight_grad = every_grad[:, : 3 * local_width]
    dense_weight_grad = every_grad[:, 3 * local_width : 4 * local_width]
    fc1_weight_grad = every_grad[:, 4 * local_width : 4 * local_width + hidden_here]
    fc2_weight_grad = every_grad[:, 4 * local_width + hidden_here :]
    tensor_pos = lax.axis_index("tensor")
    zero_index = jnp.zeros((), jnp.int32)
    qkv_bias_wide = lax.dynamic_update_slice(
        jnp.zeros((3, D), jnp.float32),
        jnp.sum(qkv_grad_full, axis=0),
        (zero_index, tensor_pos * local_width),
    )
    fc1_bias_wide = lax.dynamic_update_slice(
        jnp.zeros((FF,), jnp.float32), jnp.sum(pre_grad_full, axis=0), (tensor_pos * hidden_here,)
    )
    gain_sum, shift_sum, out_bias_sum, qkv_bias_sum, fc1_bias_sum = lax.psum(
        (
            jnp.sum(normed_grad * x_hat, axis=0),
            jnp.sum(normed_grad, axis=0),
            jnp.sum(out_grad.astype(jnp.float32), axis=0),
            qkv_bias_wide,
            fc1_bias_wide,
        ),
        ("dp", "tensor"),
    )
    qkv_bias_grad = lax.dynamic_slice(
        qkv_bias_sum, (zero_index, tensor_pos * local_width), (3, local_width)
    )
    fc1_bias_grad = lax.dynamic_slice_in_dim(fc1_bias_sum, tensor_pos * hidden_here, hidden_here, 0)
    return (
        output,
        input_grad,
        gain_sum,
        shift_sum,
        qkv_weight_grad.reshape(weight_rows, 3, local_width),
        qkv_bias_grad,
        dense_weight_grad,
        out_bias_sum,
        fc1_weight_grad,
        fc1_bias_grad,
        fc2_weight_grad,
        out_bias_sum,
    )


def solution(mesh):
    placed = (
        P(("dp", "tensor"), None),
        P(("dp", "tensor"), None),
        P("dp", None),
        P(),
        P(),
        P("dp", None, "tensor"),
        P(None, "tensor"),
        P("dp", "tensor"),
        P(),
        P("dp", "tensor"),
        P("tensor"),
        P("dp", "tensor"),
        P(),
    )
    return jax.shard_map(
        body,
        mesh=mesh,
        in_specs=placed,
        out_specs=(
            P(("dp", "tensor"), None),
            P(("dp", "tensor"), None),
            P(),
            P(),
            P("dp", None, "tensor"),
            P(None, "tensor"),
            P("dp", "tensor"),
            P(),
            P("dp", "tensor"),
            P("tensor"),
            P("dp", "tensor"),
            P(),
        ),
        check_vma=False,
    )
```

profile of v0, /device:TPU:0, one launch (start us, length us, event | category | flops | bytes accessed | tf_op | source)
XLA Modules:
  0.0 1623.1 jit_solution(1283329400450513746)
XLA Ops:
  13.9 48.3 %all-gather.11.cloned.1.call-done = bf16[2048,512]{1,0:T(8,128)(2,1)} async-done(((bf16[256,512]{1,0:T(8,128)(2,1)}), bf16[2048,512]{1,0:T(8,128)(2,1)}) %all-gather.11.cloned.1.call-update) | async-done | bytes 2097168 | tf_op jit(solution)/shard_map/all_gather | solution.py:199
  62.2 34.6 %all-gather.17.cloned.1.call-done = bf16[1024,2048]{1,0:T(8,128)(2,1)} async-done(((bf16[256,2048]{1,0:T(8,128)(2,1)}), bf16[1024,2048]{1,0:T(8,128)(2,1)}) %all-gather.17.cloned.1.call-update) | async-done | bytes 4194320 | tf_op jit(solution)/shard_map/all_gather | solution.py:245
  96.8 5.2 convolution_convert_fusion.2
  103.8 94.2 %all-gather.9.cloned.1.call-done = bf16[2048,3,512]{2,0,1:T(8,128)(2,1)} async-done(((bf16[256,3,512]{2,0,1:T(8,128)(2,1)}), bf16[2048,3,512]{2,0,1:T(8,128)(2,1)}) %all-gather.9.cloned.1.call-update) | async-done | bytes 6291472 | tf_op jit(solution)/shard_map/all_gather | solution.py:198
  198.0 8.9 copy.38
  206.9 25.8 %all-gather.7.cloned.1.call-done = bf16[1024,2048]{1,0:T(8,128)(2,1)} async-done(((bf16[256,2048]{1,0:T(8,128)(2,1)}), bf16[1024,2048]{1,0:T(8,128)(2,1)}) %all-gather.7.cloned.1.call-update) | async-done | bytes 4194320 | tf_op jit(solution)/shard_map/all_gather | solution.py:196
  232.7 10.1 broadcast_add_fusion
  251.0 51.5 %while.26 = (s32[]{:T(128)}, bf16[8,1,1024,64]{2,3,1,0:T(8,128)(2,1)S(1)}, f32[8,1,1024]{2,1,0:T(1,128)S(1)}, s32[1,1024]{1,0:T(1,128)S(1)}, bf16[8,1,1024,64]{3...) while((s32[]{:T(128)}, ...), condition=%wide.region_7.8_spmd, body=%wide.region_2.7_spmd.sunk | while | flops 279249408 | bytes 14610553 | solution.py:233
  303.5 72.0 %while.27 = (s32[]{:T(128)}, f32[8,1,1024,64]{2,3,1,0:T(8,128)}, f32[8,1,1024,64]{2,3,1,0:T(8,128)}, f32[8,1,1024,64]{2,3,1,0:T(8,128)}, s32[1,1024]{1,0:T(1,128...) while((s32[]{:T(128)}, f32[8,1,1024,64]{2,3,1,0:T(8,128)}, ...), condition=%wide.region_12.13_spmd, body=%wide.region_9.12_spmd.sunk | while | flops 684916224 | bytes 41210044 | solution.py:260
  388.2 2.9 copy.46
  391.1 4.5 fusion.60
  395.6 14.5 fusion.100
  410.1 75.1 %all-gather.15.cloned.1.call-done = bf16[2048,2048]{1,0:T(8,128)(2,1)} async-done(((bf16[256,2048]{1,0:T(8,128)(2,1)}), bf16[2048,2048]{1,0:T(8,128)(2,1)}) %all-gather.15.cloned.1.call-update) | async-done | bytes 8388624 | tf_op jit(solution)/shard_map/all_gather | solution.py:201
  485.2 20.0 %fusion.99 = (f32[2048]{0:T(1024)S(1)}, bf16[1024,2048]{1,0:T(8,128)(2,1)}) fusion(f32[1024,2048]{1,0:T(8,128)} %fusion.100, f32[2048]{0:T(1024)S(1)} %copy-done.31, bf16[1024,2048]{1,0:T(8,128)(2,1)} %all-gather.17.cloned.1.call-done, bf16[2048,2048]{1,0:T(8,128)(2,1)} %all-gather.15.cloned.1.call-done), kind=kOutput, calls=%fused_computation.177 | convolution fusion | flops 8633972736 | bytes 25182208 | tf_op jit(solution)/shard_map/dot_general | solution.py:246
  505.2 11.1 fusion.85
  516.3 10.8 bitcast_add_fusion
  527.2 16.3 %fusion.91 = f32[1024,2048]{1,0:T(8,128)S(1)} fusion(bf16[2048,2048]{1,0:T(8,128)(2,1)} %all-gather.15.cloned.1.call-done, f32[1024,2048]{1,0:T(8,128)} %fusion.100, f32[2048]{0:T(1024)S(1)} %copy-done.31), kind=kOutput, calls=%fused_computation.169 | convolution fusion | flops 8610906112 | bytes 25174016 | tf_op jit(solution)/shard_map/dot_general | solution.py:72
  543.6 5.9 convolution_add_fusion.2
  549.5 4.7 copy.48
  557.7 4.4 convolution_bitcast_fusion.3
  562.0 9.1 fusion.101
  571.4 12.0 fusion.83
  583.5 12.7 convolution_bitcast_fusion.2
  597.2 3.3 fusion.77
  600.5 71.2 %reduce-scatter.4.cloned.1.call-done = f32[256,2048]{1,0:T(8,128)} async-done(((f32[1024,2048]{1,0:T(8,128)}), f32[256,2048]{1,0:T(8,128)}) %reduce-scatter.4.cloned.1.call-update) | async-done | bytes 2097168 | tf_op jit(solution)/shard_map/reduce_scatter | solution.py:238
  671.7 5.4 convert_reduce_fusion.1
  677.2 34.3 %pad_maximum_fusion = f32[2048,6144]{0,1:T(8,128)} fusion(f32[2048,2048]{0,1:T(8,128)} %convolution_bitcast_fusion.2, f32[2048,2048]{0,1:T(8,128)} %fusion.83, f32[2048,512]{0,1:T(8,128)} %convolution_bitcast_fusion.3, f32[2048,1536]{0,1:T(8,128)} %fusion.101), kind=kLoop, calls=%fused_computation.90 | loop fusion | flops 37748736 | bytes 100663296 | tf_op jit(solution)/shard_map/concatenate | solution.py:286
  711.6 90.1 %all-reduce.3.cloned.1.call-done = (f32[2048]{0:T(1024)}, f32[2048]{0:T(1024)}, f32[3,2048]{1,0:T(4,128)}, f32[2048]{0:T(1024)}, f32[8192]{0:T(1024)}) async-done(((f32[2048]{0:T(1024)}, f32[2048]{0:T(1024)}, f32[3,2048]{1,0:T(4,128)}, f32[2048]{0:T(1024)}, f32[8192]{0:T(1024)}), (f32[2048]{0:T(1024)}, f32[2048]{0:T(1024)}, f32[3,2048]{1,0:T(4,128)}, f32[2048]{0:T(1024)}, ...) | async-done | bytes 81936 | tf_op jit(solution)/shard_map/psum | solution.py:313
  804.2 793.2 %reduce-scatter.8.cloned.1.call-done = f32[256,6144]{0,1:T(8,128)} async-done(((f32[2048,6144]{0,1:T(8,128)}), f32[256,6144]{0,1:T(8,128)}) %reduce-scatter.8.cloned.1.call-update) | async-done | bytes 6291472 | tf_op jit(solution)/shard_map/reduce_scatter | solution.py:285
  1599.5 3.8 fusion.97
  1603.3 2.9 copy.52
  1608.8 3.0 copy.49
  (402 shorter events, 168.9 us)
Async XLA Ops:
  7.2 3.7 copy-start.15
  7.2 3.6 copy-start.22
  7.2 55.0 %all-gather.11.cloned.1.call-start = ((), (), s32[]{:S(2)}) async-start(), calls=%async_computation.5 | async-start | bytes 2359296 | tf_op jit(solution)/shard_map/all_gather | solution.py:199
  7.9 88.8 %all-gather.17.cloned.1.call-start = ((), (), s32[]{:S(2)}) async-start(), calls=%async_computation.9 | async-start | bytes 5242880 | tf_op jit(solution)/shard_map/all_gather | solution.py:245
  8.7 189.3 %all-gather.9.cloned.1.call-start = ((), (), s32[]{:S(2)}) async-start(), calls=%async_computation.4 | async-start | bytes 7077888 | tf_op jit(solution)/shard_map/all_gather | solution.py:198
  9.4 223.3 %all-gather.7.cloned.1.call-start = ((), (), s32[]{:S(2)}) async-start(), calls=%async_computation.3 | async-start | bytes 5242880 | tf_op jit(solution)/shard_map/all_gather | solution.py:196
  12.3 383.3 %all-gather.13.cloned.1.call-start = ((), (), s32[]{:S(2)}) async-start(), calls=%async_computation.6 | async-start | bytes 9437184 | tf_op jit(solution)/shard_map/all_gather | solution.py:200
  12.9 472.3 %all-gather.15.cloned.1.call-start = ((), (), s32[]{:S(2)}) async-start(), calls=%async_computation.7 | async-start | bytes 9437184 | tf_op jit(solution)/shard_map/all_gather | solution.py:201
  13.5 583.7 %reduce-scatter.6.cloned.1.call-start = ((), (), s32[]{:S(2)}) async-start(), calls=%async_computation.10 | async-start | bytes 10485760 | tf_op jit(solution)/shard_map/reduce_scatter | solution.py:272
  103.8 128.9 %copy-start.30 = (f32[3,512]{1,0:T(4,128)S(1)}, f32[3,512]{1,0:T(4,128)}, u32[]{:S(2)}) copy-start(f32[3,512]{1,0:T(4,128)} %param.23) | copy-start | bytes 18436
  395.6 89.6 %copy-start.31 = (f32[2048]{0:T(1024)S(1)}, f32[2048]{0:T(1024)}, u32[]{:S(2)}) copy-start(f32[2048]{0:T(1024)} %param.27) | copy-start | bytes 24580
  485.2 20.0 %copy-start.27 = (bf16[2048,2048]{1,0:T(8,128)(2,1)S(1)}, bf16[2048,2048]{1,0:T(8,128)(2,1)}, u32[]{:S(2)}) copy-start(bf16[2048,2048]{1,0:T(8,128)(2,1)} %all-gather.13.cloned.1.call-done) | copy-start | bytes 25165828
  505.2 11.1 copy-start.2
  527.1 16.4 %copy-start.7 = (bf16[8,1,1024,64]{2,3,1,0:T(8,128)(2,1)S(1)}, bf16[8,1,1024,64]{2,3,1,0:T(8,128)(2,1)}, u32[]{:S(2)}) copy-start(bf16[8,1,1024,64]{2,3,1,0:T(8,128)(2,1)} %copy-done.6) | copy-start | bytes 3145732
  527.1 144.6 %reduce-scatter.4.cloned.1.call-start = ((), (), s32[]{:S(2)}) async-start(), calls=%async_computation.8 | async-start | bytes 10485760 | tf_op jit(solution)/shard_map/reduce_scatter | solution.py:238
  527.2 16.4 %copy-start.9 = (bf16[2048,512]{1,0:T(8,128)(2,1)S(1)}, bf16[2048,512]{1,0:T(8,128)(2,1)}, u32[]{:S(2)}) copy-start(bf16[2048,512]{1,0:T(8,128)(2,1)} %all-gather.11.cloned.1.call-done) | copy-start | bytes 6291460
  549.5 252.1 %all-reduce.3.cloned.1.call-start = ((), (), s32[]{:S(2)}) async-start(), calls=%async_computation.12 | async-start | bytes 180224 | tf_op jit(solution)/shard_map/psum | solution.py:313
  557.6 4.4 copy-start.14
  557.7 4.4 copy-start.8
  557.7 4.4 copy-start.29
  562.0 9.4 copy-start.32
  562.0 21.5 %slice-start = ((s8[8388608]{0:T(1024)(128)(4,1)}), s8[4194304]{0:T(1024)(128)(4,1)S(1)}, s32[]{:S(2)}) async-start(s8[8388608]{0:T(1024)(128)(4,1)} %bitcast.313), calls=%async_computation.13 | async-start | bytes 8388608
  571.4 12.1 copy-start.13
  571.4 12.1 slice-start.1
  583.5 13.7 copy-start.1
  583.5 13.7 copy-start.16
  583.5 13.7 copy-start.19
  583.5 13.7 copy-start.21
  596.2 75.5 %copy-start.25 = (f32[2048]{0:T(1024)S(1)}, f32[2048]{0:T(1024)}, u32[]{:S(2)}) copy-start(f32[2048]{0:T(1024)} %param.29) | copy-start | bytes 24580
  596.2 75.5 %copy-start.26 = (f32[2048]{0:T(1024)S(1)}, f32[2048]{0:T(1024)}, u32[]{:S(2)}) copy-start(f32[2048]{0:T(1024)} %param.25) | copy-start | bytes 24580
  597.2 74.5 %copy-start.4 = (f32[256,2048]{1,0:T(8,128)S(1)}, f32[256,2048]{1,0:T(8,128)}, u32[]{:S(2)}) copy-start(f32[256,2048]{1,0:T(8,128)} %reduce-scatter.6.cloned.1.call-done) | copy-start | bytes 6291460
  677.1 920.3 %reduce-scatter.8.cloned.1.call-start = ((), (), s32[]{:S(2)}) async-start(), calls=%async_computation.11 | async-start | bytes 56623104 | tf_op jit(solution)/shard_map/reduce_scatter | solution.py:285
  (20 other events, 39.6 us)
Sparse Core Ops, SparseCore 0:
  10.2 51.9 all-gather.10
  63.7 32.9 all-gather.16
  98.9 99.0 all-gather.8
  200.0 32.6 all-gather.6
  234.7 124.9 all-gather.12
  361.6 123.5 all-gather.14
  527.3 69.8 reduce-scatter.5
  599.9 71.7 reduce-scatter.3
  679.3 122.2 all-reduce.2
  805.4 791.9 reduce-scatter.7
where the time goes:
time: 1630 us; the launch traced here: 1620 us
  waiting for transfers between devices  1240 us (76%)
  matrix products  217 us (13%)
  other arithmetic  79.1 us (5%)
  local copies, waits for them, and re-layouts  74.4 us (5%)
    reduce_scatter x1, waiting for transfers between devices, body(): lax.psum_scatter(jnp.concatenate([contract_first(whole_normed, qkv_grad),...  793 us
    all_gather x1, waiting for transfers between devices, body(): lax.all_gather(qkv_weight, 'dp', axis=0, tiled=True)  94.2 us
    psum x1, waiting for transfers between devices, body(): lax.psum((jnp.sum(normed_grad * x_hat, axis=0), jnp.sum(normed_grad, axis...  90.1 us
    all_gather x1, waiting for transfers between devices, body(): lax.all_gather(fc2_weight, 'dp', axis=0, tiled=True)  75.1 us
    reduce_scatter x1, waiting for transfers between devices, body(): lax.psum_scatter(contract_last(attended_part, dense_full) + contract_last...  71.2 us
    all_gather x1, waiting for transfers between devices, body(): lax.all_gather(dense_weight, 'dp', axis=0, tiled=True)  48.3 us
    dot_general x4, matrix products, contract_last(): lax.dot_general(left, right, (((1,), (1,)), ((), ())), preferred_element_...  44.1 us
    dot_general x32, matrix products, masked_scores(): jnp.einsum('sqd,skd->sqk', query_block, key_heads, preferred_element_type...  39.1 us
  transfers between devices with their start and end apart: 10, of which 9 were waited for; matrix products, arithmetic and copies ran while one was open for 19% of the time, Pallas kernels for 0%

commit v1 on v0

v1 whole, which is shorter than its diff:
```python
import functools
import math

import jax
import jax.numpy as jnp
import numpy as np
from jax import lax
from jax.experimental import pallas as pl
from jax.experimental.pallas import tpu as pltpu
from jax.sharding import Mesh
from jax.sharding import PartitionSpec as P

D = 2048
H = 32
ROT = 32
LEN = 1024
LONGEST = LEN // 3
HEAD = D // H
QB = 128
BACK = -(-(LONGEST - 1) // QB)

EPSILON = 1e-05
GELU_SCALE = math.sqrt(2.0 / math.pi)
GELU_CUBIC = 0.044715
MASK_VALUE = -1e30
ROPE_BASE = 10000.0
LOW = jnp.bfloat16
FULL = jnp.float32


def gelu_both(pre_gelu):
    square = pre_gelu * pre_gelu
    tangent = jnp.tanh(GELU_SCALE * pre_gelu * (1.0 + GELU_CUBIC * square))
    value = 0.5 * pre_gelu * (1.0 + tangent)
    slope = 0.5 * (1.0 + tangent) + 0.5 * pre_gelu * (1.0 - tangent * tangent) * GELU_SCALE * (
        1.0 + 3.0 * GELU_CUBIC * square
    )
    return value, slope


def normalize_rows(token_rows):
    values = token_rows.astype(FULL)
    centered = values - jnp.mean(values, axis=-1, keepdims=True)
    inv_std = lax.rsqrt(jnp.mean(centered * centered, axis=-1, keepdims=True) + EPSILON)
    return (centered * inv_std, inv_std)


def rotary_lanes():
    half = ROT // 2
    inverse = ROPE_BASE ** (-(2.0 * np.arange(half)) / ROT)
    angles = np.arange(LEN)[:, None] * inverse[None, :]
    rest = np.zeros((LEN, HEAD - ROT))
    cosine = np.concatenate([np.cos(angles), np.cos(angles), rest + 1.0], axis=1)
    sine = np.concatenate([-np.sin(angles), np.sin(angles), rest], axis=1)
    return tuple(jnp.asarray(np.tile(table, (1, 2)), FULL) for table in (cosine, sine))


def matmul(left, right, left_dim, right_dim):
    return lax.dot_general(
        left, right, (((left_dim,), (right_dim,)), ((), ())), preferred_element_type=FULL
    )


def attention_kernel(
    proj_ref, grad_ref, start_ref, cos_ref, sin_ref, att_ref, dqkv_ref, sums_ref,
    q_st, g_st, k_low, v_low, k_turn, v_turn, dk_sum, dv_sum, dq_sum,
):
    pair = 2 * HEAD
    scale = 1.0 / math.sqrt(HEAD)
    lane = lax.broadcasted_iota(jnp.int32, (LEN, pair), 1)
    first = lane < HEAD
    near = lane % HEAD < ROT // 2
    cosine, sine = cos_ref[...], sin_ref[...]

    def partner(x):
        return jnp.where(near, pltpu.roll(x, pair - ROT // 2, 1), pltpu.roll(x, ROT // 2, 1))

    def rotate(x):
        return x * cosine + partner(x) * sine

    def unrotate(x):
        return x * cosine - partner(x) * sine

    q = rotate(proj_ref[:, 0:pair]) * scale
    k = rotate(proj_ref[:, pair : 2 * pair])
    v = proj_ref[:, 2 * pair : 3 * pair]
    g = grad_ref[...].astype(FULL)
    zero = jnp.zeros_like(q)
    blocks = LEN // QB
    for stacked, whole in ((q_st, q), (g_st, g)):
        for head, part in enumerate(
            (jnp.where(first, whole, zero), jnp.where(first, zero, whole))
        ):
            stacked[:, head * QB : (head + 1) * QB, :] = part.astype(LOW).reshape(blocks, QB, pair)
    k_low[...] = k.astype(LOW)
    v_low[...] = v.astype(LOW)
    k_turn[...] = k.T.astype(LOW)
    v_turn[...] = v.T.astype(LOW)
    dk_sum[...] = jnp.zeros_like(dk_sum)
    dv_sum[...] = jnp.zeros_like(dv_sum)
    upper = lax.broadcasted_iota(jnp.int32, (pair, QB), 0) < HEAD
    for block in range(blocks):
        begin = max(0, block - BACK) * QB
        keys = slice(begin, (block + 1) * QB)
        rows = slice(block * QB, (block + 1) * QB)
        width = (block + 1) * QB - begin
        key_at = begin + lax.broadcasted_iota(jnp.int32, (width, QB), 0)
        query_at = block * QB + lax.broadcasted_iota(jnp.int32, (width, QB), 1)
        allowed = (key_at >= start_ref[0, block : block + 1, :]) & (key_at <= query_at)
        allowed = jnp.concatenate([allowed, allowed], axis=1)
        queries, grads = q_st[block], g_st[block]
        scores = jnp.where(allowed, matmul(k_low[keys], queries, 1, 1), MASK_VALUE)
        powers = jnp.exp(scores - jnp.max(scores, axis=0, keepdims=True))
        probs = powers * (1.0 / jnp.sum(powers, axis=0, keepdims=True))
        probs_low = probs.astype(LOW)
        prob_grad = matmul(v_low[keys], grads, 1, 1)
        row_dot = jnp.sum(probs * prob_grad, axis=0, keepdims=True)
        score_grad = (probs * (prob_grad - row_dot)).astype(LOW)
        dv_sum[keys] += matmul(probs_low, grads, 1, 0)
        dk_sum[keys] += matmul(score_grad, queries, 1, 0)
        turned = matmul(v_turn[:, keys], probs_low, 1, 0)
        att_ref[rows, :] = jnp.where(upper, turned[:, :QB], turned[:, QB:]).T.astype(LOW)
        turned = matmul(k_turn[:, keys], score_grad, 1, 0)
        dq_sum[rows, :] = jnp.where(upper, turned[:, :QB], turned[:, QB:]).T
    for part, grad in enumerate((unrotate(dq_sum[...] * scale), unrotate(dk_sum[...]), dv_sum[...])):
        columns = slice(part * pair, (part + 1) * pair)
        dqkv_ref[:, columns] = grad.astype(LOW)
        sums_ref[0, :, columns] = jnp.sum(grad, axis=0, keepdims=True)


def attention(projected, grads, starts):
    rows, width = projected.shape
    seqs, pair = rows // LEN, 2 * HEAD
    pairs = width // (3 * pair)
    cosine, sine = rotary_lanes()
    table = pl.BlockSpec((LEN, pair), lambda s, h: (0, 0))
    return pl.pallas_call(
        attention_kernel,
        grid=(seqs, pairs),
        in_specs=[
            pl.BlockSpec((LEN, 3 * pair), lambda s, h: (s, h)),
            pl.BlockSpec((LEN, pair), lambda s, h: (s, h)),
            pl.BlockSpec((1, LEN // QB, QB), lambda s, h: (s, 0, 0)),
            table,
            table,
        ],
        out_specs=[
            pl.BlockSpec((LEN, pair), lambda s, h: (s, h)),
            pl.BlockSpec((LEN, 3 * pair), lambda s, h: (s, h)),
            pl.BlockSpec((1, 1, 3 * pair), lambda s, h: (s, 0, h)),
        ],
        out_shape=[
            jax.ShapeDtypeStruct((rows, pairs * pair), LOW),
            jax.ShapeDtypeStruct((rows, width), LOW),
            jax.ShapeDtypeStruct((seqs, 1, width), FULL),
        ],
        scratch_shapes=[
            pltpu.VMEM((LEN // QB, 2 * QB, pair), LOW),
            pltpu.VMEM((LEN // QB, 2 * QB, pair), LOW),
            pltpu.VMEM((LEN, pair), LOW),
            pltpu.VMEM((LEN, pair), LOW),
            pltpu.VMEM((pair, LEN), LOW),
            pltpu.VMEM((pair, LEN), LOW),
            pltpu.VMEM((LEN, pair), FULL),
            pltpu.VMEM((LEN, pair), FULL),
            pltpu.VMEM((LEN, pair), FULL),
        ],
        compiler_params=pltpu.CompilerParams(vmem_limit_bytes=40 << 20),
        cost_estimate=pl.CostEstimate(
            flops=seqs * pairs * 6 * 2 * 2 * LEN * QB * (BACK + 1) * pair,
            transcendentals=seqs * pairs * 2 * LEN * QB * (BACK + 1),
            bytes_accessed=rows * (width * 6 + pairs * pair * 4),
        ),
        name="attention_both_ways",
    )(projected, grads, starts.reshape(seqs, LEN // QB, QB), cosine, sine)


def swap(value, axis, bit):
    return lax.ppermute(value, axis, [(i, i ^ bit) for i in range(lax.axis_size(axis))])


def sum_over(value, axis):
    bit = 1
    while bit < lax.axis_size(axis):
        value = value + swap(value, axis, bit)
        bit *= 2
    return value


def pick(value, index, axis):
    return lax.dynamic_index_in_dim(value, index, axis, keepdims=False)


def in_order(mine, other, index, axis):
    return jnp.where(
        index == 0, jnp.concatenate([mine, other], axis), jnp.concatenate([other, mine], axis)
    )


def share_over_x(halves, x_at):
    mine = pick(halves, x_at, 1)
    other = swap(pick(halves, 1 - x_at, 1), "x", 1)
    return in_order(mine, other, x_at, 0)


def reduce_over_z(partial, z_at):
    count = lax.axis_size("z")
    blocks = partial.astype(LOW).reshape(count, partial.shape[0] // count, partial.shape[1])
    bit = 1
    while count > 1:
        paired = blocks.reshape(count // 2, 2, *blocks.shape[1:])
        low = (z_at // bit) % 2
        other = swap(pick(paired, 1 - low, 1), "z", bit)
        blocks = pick(paired, low, 1).astype(FULL) + other.astype(FULL)
        count //= 2
        bit *= 2
        if count > 1:
            blocks = blocks.astype(LOW)
    return blocks[0]


def return_over_x(block, x_at):
    rows, columns = block.shape
    parts = block.reshape(2, rows // 2, columns)
    mine = pick(parts, x_at, 0)[:, None, :]
    other = swap(pick(parts, 1 - x_at, 0).astype(LOW), "x", 1)[:, None, :].astype(FULL)
    return in_order(mine, other, x_at, 1)


def by_pair(flat, lead):
    halves = flat.shape[-1] // 2
    pairs = halves // (2 * HEAD)
    shaped = flat.reshape(lead, 3, 2, pairs, 2 * HEAD)
    return shaped.transpose(0, 2, 3, 1, 4).reshape(lead, 2, 3 * halves)


def from_pair(halves, lead):
    pairs = halves.shape[-1] // (6 * HEAD)
    shaped = halves.reshape(lead, 2, pairs, 3, 2 * HEAD)
    return shaped.transpose(0, 3, 1, 2, 4).reshape(lead, 3, 4 * pairs * HEAD)


def body(
    tokens,
    out_grad,
    segments,
    ln_gain,
    ln_bias,
    qkv_weight,
    qkv_bias,
    dense_weight,
    dense_bias,
    fc1_weight,
    fc1_bias,
    fc2_weight,
    fc2_bias,
):
    x_at, z_at = lax.axis_index("x"), lax.axis_index("z")
    weight_rows = qkv_weight.shape[0]
    dense_half = dense_weight.shape[1] // 2
    qkv_half = 3 * dense_half
    hidden_half = fc1_weight.shape[1] // 2

    heads_halves = jnp.concatenate(
        [by_pair(qkv_weight, weight_rows), dense_weight.reshape(weight_rows, 2, dense_half)], axis=2
    )
    heads_full, fc1_full, fc2_full = (
        lax.all_gather(share_over_x(halves, x_at), "z", axis=0, tiled=True)
        for halves in (
            heads_halves,
            fc1_weight.reshape(weight_rows, 2, hidden_half),
            fc2_weight.reshape(weight_rows, 2, hidden_half),
        )
    )
    qkv_full, dense_full = heads_full[:, :qkv_half], heads_full[:, qkv_half:]

    x_hat, inv_std = normalize_rows(tokens)
    normed = (x_hat * ln_gain + ln_bias).astype(LOW)
    all_normed = lax.all_gather(normed, ("x", "t"), axis=0, tiled=True)
    all_grad = lax.all_gather(out_grad, ("x", "t"), axis=0, tiled=True)
    all_segments = in_order(segments, swap(segments, "x", 1), x_at, 0)
    starts = jnp.sum(
        (all_segments[:, None, :] < all_segments[:, :, None]).astype(jnp.int32), axis=2
    )

    bias_here = pick(by_pair(qkv_bias[None], 1)[0], x_at, 0)
    projected = matmul(all_normed, qkv_full, 1, 0) + bias_here
    attended_grad = matmul(all_grad, dense_full, 1, 0).astype(LOW)
    attended, qkv_grad, qkv_sums = attention(projected, attended_grad, starts)

    pre_gelu = matmul(all_normed, fc1_full, 1, 0) + pick(
        fc1_bias.reshape(2, hidden_half), x_at, 0
    )
    value, slope = gelu_both(pre_gelu)
    activated = value.astype(LOW)
    pre_grad_full = matmul(all_grad, fc2_full, 1, 0) * slope
    pre_grad = pre_grad_full.astype(LOW)

    heads_grad = jnp.concatenate(
        [matmul(all_normed, qkv_grad, 0, 0), matmul(all_grad, attended, 0, 0)], axis=1
    )
    heads_grad, fc1_grad, fc2_grad = (
        return_over_x(reduce_over_z(partial, z_at), x_at)
        for partial in (
            heads_grad,
            matmul(all_normed, pre_grad, 0, 0),
            matmul(all_grad, activated, 0, 0),
        )
    )

    branch = lax.psum_scatter(
        (matmul(attended, dense_full, 1, 1) + matmul(activated, fc2_full, 1, 1)).astype(LOW),
        ("x", "t"),
        scatter_dimension=0,
        tiled=True,
    )
    output = (
        tokens.astype(FULL) + branch.astype(FULL) + dense_bias + fc2_bias
    ).astype(LOW)
    normed_grad = lax.psum_scatter(
        (matmul(qkv_grad, qkv_full, 1, 1) + matmul(pre_grad, fc1_full, 1, 1)).astype(LOW),
        ("x", "t"),
        scatter_dimension=0,
        tiled=True,
    ).astype(FULL)
    scaled = normed_grad * ln_gain
    token_grad = inv_std * (
        scaled
        - jnp.mean(scaled, axis=-1, keepdims=True)
        - x_hat * jnp.mean(scaled * x_hat, axis=-1, keepdims=True)
    )
    input_grad = (out_grad.astype(FULL) + token_grad).astype(LOW)

    sums = jnp.concatenate(
        [
            jnp.sum(all_grad.astype(FULL), axis=0),
            jnp.sum(qkv_sums, axis=(0, 1)),
            jnp.sum(pre_grad_full, axis=0),
        ]
    )
    sums = sum_over(sums, "z")
    out_bias_sum, here = sums[:D], sums[D:]
    both = in_order(here[None], swap(here, "x", 1)[None], x_at, 0)
    qkv_bias_grad = from_pair(both[None, :, :qkv_half], 1)[0]
    fc1_bias_grad = both[:, qkv_half:].reshape(2 * hidden_half)
    norm_sums = jnp.stack([jnp.sum(normed_grad * x_hat, axis=0), jnp.sum(normed_grad, axis=0)])
    for axis in ("t", "x", "z"):
        norm_sums = sum_over(norm_sums, axis)
    return (
        output,
        input_grad,
        norm_sums[0],
        norm_sums[1],
        from_pair(heads_grad[:, :, :qkv_half], weight_rows),
        qkv_bias_grad,
        heads_grad[:, :, qkv_half:].reshape(weight_rows, 2 * dense_half),
        out_bias_sum,
        fc1_grad.reshape(weight_rows, 2 * hidden_half),
        fc1_bias_grad,
        fc2_grad.reshape(weight_rows, 2 * hidden_half),
        out_bias_sum,
    )


def solution(mesh):
    dp, tensor = mesh.shape["dp"], mesh.shape["tensor"]
    split = Mesh(np.asarray(mesh.devices).reshape(dp // 2, 2, tensor), ("z", "x", "t"))
    rows = ("z", "x")
    everywhere = ("z", "x", "t")
    return jax.shard_map(
        body,
        mesh=split,
        in_specs=(
            P(everywhere, None),
            P(everywhere, None),
            P(rows, None),
            P(),
            P(),
            P(rows, None, "t"),
            P(None, "t"),
            P(rows, "t"),
            P(),
            P(rows, "t"),
            P("t"),
            P(rows, "t"),
            P(),
        ),
        out_specs=(
            P(everywhere, None),
            P(everywhere, None),
            P(),
            P(),
            P(rows, None, "t"),
            P(None, "t"),
            P(rows, "t"),
            P(),
            P(rows, "t"),
            P("t"),
            P(rows, "t"),
            P(),
        ),
        check_vma=False,
    )
```

time: 1630 us -> 834 us (0.51)
  waiting for transfers between devices: 1240 us -> 489 us
  matrix products: 217 us -> 152 us
  other arithmetic: 79.1 us -> 43.8 us
  starting transfers between devices: 0.39 us -> 22.5 us
  Pallas kernels: 0 us -> 20.9 us
    reduce_scatter x3 -> x2, waiting for transfers between devices: 865 us -> 0.01 us  [the longest x1 0.01 us: body(): lax.psum_scatter((matmul(qkv_grad, qkv_full, 1, 1) + matmul(pre_grad, fc1...]
    ppermute x0 -> x21, waiting for transfers between devices: none -> 229 us  [swap(): lax.ppermute(value, axis, [(i, i ^ bit) for i in range(lax.axis_size(axis...]
    psum x1 -> x0, waiting for transfers between devices: 90.1 us -> none  [body(): lax.psum((jnp.sum(normed_grad * x_hat, axis=0), jnp.sum(normed_grad, axis...]
    dot_general x124 -> x12, matrix products: 217 us -> 152 us  [matmul(): lax.dot_general(left, right, (((left_dim,), (right_dim,)), ((), ())), pre...]
    concatenate x3 -> x2, other arithmetic: 38.5 us -> 0.08 us  [the longest x1 0.08 us: body(): jnp.concatenate([by_pair(qkv_weight, weight_rows), dense_weight.reshape(w...]
    unnamed x76 -> x92, local copies, waits for them, and re-layouts: 14.4 us -> 40.8 us
    ppermute x0 -> x21, starting transfers between devices: none -> 22 us  [swap(): lax.ppermute(value, axis, [(i, i ^ bit) for i in range(lax.axis_size(axis...]
    pallas_call x0 -> x1, Pallas kernels: none -> 20.9 us  [attention(): pl.pallas_call(attention_kernel, grid=(seqs, pairs), in_specs=[pl.BlockSp...]
  transfers between devices with their start and end apart: 10 -> 28, of which waited for: 9 -> 15; matrix products, arithmetic and copies ran while one was open for 19% -> 28% of each run, Pallas kernels for 0% -> 3%
where the time goes in v1:
time: 834 us; the launch traced here: 827 us
  waiting for transfers between devices  489 us (59%)
  matrix products  152 us (18%)
  local copies, waits for them, and re-layouts  84.1 us (10%)
  other arithmetic  43.8 us (5%)
  starting transfers between devices  22.5 us (3%)
  Pallas kernels  20.9 us (3%)
  between operations  15.4 us (2%)
    ppermute x21, waiting for transfers between devices, swap(): lax.ppermute(value, axis, [(i, i ^ bit) for i in range(lax.axis_size(axis...  229 us
    all_gather x3, waiting for transfers between devices, body(): lax.all_gather(share_over_x(halves, x_at), 'z', axis=0, tiled=True)  154 us
    dot_general x12, matrix products, matmul(): lax.dot_general(left, right, (((left_dim,), (right_dim,)), ((), ())), pre...  152 us
    all_gather x1, waiting for transfers between devices, body(): all_grad = lax.all_gather(out_grad, ('x', 't'), axis=0, tiled=True)  54.8 us
    all_gather x1, waiting for transfers between devices, body(): all_normed = lax.all_gather(normed, ('x', 't'), axis=0, tiled=True)  50.9 us
    unnamed x92, local copies, waits for them, and re-layouts  40.8 us
    ppermute x21, starting transfers between devices, swap(): lax.ppermute(value, axis, [(i, i ^ bit) for i in range(lax.axis_size(axis...  22 us
    pallas_call x1, Pallas kernels, attention(): pl.pallas_call(attention_kernel, grid=(seqs, pairs), in_specs=[pl.BlockSp...  20.9 us
  transfers between devices with their start and end apart: 28, of which 15 were waited for; matrix products, arithmetic and copies ran while one was open for 28% of the time, Pallas kernels for 3%

profile of v1, /device:TPU:0, one launch (start us, length us, event | category | flops | bytes accessed | tf_op | source)
XLA Modules:
  0.0 827.5 jit_solution(1911053371083462491)
XLA Ops:
  13.3 11.7 %collective-permute-done = bf16[256,1024]{1,0:T(8,128)(2,1)S(1)} collective-permute-done((bf16[256,1024]{1,0:T(8,128)(2,1)S(1)}, bf16[256,1024]{1,0:T(8,128)(2,1)S(1)}, u32[]{:S(2)}, u32[]{:S(2)}) %collective-permute-start) | collective-permute-done | bytes 524320 | tf_op jit(solution)/shard_map/ppermute | solution.py:179
  33.2 11.4 %collective-permute-done.2 = bf16[256,1024]{1,0:T(8,128)(2,1)S(1)} collective-permute-done((bf16[256,1024]{1,0:T(8,128)(2,1)}, bf16[256,1024]{1,0:T(8,128)(2,1)S(1)}, u32[]{:S(2)}, u32[]{:S(2)}) %collective-permute-start.2) | collective-permute-done | bytes 524320 | tf_op jit(solution)/shard_map/ppermute | solution.py:179
  49.3 10.1 %collective-permute-done.1 = s32[1,1024]{1,0:T(1,128)S(1)} collective-permute-done((s32[1,1024]{1,0:T(1,128)S(1)}, s32[1,1024]{1,0:T(1,128)S(1)}, u32[]{:S(2)}, u32[]{:S(2)}) %collective-permute-start.1) | collective-permute-done | bytes 4128 | tf_op jit(solution)/shard_map/ppermute | solution.py:179
  62.3 46.6 %all-gather.8.cloned.1.call-done = bf16[2048,1024]{1,0:T(8,128)(2,1)} async-done(((bf16[512,1024]{1,0:T(8,128)(2,1)}), bf16[2048,1024]{1,0:T(8,128)(2,1)}) %all-gather.8.cloned.1.call-update) | async-done | bytes 4194320 | tf_op jit(solution)/shard_map/all_gather | solution.py:268
  109.0 54.8 %all-gather.10.cloned.1.call-done = bf16[2048,2048]{1,0:T(8,128)(2,1)} async-done(((bf16[256,2048]{1,0:T(8,128)(2,1)}), bf16[2048,2048]{1,0:T(8,128)(2,1)}) %all-gather.10.cloned.1.call-update) | async-done | bytes 8388624 | tf_op jit(solution)/shard_map/all_gather | solution.py:280
  163.8 6.0 fusion.14.grad_ref
  169.8 50.9 %all-gather.6.cloned.1.call-done = bf16[2048,2048]{1,0:T(8,128)(2,1)} async-done(((bf16[256,2048]{1,0:T(8,128)(2,1)}), bf16[2048,2048]{1,0:T(8,128)(2,1)}) %all-gather.6.cloned.1.call-update) | async-done | bytes 8388624 | tf_op jit(solution)/shard_map/all_gather | solution.py:279
  220.7 10.0 %broadcast_add_fusion.proj_ref = f32[2048,768]{1,0:T(8,128)S(1)} fusion(f32[768]{0:T(1024)S(1)} %fusion.41, bf16[2048,2048]{1,0:T(8,128)(2,1)} %all-gather.6.cloned.1.call-done, bf16[2048,1024]{1,0:T(8,128)(2,1)} %all-gather.8.cloned.1.call-done), kind=kOutput, calls=%fused_computation.23 | convolution fusion | flops 6444023808 | bytes 17828864 | tf_op jit(solution)/shard_map/dot_general | solution.py:59
  230.8 20.9 %attention_both_ways.1 = (bf16[2048,256]{1,0:T(8,128)(2,1)S(1)}, bf16[2048,768]{1,0:T(8,128)(2,1)S(1)}, f32[2,1,768]{2,1,0:T(1,128)S(1)}) custom-call(f32[2048,768]{1,0:T(8,128)S(1)} %broadcast_add_fusion.proj_ref, bf16[2048,256]{1,0:T(8,128)(2,1)S(1)} %fusion.14.grad_ref, s32[2,8,128]{2,1,0:T(8,128)S(1)} %bitcast.114, f32[1024,128]{1,0:T(8,128)S(1)} %copy-done.1, ...), custom_call_target="tpu_custom_call" | custom-call | flops 6442450944 | bytes 11534336 | tf_op jit(solution)/shard_map/attention_both_ways/pallas_call | solution.py:137
  253.3 9.6 %fusion.6 = f32[2048,2048]{1,0:T(8,128)} fusion(bf16[2048,768]{1,0:T(8,128)(2,1)S(1)} %get-tuple-element.16, bf16[2048,1024]{1,0:T(8,128)(2,1)S(1)} %copy-done.23), kind=kOutput, calls=%fused_computation.30 | convolution fusion | flops 6442450944 | bytes 23068672 | tf_op jit(solution)/shard_map/dot_general | solution.py:59
  262.9 40.6 %all-gather.12.cloned.1.call-done = bf16[2048,1024]{1,0:T(8,128)(2,1)} async-done(((bf16[512,1024]{1,0:T(8,128)(2,1)}), bf16[2048,1024]{1,0:T(8,128)(2,1)}) %all-gather.12.cloned.1.call-update) | async-done | bytes 4194320 | tf_op jit(solution)/shard_map/all_gather | solution.py:268
  303.5 14.9 %fusion.46 = f32[2048,1024]{1,0:T(8,128)} fusion(bf16[2048,2048]{1,0:T(8,128)(2,1)} %all-gather.6.cloned.1.call-done, bf16[2048,1024]{1,0:T(8,128)(2,1)} %all-gather.12.cloned.1.call-done), kind=kOutput, calls=%fused_computation.117 | convolution fusion | flops 8589934592 | bytes 20971520 | tf_op jit(solution)/shard_map/dot_general | solution.py:59
  318.4 66.4 %all-gather.14.cloned.1.call-done = bf16[2048,1024]{1,0:T(8,128)(2,1)} async-done(((bf16[512,1024]{1,0:T(8,128)(2,1)}), bf16[2048,1024]{1,0:T(8,128)(2,1)}) %all-gather.14.cloned.1.call-update) | async-done | bytes 4194320 | tf_op jit(solution)/shard_map/all_gather | solution.py:268
  384.8 19.4 %fusion.45 = (f32[1024]{0:T(1024)S(1)}, bf16[2048,1024]{1,0:T(8,128)(2,1)}) fusion(f32[2048,1024]{1,0:T(8,128)} %fusion.46, f32[1024]{0:T(1024)S(1)} %bitcast.152, bf16[2048,2048]{1,0:T(8,128)(2,1)} %all-gather.10.cloned.1.call-done, bf16[2048,1024]{1,0:T(8,128)(2,1)} %all-gather.14.cloned.1.call-done), kind=kOutput, calls=%fused_computation.116 | convolution fusion | flops 8631876608 | bytes 25174016 | tf_op jit(solution)/shard_map/dot_general | solution.py:59
  404.2 15.9 %add_convert_fusion = bf16[2048,2048]{1,0:T(8,128)(2,1)} fusion(f32[2048,2048]{1,0:T(8,128)} %fusion.6, bf16[2048,1024]{1,0:T(8,128)(2,1)S(1)} %copy-done.37, bf16[2048,1024]{1,0:T(8,128)(2,1)} %get-tuple-element.83), kind=kOutput, calls=%fused_computation.1 | convolution fusion | flops 8598323200 | bytes 33554432 | tf_op jit(solution)/shard_map/dot_general | solution.py:59
  420.2 5.8 fusion.13
  428.0 11.9 %convolution_convert_fusion.1 = bf16[2048,768]{1,0:T(8,128)(2,1)S(1)} fusion(bf16[2048,2048]{1,0:T(8,128)(2,1)} %all-gather.6.cloned.1.call-done, bf16[2048,768]{1,0:T(8,128)(2,1)} %copy-done.2), kind=kOutput, calls=%fused_computation.19 | convolution fusion | flops 6444023808 | bytes 14680064 | tf_op jit(solution)/shard_map/dot_general | solution.py:59
  443.2 10.0 %fusion.33 = f32[2048,2048]{1,0:T(8,128)} fusion(bf16[2048,256]{1,0:T(8,128)(2,1)S(1)} %get-tuple-element.15, bf16[2048,1024]{1,0:T(8,128)(2,1)} %all-gather.8.cloned.1.call-done), kind=kOutput, calls=%fused_computation.79 | convolution fusion | flops 2147483648 | bytes 18874368 | tf_op jit(solution)/shard_map/dot_general | solution.py:59
  453.1 18.3 %add_convert_fusion.1 = bf16[2048,2048]{1,0:T(8,128)(2,1)} fusion(f32[2048,2048]{1,0:T(8,128)} %fusion.33, bf16[2048,1024]{1,0:T(8,128)(2,1)} %all-gather.14.cloned.1.call-done, f32[2048,1024]{1,0:T(8,128)} %fusion.46, f32[1024]{0:T(1024)S(1)} %bitcast.153), kind=kOutput, calls=%fused_computation.2 | convolution fusion | flops 8619294720 | bytes 37752832 | tf_op jit(solution)/shard_map/dot_general | solution.py:59
  471.5 17.4 %convert_bitcast_fusion = bf16[2048,1024]{0,1:T(8,128)(2,1)} fusion(bf16[2048,2048]{1,0:T(8,128)(2,1)} %all-gather.10.cloned.1.call-done, f32[2048,1024]{1,0:T(8,128)} %fusion.46, f32[1024]{0:T(1024)S(1)} %bitcast.154), kind=kOutput, calls=%fused_computation.17 | convolution fusion | flops 8613003264 | bytes 20975616 | tf_op jit(solution)/shard_map/dot_general | solution.py:59
  488.9 12.8 %convolution_convert_fusion = bf16[2048,1024]{1,0:T(8,128)(2,1)} fusion(bf16[2048,2048]{1,0:T(8,128)(2,1)} %all-gather.6.cloned.1.call-done, bf16[2048,1024]{1,0:T(8,128)(2,1)S(1)} %copy-done.38), kind=kOutput, calls=%fused_computation.18 | convolution fusion | flops 8592031744 | bytes 16777216 | tf_op jit(solution)/shard_map/dot_general | solution.py:59
  501.8 8.4 %reshape_reshape.8 = bf16[2,2,512,1024]{2,1,0,3:T(2,128)(2,1)} reshape(bf16[2048,1024]{0,1:T(8,128)(2,1)} %convert_bitcast_fusion) | data formatting | bytes 8388608 | tf_op jit(solution)/shard_map/reshape;reshape | solution.py:211
  515.5 9.8 %constant_dynamic-slice_fusion.2 = (bf16[2,1,512,1024]{2,1,0,3:T(2,128)(2,1)}, bf16[2,1,512,1024]{2,1,0,3:T(2,128)(2,1)}) fusion(bf16[2,2,512,1024]{2,1,0,3:T(2,128)(2,1)S(1)} %copy-done.3, s32[]{:T(128)S(6)} %select_n.146, s32[]{:T(128)S(6)} %select_n.147), kind=kLoop, calls=%fused_computation.99 | loop fusion | bytes 8388616 | tf_op jit(solution)/shard_map/jit(dynamic_index_in_dim)/dynamic_slice | solution.py:191
  525.3 10.9 %copy.126 = bf16[2,1,512,1024]{3,2,0,1:T(8,128)(2,1)} copy(bf16[2,1,512,1024]{2,1,0,3:T(2,128)(2,1)} %get-tuple-element.71) | data formatting | bytes 4194304
  536.3 4.8 convert_reduce_fusion
  543.2 63.2 %collective-permute-done.12 = f32[3840]{0:T(1024)S(1)} collective-permute-done((f32[3840]{0:T(1024)S(1)}, f32[3840]{0:T(1024)S(1)}, u32[]{:S(2)}, u32[]{:S(2)}) %collective-permute-start.12) | collective-permute-done | bytes 15392 | tf_op jit(solution)/shard_map/ppermute | solution.py:179
  606.6 4.5 collective-permute-done.13
  612.4 10.6 %copy.125 = bf16[2,1,512,1024]{3,2,0,1:T(8,128)(2,1)} copy(bf16[2,1,512,1024]{2,1,0,3:T(2,128)(2,1)} %get-tuple-element.70) | data formatting | bytes 4194304
  640.1 78.7 %collective-permute-done.10 = bf16[1,512,1024]{2,1,0:T(8,128)(2,1)S(1)} collective-permute-done((bf16[1,512,1024]{2,1,0:T(8,128)(2,1)}, bf16[1,512,1024]{2,1,0:T(8,128)(2,1)S(1)}, u32[]{:S(2)}, u32[]{:S(2)}) %collective-permute-start.10) | collective-permute-done | bytes 1048608 | tf_op jit(solution)/shard_map/ppermute | solution.py:179
  721.5 19.9 %collective-permute-done.16 = bf16[1,512,1024]{2,1,0:T(8,128)(2,1)} collective-permute-done((bf16[1,512,1024]{2,1,0:T(8,128)(2,1)}, bf16[1,512,1024]{2,1,0:T(8,128)(2,1)}, u32[]{:S(2)}, u32[]{:S(2)}) %collective-permute-start.16) | collective-permute-done | bytes 1048608 | tf_op jit(solution)/shard_map/ppermute | solution.py:179
  744.1 18.8 %collective-permute-done.19 = bf16[1,512,1024]{2,1,0:T(8,128)(2,1)} collective-permute-done((bf16[1,512,1024]{2,1,0:T(8,128)(2,1)}, bf16[1,512,1024]{2,1,0:T(8,128)(2,1)}, u32[]{:S(2)}, u32[]{:S(2)}) %collective-permute-start.19) | collective-permute-done | bytes 1048608 | tf_op jit(solution)/shard_map/ppermute | solution.py:179
  770.8 6.7 collective-permute-done.20
  (217 shorter events, 110.5 us)
Async XLA Ops:
  7.2 101.8 %all-gather.8.cloned.1.call-start = ((), (), s32[]{:S(2)}) async-start(), calls=%async_computation.3 | async-start | bytes 5242880 | tf_op jit(solution)/shard_map/all_gather | solution.py:268
  10.1 14.9 %collective-permute-start = (bf16[256,1024]{1,0:T(8,128)(2,1)S(1)}, bf16[256,1024]{1,0:T(8,128)(2,1)S(1)}, u32[]{:S(2)}, u32[]{:S(2)}) collective-permute-start(bf16[256,1024]{1,0:T(8,128)(2,1)S(1)} %bitcast.139), channel_id=1, source_target_pairs={{0,4},{4,0},{1,5},{5,1},{2,6},{6,2},{3,7},{7,3},{8,12},{12,8},{9,1... | collective-permute-start | bytes 1572872 | tf_op jit(solution)/shard_map/ppermute | solution.py:179
  26.5 137.3 %all-gather.10.cloned.1.call-start = ((), (), s32[]{:S(2)}) async-start(), calls=%async_computation.4 | async-start | bytes 9437184 | tf_op jit(solution)/shard_map/all_gather | solution.py:280
  27.3 193.4 %all-gather.6.cloned.1.call-start = ((), (), s32[]{:S(2)}) async-start(), calls=%async_computation.2 | async-start | bytes 9437184 | tf_op jit(solution)/shard_map/all_gather | solution.py:279
  29.5 274.0 %all-gather.12.cloned.1.call-start = ((), (), s32[]{:S(2)}) async-start(), calls=%async_computation.5 | async-start | bytes 5242880 | tf_op jit(solution)/shard_map/all_gather | solution.py:268
  31.2 13.3 %collective-permute-start.2 = (bf16[256,1024]{1,0:T(8,128)(2,1)}, bf16[256,1024]{1,0:T(8,128)(2,1)S(1)}, u32[]{:S(2)}, u32[]{:S(2)}) collective-permute-start(bf16[256,1024]{1,0:T(8,128)(2,1)} %bitcast.11), channel_id=1, source_target_pairs={{0,4},{4,0},{1,5},{5,1},{2,6},{6,2},{3,7},{7,3},{8,12},{12,8},{9,1... | collective-permute-start | bytes 1572872 | tf_op jit(solution)/shard_map/ppermute | solution.py:179
  46.0 338.8 %all-gather.14.cloned.1.call-start = ((), (), s32[]{:S(2)}) async-start(), calls=%async_computation.6 | async-start | bytes 5242880 | tf_op jit(solution)/shard_map/all_gather | solution.py:268
  46.9 13.6 %collective-permute-start.3 = (bf16[256,1024]{1,0:T(8,128)(2,1)S(1)}, bf16[256,1024]{1,0:T(8,128)(2,1)S(1)}, u32[]{:S(2)}, u32[]{:S(2)}) collective-permute-start(bf16[256,1024]{1,0:T(8,128)(2,1)S(1)} %bitcast.138), channel_id=1, source_target_pairs={{0,4},{4,0},{1,5},{5,1},{2,6},{6,2},{3,7},{7,3},{8,12},{12,8},{9,1... | collective-permute-start | bytes 1572872 | tf_op jit(solution)/shard_map/ppermute | solution.py:179
  48.4 11.0 %collective-permute-start.1 = (s32[1,1024]{1,0:T(1,128)S(1)}, s32[1,1024]{1,0:T(1,128)S(1)}, u32[]{:S(2)}, u32[]{:S(2)}) collective-permute-start(s32[1,1024]{1,0:T(1,128)S(1)} %copy-done.36), channel_id=1, source_target_pairs={{0,4},{4,0},{1,5},{5,1},{2,6},{6,2},{3,7},{7,3},{8,12},{12,8},{9,1... | collective-permute-start | bytes 12296 | tf_op jit(solution)/shard_map/ppermute | solution.py:179
  62.1 716.5 %reduce-scatter.5.cloned.1.call-start = ((), (), s32[]{:S(2)}) async-start(), calls=%async_computation.8 | async-start | bytes 9437184 | tf_op jit(solution)/shard_map/reduce_scatter | solution.py:320
  169.8 60.9 %copy-start = (f32[1024,128]{1,0:T(8,128)S(1)}, f32[1024,128]{1,0:T(8,128)}, u32[]{:S(2)}) copy-start(f32[1024,128]{1,0:T(8,128)} %constant.157.clone.sin_ref) | copy-start | bytes 1572868
  169.8 60.9 %copy-start.1 = (f32[1024,128]{1,0:T(8,128)S(1)}, f32[1024,128]{1,0:T(8,128)}, u32[]{:S(2)}) copy-start(f32[1024,128]{1,0:T(8,128)} %constant.156.clone.cos_ref) | copy-start | bytes 1572868
  420.1 394.9 %reduce-scatter.3.cloned.1.call-start = ((), (), s32[]{:S(2)}) async-start(), calls=%async_computation.7 | async-start | bytes 9437184 | tf_op jit(solution)/shard_map/reduce_scatter | solution.py:311
  443.2 179.9 %collective-permute-start.9 = (bf16[2,512,1024]{2,1,0:T(8,128)(2,1)}, bf16[2,512,1024]{2,1,0:T(8,128)(2,1)}, u32[]{:S(2)}, u32[]{:S(2)}) collective-permute-start(bf16[2,512,1024]{2,1,0:T(8,128)(2,1)} %fusion.28), channel_id=1, source_target_pairs={{0,8},{8,0},{16,24},{24,16},{1,9},{9,1},{17,25},{25,17},{2,10},{10... | collective-permute-start | bytes 6291464 | tf_op jit(solution)/shard_map/ppermute | solution.py:179
  513.5 113.9 %collective-permute-start.15 = (bf16[2,512,1024]{2,1,0:T(8,128)(2,1)}, bf16[2,512,1024]{2,1,0:T(8,128)(2,1)}, u32[]{:S(2)}, u32[]{:S(2)}) collective-permute-start(bf16[2,512,1024]{2,1,0:T(8,128)(2,1)} %dynamic-slice_bitcast_fusion), channel_id=1, source_target_pairs={{0,8},{8,0},{16,24},{24,16},{1,9},{9,1},{17,25},{25,17},{2,10},{10... | collective-permute-start | bytes 6291464 | tf_op jit(solution)/shard_map/ppermute | solution.py:179
  536.2 97.1 %collective-permute-start.18 = (bf16[2,512,1024]{2,1,0:T(8,128)(2,1)}, bf16[2,512,1024]{2,1,0:T(8,128)(2,1)}, u32[]{:S(2)}, u32[]{:S(2)}) collective-permute-start(bf16[2,512,1024]{2,1,0:T(8,128)(2,1)} %bitcast.47), channel_id=1, source_target_pairs={{0,8},{8,0},{16,24},{24,16},{1,9},{9,1},{17,25},{25,17},{2,10},{10... | collective-permute-start | bytes 6291464 | tf_op jit(solution)/shard_map/ppermute | solution.py:179
  541.1 82.0 %copy-start.7 = (bf16[2048,768]{1,0:T(8,128)(2,1)S(1)}, bf16[2048,768]{1,0:T(8,128)(2,1)}, u32[]{:S(2)}) copy-start(bf16[2048,768]{1,0:T(8,128)(2,1)} %copy-done.6) | copy-start | bytes 9437188
  541.1 65.2 %collective-permute-start.12 = (f32[3840]{0:T(1024)S(1)}, f32[3840]{0:T(1024)S(1)}, u32[]{:S(2)}, u32[]{:S(2)}) collective-permute-start(f32[3840]{0:T(1024)S(1)} %pad_maximum_fusion.1), channel_id=1, source_target_pairs={{0,8},{8,0},{16,24},{24,16},{1,9},{9,1},{17,25},{25,17},{2,10},{10... | collective-permute-start | bytes 46088 | tf_op jit(solution)/shard_map/ppermute | solution.py:179
  606.4 4.6 collective-permute-start.13
  611.0 12.0 %collective-permute-start.14 = (f32[1792]{0:T(1024)S(1)}, f32[1792]{0:T(1024)S(1)}, u32[]{:S(2)}, u32[]{:S(2)}) collective-permute-start(f32[1792]{0:T(1024)S(1)} %slice.45), channel_id=1, source_target_pairs={{0,4},{4,0},{1,5},{5,1},{2,6},{6,2},{3,7},{7,3},{8,12},{12,8},{9,1... | collective-permute-start | bytes 21512 | tf_op jit(solution)/shard_map/ppermute | solution.py:179
  623.0 196.6 %copy-start.26 = (f32[2048]{0:T(1024)}, f32[2048]{0:T(1024)S(1)}, u32[]{:S(2)}) copy-start(f32[2048]{0:T(1024)S(1)} %slice.48) | copy-start | bytes 24580
  626.8 92.1 %collective-permute-start.10 = (bf16[1,512,1024]{2,1,0:T(8,128)(2,1)}, bf16[1,512,1024]{2,1,0:T(8,128)(2,1)S(1)}, u32[]{:S(2)}, u32[]{:S(2)}) collective-permute-start(bf16[1,512,1024]{2,1,0:T(8,128)(2,1)} %constant_dynamic-slice_fusion.4), channel_id=1, source_target_pairs={{0,16},{8,24},{16,0},{24,8},{1,17},{9,25},{17,1},{25,9},{2,18},{10... | collective-permute-start | bytes 3145736 | tf_op jit(solution)/shard_map/ppermute | solution.py:179
  631.0 110.4 %collective-permute-start.16 = (bf16[1,512,1024]{2,1,0:T(8,128)(2,1)}, bf16[1,512,1024]{2,1,0:T(8,128)(2,1)}, u32[]{:S(2)}, u32[]{:S(2)}) collective-permute-start(bf16[1,512,1024]{2,1,0:T(8,128)(2,1)} %constant_dynamic-slice_fusion.3), channel_id=1, source_target_pairs={{0,16},{8,24},{16,0},{24,8},{1,17},{9,25},{17,1},{25,9},{2,18},{10... | collective-permute-start | bytes 3145736 | tf_op jit(solution)/shard_map/ppermute | solution.py:179
  638.3 124.6 %collective-permute-start.19 = (bf16[1,512,1024]{2,1,0:T(8,128)(2,1)}, bf16[1,512,1024]{2,1,0:T(8,128)(2,1)}, u32[]{:S(2)}, u32[]{:S(2)}) collective-permute-start(bf16[1,512,1024]{2,1,0:T(8,128)(2,1)} %constant_dynamic-slice_fusion), channel_id=1, source_target_pairs={{0,16},{8,24},{16,0},{24,8},{1,17},{9,25},{17,1},{25,9},{2,18},{10... | collective-permute-start | bytes 3145736 | tf_op jit(solution)/shard_map/ppermute | solution.py:179
  720.6 48.0 %collective-permute-start.11 = (bf16[256,1024]{1,0:T(8,128)(2,1)S(1)}, bf16[256,1024]{1,0:T(8,128)(2,1)S(1)}, u32[]{:S(2)}, u32[]{:S(2)}) collective-permute-start(bf16[256,1024]{1,0:T(8,128)(2,1)S(1)} %fusion.36), channel_id=1, source_target_pairs={{0,4},{4,0},{1,5},{5,1},{2,6},{6,2},{3,7},{7,3},{8,12},{12,8},{9,1... | collective-permute-start | bytes 1572872 | tf_op jit(solution)/shard_map/ppermute | solution.py:179
  743.1 26.6 %collective-permute-start.17 = (bf16[256,1024]{1,0:T(8,128)(2,1)S(1)}, bf16[256,1024]{1,0:T(8,128)(2,1)S(1)}, u32[]{:S(2)}, u32[]{:S(2)}) collective-permute-start(bf16[256,1024]{1,0:T(8,128)(2,1)S(1)} %fusion.37), channel_id=1, source_target_pairs={{0,4},{4,0},{1,5},{5,1},{2,6},{6,2},{3,7},{7,3},{8,12},{12,8},{9,1... | collective-permute-start | bytes 1572872 | tf_op jit(solution)/shard_map/ppermute | solution.py:179
  764.5 12.9 %collective-permute-start.20 = (bf16[256,1024]{1,0:T(8,128)(2,1)S(1)}, bf16[256,1024]{1,0:T(8,128)(2,1)S(1)}, u32[]{:S(2)}, u32[]{:S(2)}) collective-permute-start(bf16[256,1024]{1,0:T(8,128)(2,1)S(1)} %fusion.38), channel_id=1, source_target_pairs={{0,4},{4,0},{1,5},{5,1},{2,6},{6,2},{3,7},{7,3},{8,12},{12,8},{9,1... | collective-permute-start | bytes 1572872 | tf_op jit(solution)/shard_map/ppermute | solution.py:179
  781.0 2.8 collective-permute-start.4
  783.9 4.7 collective-permute-start.5
  788.6 21.6 %collective-permute-start.6 = (f32[2,2048]{1,0:T(2,128)S(1)}, f32[2,2048]{1,0:T(2,128)S(1)}, u32[]{:S(2)}, u32[]{:S(2)}) collective-permute-start(f32[2,2048]{1,0:T(2,128)S(1)} %fusion.65), channel_id=1, source_target_pairs={{0,4},{4,0},{1,5},{5,1},{2,6},{6,2},{3,7},{7,3},{8,12},{12,8},{9,1... | collective-permute-start | bytes 49160 | tf_op jit(solution)/shard_map/ppermute | solution.py:179
  810.2 3.8 collective-permute-start.7
  814.0 4.9 collective-permute-start.8
  (36 other events, 353.5 us)
Sparse Core Ops, SparseCore 0:
  26.7 82.2 all-gather.7
  110.9 52.9 all-gather.9
  166.3 54.3 all-gather.5
  222.7 80.7 all-gather.11
  305.5 79.2 all-gather.13
  420.2 69.7 reduce-scatter.4
  493.9 71.2 reduce-scatter.2

commit v2 on v1

v2 whole, which is shorter than its diff:
```python
import functools
import math

import jax
import jax.numpy as jnp
import numpy as np
from jax import lax
from jax.experimental import pallas as pl
from jax.experimental.pallas import tpu as pltpu
from jax.sharding import Mesh
from jax.sharding import PartitionSpec as P

D = 2048
H = 32
ROT = 32
LEN = 1024
LONGEST = LEN // 3
HEAD = D // H
QB = 128
BACK = -(-(LONGEST - 1) // QB)

EPSILON = 1e-05
GELU_SCALE = math.sqrt(2.0 / math.pi)
GELU_CUBIC = 0.044715
MASK_VALUE = -1e30
ROPE_BASE = 10000.0
LOW = jnp.bfloat16
FULL = jnp.float32


def gelu_both(pre_gelu):
    square = pre_gelu * pre_gelu
    tangent = jnp.tanh(GELU_SCALE * pre_gelu * (1.0 + GELU_CUBIC * square))
    value = 0.5 * pre_gelu * (1.0 + tangent)
    slope = 0.5 * (1.0 + tangent) + 0.5 * pre_gelu * (1.0 - tangent * tangent) * GELU_SCALE * (
        1.0 + 3.0 * GELU_CUBIC * square
    )
    return value, slope


def rotary_lanes():
    half = ROT // 2
    inverse = ROPE_BASE ** (-(2.0 * np.arange(half)) / ROT)
    angles = np.arange(LEN)[:, None] * inverse[None, :]
    rest = np.zeros((LEN, HEAD - ROT))
    cosine = np.concatenate([np.cos(angles), np.cos(angles), rest + 1.0], axis=1)
    sine = np.concatenate([-np.sin(angles), np.sin(angles), rest], axis=1)
    return tuple(jnp.asarray(np.tile(table, (1, 2)), FULL) for table in (cosine, sine))


def matmul(left, right, left_dim, right_dim):
    return lax.dot_general(
        left, right, (((left_dim,), (right_dim,)), ((), ())), preferred_element_type=FULL
    )


def attention_kernel(
    place_ref, proj_ref, grad_ref, start_ref, cos_ref, sin_ref, att_ref, dqkv_ref, sums_ref,
    q_st, g_st, k_low, v_low, k_turn, v_turn, dk_sum, dv_sum, dq_sum,
):
    pair = 2 * HEAD
    scale = 1.0 / math.sqrt(HEAD)
    part_rows = proj_ref.shape[3]
    parts = LEN // part_rows
    lane = lax.broadcasted_iota(jnp.int32, (part_rows, pair), 1)
    first = lane < HEAD
    near = lane % HEAD < ROT // 2
    y_at, core_at = place_ref[0], place_ref[1]

    def where_is(part):
        return (part % 2) ^ core_at, (part // 2) ^ y_at

    def partner(x):
        return jnp.where(near, pltpu.roll(x, pair - ROT // 2, 1), pltpu.roll(x, ROT // 2, 1))

    per_part = part_rows // QB
    for part in range(parts):
        core, y = where_is(part)
        rows = slice(part * part_rows, (part + 1) * part_rows)
        cosine, sine = cos_ref[rows, :], sin_ref[rows, :]
        projected = proj_ref[core, y, 0]
        q = projected[:, 0:pair]
        k = projected[:, pair : 2 * pair]
        v = projected[:, 2 * pair : 3 * pair]
        q = (q * cosine + partner(q) * sine) * scale
        k = k * cosine + partner(k) * sine
        g = grad_ref[core, y, 0].astype(FULL)
        zero = jnp.zeros_like(q)
        for stacked, whole in ((q_st, q), (g_st, g)):
            for head, own in enumerate(
                (jnp.where(first, whole, zero), jnp.where(first, zero, whole))
            ):
                stacked[
                    part * per_part : (part + 1) * per_part, head * QB : (head + 1) * QB, :
                ] = own.astype(LOW).reshape(per_part, QB, pair)
        k_low[rows, :] = k.astype(LOW)
        v_low[rows, :] = v.astype(LOW)
        k_turn[:, rows] = k.T.astype(LOW)
        v_turn[:, rows] = v.T.astype(LOW)
    dk_sum[...] = jnp.zeros_like(dk_sum)
    dv_sum[...] = jnp.zeros_like(dv_sum)
    upper = lax.broadcasted_iota(jnp.int32, (pair, QB), 0) < HEAD
    for block in range(LEN // QB):
        begin = max(0, block - BACK) * QB
        keys = slice(begin, (block + 1) * QB)
        rows = slice(block * QB, (block + 1) * QB)
        width = (block + 1) * QB - begin
        key_at = begin + lax.broadcasted_iota(jnp.int32, (width, QB), 0)
        query_at = block * QB + lax.broadcasted_iota(jnp.int32, (width, QB), 1)
        allowed = (key_at >= start_ref[0, block : block + 1, :]) & (key_at <= query_at)
        allowed = jnp.concatenate([allowed, allowed], axis=1)
        queries, grads = q_st[block], g_st[block]
        scores = jnp.where(allowed, matmul(k_low[keys], queries, 1, 1), MASK_VALUE)
        powers = jnp.exp(scores - jnp.max(scores, axis=0, keepdims=True))
        probs = powers * (1.0 / jnp.sum(powers, axis=0, keepdims=True))
        probs_low = probs.astype(LOW)
        prob_grad = matmul(v_low[keys], grads, 1, 1)
        row_dot = jnp.sum(probs * prob_grad, axis=0, keepdims=True)
        score_grad = (probs * (prob_grad - row_dot)).astype(LOW)
        dv_sum[keys] += matmul(probs_low, grads, 1, 0)
        dk_sum[keys] += matmul(score_grad, queries, 1, 0)
        turned = matmul(v_turn[:, keys], probs_low, 1, 0)
        core, y = where_is(block // per_part)
        here = slice((block % per_part) * QB, (block % per_part + 1) * QB)
        att_ref[core, y, 0, here, :] = jnp.where(upper, turned[:, :QB], turned[:, QB:]).T.astype(LOW)
        turned = matmul(k_turn[:, keys], score_grad, 1, 0)
        dq_sum[rows, :] = jnp.where(upper, turned[:, :QB], turned[:, QB:]).T
    totals = [jnp.zeros((1, pair), FULL)] * 3
    for part in range(parts):
        core, y = where_is(part)
        rows = slice(part * part_rows, (part + 1) * part_rows)
        cosine, sine = cos_ref[rows, :], sin_ref[rows, :]
        dq, dk = dq_sum[rows, :] * scale, dk_sum[rows, :]
        grads = (
            dq * cosine - partner(dq) * sine,
            dk * cosine - partner(dk) * sine,
            dv_sum[rows, :],
        )
        for at, grad in enumerate(grads):
            dqkv_ref[core, y, 0, :, at * pair : (at + 1) * pair] = grad.astype(LOW)
            totals[at] = totals[at] + jnp.sum(grad, axis=0, keepdims=True)
    for at, total in enumerate(totals):
        sums_ref[0, :, at * pair : (at + 1) * pair] = total


def attention(projected, grads, starts, place):
    rows, width = projected.shape
    seqs, pair = rows // LEN, 2 * HEAD
    pairs = width // (3 * pair)
    part_rows = rows // 8
    cosine, sine = rotary_lanes()
    table = pl.BlockSpec((LEN, pair), lambda s, h, place: (0, 0))

    def block(columns):
        return pl.BlockSpec((2, 2, 1, part_rows, columns), lambda s, h, place: (0, 0, s, 0, h))

    def view(columns):
        return (2, 2, seqs, part_rows, columns)

    attended, grad, sums = pl.pallas_call(
        attention_kernel,
        grid_spec=pltpu.PrefetchScalarGridSpec(
            num_scalar_prefetch=1,
            grid=(seqs, pairs),
            in_specs=[
                block(3 * pair),
                block(pair),
                pl.BlockSpec((1, LEN // QB, QB), lambda s, h, place: (s, 0, 0)),
                table,
                table,
            ],
            out_specs=[
                block(pair),
                block(3 * pair),
                pl.BlockSpec((1, 1, 3 * pair), lambda s, h, place: (s, 0, h)),
            ],
            scratch_shapes=[
                pltpu.VMEM((LEN // QB, 2 * QB, pair), LOW),
                pltpu.VMEM((LEN // QB, 2 * QB, pair), LOW),
                pltpu.VMEM((LEN, pair), LOW),
                pltpu.VMEM((LEN, pair), LOW),
                pltpu.VMEM((pair, LEN), LOW),
                pltpu.VMEM((pair, LEN), LOW),
                pltpu.VMEM((LEN, pair), FULL),
                pltpu.VMEM((LEN, pair), FULL),
                pltpu.VMEM((LEN, pair), FULL),
            ],
        ),
        out_shape=[
            jax.ShapeDtypeStruct(view(pairs * pair), LOW),
            jax.ShapeDtypeStruct(view(width), LOW),
            jax.ShapeDtypeStruct((seqs, 1, width), FULL),
        ],
        compiler_params=pltpu.CompilerParams(vmem_limit_bytes=40 << 20),
        cost_estimate=pl.CostEstimate(
            flops=seqs * LEN * QB * (BACK + 1) * pair // 8,
            transcendentals=0,
            bytes_accessed=rows * width // 8,
        ),
        name="attention_both_ways",
    )(
        place,
        projected.reshape(view(width)),
        grads.reshape(view(pairs * pair)),
        starts.reshape(seqs, LEN // QB, QB),
        cosine,
        sine,
    )
    return attended.reshape(rows, pairs * pair), grad.reshape(rows, width), sums


def swap(value, axis, bit):
    return lax.ppermute(value, axis, [(i, i ^ bit) for i in range(lax.axis_size(axis))])


def sum_over(value, axis):
    bit = 1
    while bit < lax.axis_size(axis):
        value = value + swap(value, axis, bit)
        bit *= 2
    return value


def normalize_rows(token_rows):
    values = token_rows.astype(FULL)
    centered = values - jnp.mean(values, axis=-1, keepdims=True)
    inv_std = lax.rsqrt(jnp.mean(centered * centered, axis=-1, keepdims=True) + EPSILON)
    return centered * inv_std, inv_std


def row_blocks(columns, rows):
    return pl.BlockSpec((rows, columns), lambda i, *_: (i, 0))


def resident(*shape):
    return pl.BlockSpec(shape, lambda i, *_: (0,) * len(shape), pipeline_mode=pl.Buffered(1))


def like(*shape, dtype=LOW):
    return jax.ShapeDtypeStruct(shape, dtype)


def run_kernel(kernel, steps, in_specs, out_specs, out_shape, name, *operands, scalars=()):
    if scalars:
        scalars = (jnp.stack([jnp.asarray(scalar, jnp.int32) for scalar in scalars]),)
    return pl.pallas_call(
        kernel,
        grid_spec=pltpu.PrefetchScalarGridSpec(
            num_scalar_prefetch=len(scalars),
            grid=(steps,),
            in_specs=in_specs,
            out_specs=out_specs,
        ),
        out_shape=out_shape,
        compiler_params=pltpu.CompilerParams(vmem_limit_bytes=52 << 20),
        cost_estimate=pl.CostEstimate(flops=1 << 24, transcendentals=0, bytes_accessed=1 << 18),
        name=name,
    )(*scalars, *operands)


def whole(*values):
    return [resident(*value.shape) for value in values]


def halves_kernel(low_ref, *refs):
    count = len(refs) // 3
    for source, mine, given in zip(refs[:count], refs[count : 2 * count], refs[2 * count :]):
        columns = mine.shape[1]
        for target, at in ((mine, low_ref[0]), (given, 1 - low_ref[0])):
            target[...] = source[:, pl.ds(pl.multiple_of(at * columns, columns), columns)]


def halves_of(low_at, *weights):
    outs = [like(weight.shape[0], weight.shape[1] // 2) for weight in weights] * 2
    found = run_kernel(
        halves_kernel, 1, whole(*weights), whole(*outs), outs, "halves", *weights, scalars=[low_at]
    )
    return found[: len(weights)], found[len(weights) :]


def heads_halves_kernel(low_ref, q_ref, k_ref, v_ref, dense_ref, mine_ref, given_ref):
    pair = 2 * HEAD
    half = dense_ref.shape[1] // 2
    for target, at in ((mine_ref, low_ref[0]), (given_ref, 1 - low_ref[0])):
        for which in range(half // pair):
            columns = pl.ds(pl.multiple_of(at * half + which * pair, pair), pair)
            for part, source in enumerate((q_ref, k_ref, v_ref)):
                begin = (3 * which + part) * pair
                target[:, begin : begin + pair] = source[:, columns]
        target[:, 3 * half :] = dense_ref[:, pl.ds(pl.multiple_of(at * half, half), half)]


def heads_halves(low_at, qkv_weight, dense_weight):
    operands = (*(qkv_weight[:, part] for part in range(3)), dense_weight)
    out = like(dense_weight.shape[0], 2 * dense_weight.shape[1])
    return run_kernel(
        heads_halves_kernel,
        1,
        whole(*operands),
        whole(out, out),
        [out, out],
        "heads_halves",
        *operands,
        scalars=[low_at],
    )


def shard_kernel(low_ref, mine_ref, got_ref, *shard_refs):
    rows, columns = mine_ref.shape[0], shard_refs[0].shape[1]
    for source, at in ((mine_ref, low_ref[0]), (got_ref, 1 - low_ref[0])):
        for which, shard_ref in enumerate(shard_refs):
            here = slice(which * columns, (which + 1) * columns)
            shard_ref[pl.ds(pl.multiple_of(at * rows, rows), rows), :] = source[:, here]


def shards_of(low_at, mine, got):
    out = like(2 * mine.shape[0], mine.shape[1] // 2)
    return run_kernel(
        shard_kernel,
        1,
        whole(mine, got),
        whole(out, out),
        [out, out],
        "shards",
        mine,
        got,
        scalars=[low_at],
    )


def place_kernel(at_ref, *refs):
    *pieces, full = refs
    rows = pieces[0].shape[0] // 2
    for at, piece in enumerate(pieces):
        slot = 4 * (at_ref[0] ^ (at // 2)) + (at_ref[1] ^ (at % 2))
        for low in (0, 1):
            begin = pl.multiple_of((slot + 2 * low) * rows, rows)
            full[pl.ds(begin, rows), :] = piece[low * rows : (low + 1) * rows, :]


def place_pieces(high_at, x_at, *pieces):
    rows, columns = pieces[0].shape
    steps = 2
    block = pl.BlockSpec((rows, columns // steps), lambda i, *_: (0, i))
    return run_kernel(
        place_kernel,
        steps,
        [block] * 4,
        pl.BlockSpec((4 * rows, columns // steps), lambda i, *_: (0, i)),
        like(4 * rows, columns),
        "place_pieces",
        *pieces,
        scalars=[high_at, x_at],
    )


def from_piece(pieces, use):
    for at, piece in enumerate(pieces):

        @pl.when(pl.program_id(0) == at)
        def _(piece=piece):
            use(piece)


def normalize_kernel(*refs):
    *pieces, gain_ref, shift_ref, normed_ref = refs

    def use(piece):
        x_hat, _ = normalize_rows(piece[...])
        normed_ref[...] = (x_hat * gain_ref[...] + shift_ref[...]).astype(LOW)

    from_piece(pieces, use)


def normalize_all(pieces, gain, shift):
    step, width = pieces[0].shape
    return run_kernel(
        normalize_kernel,
        len(pieces),
        whole(*pieces, gain, shift),
        row_blocks(width, step),
        like(step * len(pieces), width),
        "normalize_all",
        *pieces,
        gain,
        shift,
    )


def stack_kernel(*refs):
    *pieces, whole_ref, sums_ref = refs

    @pl.when(pl.program_id(0) == 0)
    def _():
        sums_ref[...] = jnp.zeros_like(sums_ref)

    def use(piece):
        whole_ref[...] = piece[...]
        sums_ref[...] += jnp.sum(piece[...].astype(FULL), axis=0, keepdims=True)

    from_piece(pieces, use)


def stack_pieces(pieces):
    step, width = pieces[0].shape
    return run_kernel(
        stack_kernel,
        len(pieces),
        whole(*pieces),
        [row_blocks(width, step), resident(1, width)],
        [like(step * len(pieces), width), like(1, width, dtype=FULL)],
        "stack_pieces",
        *pieces,
    )


def column_parts(width, count):
    return [slice(at * width // count, (at + 1) * width // count) for at in range(count)]


def hidden_kernel(normed_ref, *refs):
    *weight_refs, bias_ref, activated_ref, slope_ref = refs
    for weight_ref, here in zip(weight_refs, column_parts(bias_ref.shape[1], len(weight_refs))):
        pre_gelu = matmul(normed_ref[...], weight_ref[...], 1, 0) + bias_ref[:, here]
        value, slope = gelu_both(pre_gelu)
        activated_ref[:, here] = value.astype(LOW)
        slope_ref[:, here] = slope.astype(LOW)


def hidden_forward(normed, weights, bias):
    rows, columns, step = normed.shape[0], bias.shape[1], 256
    return run_kernel(
        hidden_kernel,
        rows // step,
        [row_blocks(normed.shape[1], step), *whole(*weights, bias)],
        [row_blocks(columns, step)] * 2,
        [like(rows, columns)] * 2,
        "hidden_forward",
        normed,
        *weights,
        bias,
    )


def hidden_back_kernel(grad_ref, *refs):
    *weight_refs, slope_ref, pre_grad_ref, sums_ref = refs

    @pl.when(pl.program_id(0) == 0)
    def _():
        sums_ref[...] = jnp.zeros_like(sums_ref)

    for weight_ref, here in zip(weight_refs, column_parts(slope_ref.shape[1], len(weight_refs))):
        pre_grad = matmul(grad_ref[...], weight_ref[...], 1, 0) * slope_ref[:, here].astype(FULL)
        pre_grad_ref[:, here] = pre_grad.astype(LOW)
        sums_ref[:, here] += jnp.sum(pre_grad, axis=0, keepdims=True)


def hidden_back(grad, weights, slope):
    rows, columns, step = grad.shape[0], slope.shape[1], 256
    return run_kernel(
        hidden_back_kernel,
        rows // step,
        [row_blocks(grad.shape[1], step), *whole(*weights), row_blocks(columns, step)],
        [row_blocks(columns, step), resident(1, columns)],
        [like(rows, columns), like(1, columns, dtype=FULL)],
        "hidden_back",
        grad,
        *weights,
        slope,
    )


def heads_kernel(normed_ref, grad_ref, left_ref, right_ref, bias_ref, projected_ref, back_ref):
    columns = left_ref.shape[1]
    split = projected_ref.shape[1] - columns
    projected_ref[:, :columns] = (
        matmul(normed_ref[...], left_ref[...], 1, 0) + bias_ref[:, :columns]
    )
    projected_ref[:, columns:] = (
        matmul(normed_ref[...], right_ref[:, :split], 1, 0) + bias_ref[:, columns:]
    )
    back_ref[...] = matmul(grad_ref[...], right_ref[:, split:], 1, 0).astype(LOW)


def heads_inputs(normed, grad, weights, bias):
    rows, split, step = normed.shape[0], bias.shape[1], 256
    columns = sum(weight.shape[1] for weight in weights) - split
    return run_kernel(
        heads_kernel,
        rows // step,
        [
            row_blocks(normed.shape[1], step),
            row_blocks(grad.shape[1], step),
            *whole(*weights, bias),
        ],
        [row_blocks(split, step), row_blocks(columns, step)],
        [like(rows, split, dtype=FULL), like(rows, columns)],
        "heads_inputs",
        normed,
        grad,
        *weights,
        bias,
    )


def products_of(lefts, rights):
    values = [matmul(left[...], right[...], 0, 0).astype(LOW) for left, right in zip(lefts, rights)]
    return values[0] if len(values) == 1 else jnp.concatenate(values, axis=1)


def weight_grad_kernel(count, x_ref, *refs):
    lefts, rights, outs = refs[:count], refs[count : 2 * count], refs[2 * count :]
    value = products_of(lefts, rights)
    columns = outs[0].shape[1]
    for first, targets in ((True, outs[:2]), (False, outs[2:])):

        @pl.when((pl.program_id(0) < 4) == first)
        def _(targets=targets):
            for which, target in enumerate(targets):
                target[...] = value[:, which * columns : (which + 1) * columns]


def weight_grad(x_at, *products):
    lefts, rights = zip(*products)
    tokens, width = lefts[0].shape
    columns, step = sum(right.shape[1] for right in rights) // 2, width // 8

    def rows_of(i, x_ref):
        return (0, (i % 4) * 2 + jnp.where(i < 4, 1 - x_ref[0], x_ref[0]))

    return run_kernel(
        functools.partial(weight_grad_kernel, len(products)),
        8,
        [pl.BlockSpec((tokens, step), rows_of)] * len(products) + whole(*rights),
        [pl.BlockSpec((step, columns), lambda i, *_: (jnp.minimum(i, 3), 0))] * 2
        + [pl.BlockSpec((step, columns), lambda i, *_: (jnp.maximum(i - 4, 0), 0))] * 2,
        [like(width // 2, columns)] * 4,
        "weight_grad",
        *lefts,
        *rights,
        scalars=[x_at],
    )


def weight_grad_plain_kernel(count, *refs):
    lefts, rights, outs = refs[:count], refs[count : 2 * count], refs[2 * count :]
    value = products_of(lefts, rights)
    for out_ref, here in zip(outs, column_parts(value.shape[1], 2)):
        out_ref[...] = value[:, here]


def weight_grad_plain(*products):
    lefts, rights = zip(*products)
    tokens, width = lefts[0].shape
    columns, step = sum(right.shape[1] for right in rights) // 2, 256
    return run_kernel(
        functools.partial(weight_grad_plain_kernel, len(products)),
        width // step,
        [pl.BlockSpec((tokens, step), lambda i, *_: (0, i))] * len(products) + whole(*rights),
        [row_blocks(columns, step)] * 2,
        [like(width, columns)] * 2,
        "weight_grad",
        *lefts,
        *rights,
    )


def fold_kernel(at_ref, kept_ref, got_ref, mine_ref, given_ref):
    rows = mine_ref.shape[0]
    for target, at in ((mine_ref, at_ref[0]), (given_ref, 1 - at_ref[0])):
        here = pl.ds(pl.multiple_of(at * rows, rows), rows)
        target[...] = (kept_ref[here, :].astype(FULL) + got_ref[here, :].astype(FULL)).astype(LOW)


def fold(at, kept, got):
    out = like(kept.shape[0] // 2, kept.shape[1])
    return run_kernel(
        fold_kernel, 1, whole(kept, got), whole(out, out), [out, out], "fold", kept, got, scalars=[at]
    )


def final_kernel(low_ref, *refs):
    *pairs, out_ref = refs
    columns = pairs[0].shape[1]
    for which in (0, 1):
        for source, at in ((pairs[2 * which], low_ref[0]), (pairs[2 * which + 1], 1 - low_ref[0])):
            begin = pl.multiple_of((2 * at + which) * columns, columns)
            out_ref[:, pl.ds(begin, columns)] = source[...].astype(FULL)


def final_grad(low_at, *pairs):
    out = like(pairs[0].shape[0], 4 * pairs[0].shape[1], dtype=FULL)
    return run_kernel(
        final_kernel, 1, whole(*pairs), resident(*out.shape), out, "final_grad", *pairs, scalars=[low_at]
    )


def final_heads_kernel(low_ref, *refs):
    pairs, (q_ref, k_ref, v_ref, dense_ref) = refs[:4], refs[4:]
    pair = 2 * HEAD
    half = dense_ref.shape[1] // 2
    for own, at in ((0, low_ref[0]), (1, 1 - low_ref[0])):
        source = jnp.concatenate([pairs[own][...], pairs[2 + own][...]], axis=1).astype(FULL)
        for which in range(half // pair):
            columns = pl.ds(pl.multiple_of(at * half + which * pair, pair), pair)
            for part, target in enumerate((q_ref, k_ref, v_ref)):
                begin = (3 * which + part) * pair
                target[:, columns] = source[:, begin : begin + pair]
        dense_ref[:, pl.ds(pl.multiple_of(at * half, half), half)] = source[:, 3 * half :]


def final_heads(low_at, *pairs):
    out = like(pairs[0].shape[0], pairs[0].shape[1], dtype=FULL)
    return run_kernel(
        final_heads_kernel,
        1,
        whole(*pairs),
        whole(*[out] * 4),
        [out] * 4,
        "final_heads",
        *pairs,
        scalars=[low_at],
    )


def sum_of_products(left_refs, right_refs, terms):
    total = None
    for left_at, left_columns, right_at, right_columns in terms:
        product = matmul(left_refs[left_at][:, left_columns], right_refs[right_at][:, right_columns], 1, 1)
        total = product if total is None else total + product
    return total


def far_rows_first(i):
    return jnp.where(i < 4, i + 4, i - 4)


def to_given_or_kept(value, given_ref, kept_ref):
    @pl.when(pl.program_id(0) < 4)
    def _():
        given_ref[...] = value

    @pl.when(pl.program_id(0) >= 4)
    def _():
        kept_ref[...] = value


def branch_kernel(counts, terms, *refs):
    lefts, rights = refs[: counts[0]], refs[counts[0] : sum(counts)]
    total = sum_of_products(lefts, rights, terms)
    to_given_or_kept(total.astype(LOW), *refs[sum(counts) :])


def token_grad_kernel(counts, terms, *refs):
    lefts, rights = refs[: counts[0]], refs[counts[0] : sum(counts)]
    pieces, (given_ref, kept_ref, sums_ref) = refs[sum(counts) : -3], refs[-3:]

    @pl.when(pl.program_id(0) == 0)
    def _():
        sums_ref[...] = jnp.zeros_like(sums_ref)

    grad = sum_of_products(lefts, rights, terms)
    to_given_or_kept(grad.astype(LOW), given_ref, kept_ref)
    sums_ref[1:2, :] += jnp.sum(grad, axis=0, keepdims=True)

    def use(piece):
        x_hat, _ = normalize_rows(piece[...])
        sums_ref[0:1, :] += jnp.sum(grad * x_hat, axis=0, keepdims=True)

    from_piece([*pieces[4:], *pieces[:4]], use)


def over_tokens(kernel, name, lefts, rights, terms, pieces=()):
    rows, width = lefts[0].shape[0], rights[0].shape[0]
    step = rows // 8
    sums = [like(2, width, dtype=FULL)] if pieces else []
    return run_kernel(
        functools.partial(kernel, (len(lefts), len(rights)), terms),
        8,
        [
            pl.BlockSpec((step, left.shape[1]), lambda i, *_: (far_rows_first(i), 0))
            for left in lefts
        ]
        + whole(*rights, *pieces),
        [
            pl.BlockSpec((step, width), lambda i, *_: (jnp.minimum(i, 3), 0)),
            pl.BlockSpec((step, width), lambda i, *_: (jnp.maximum(i - 4, 0), 0)),
            *whole(*sums),
        ],
        [like(rows // 2, width)] * 2 + sums,
        name,
        *lefts,
        *rights,
        *pieces,
    )


def link_kernel(kept_ref, got_ref, left_ref, left_given_ref, right_ref, right_given_ref):
    quarter, columns = left_ref.shape
    part = quarter // 2
    y, low = pl.program_id(0) // 2, pl.program_id(0) % 2
    held = (kept_ref[...].astype(FULL) + got_ref[...].astype(FULL)).astype(LOW)

    for at in range(4):

        @pl.when(pl.program_id(0) == at)
        def _(y=at // 2, low=at % 2):
            left = left_given_ref if y else left_ref
            left[low * part : (low + 1) * part, :] = held[:, :columns]
            right = right_given_ref if low else right_ref
            right[y * part : (y + 1) * part, :] = held[:, columns:]


def link_stage(kept, got):
    rows, width = kept.shape
    out = like(rows // 2, width // 2)
    return run_kernel(
        link_kernel,
        4,
        [row_blocks(width, rows // 4)] * 2,
        whole(*[out] * 4),
        [out] * 4,
        "link_stage",
        kept,
        got,
    )


def last_kernel(left_ref, left_got_ref, right_ref, right_got_ref, *outs):
    rows = outs[0].shape[0]
    pairs = ((left_ref, left_got_ref), (right_ref, right_got_ref))
    for at, (kept_ref, got_ref) in enumerate(pairs):
        total = (kept_ref[...].astype(FULL) + got_ref[...].astype(FULL)).astype(LOW)
        outs[2 * at][...] = total[:rows]
        outs[2 * at + 1][...] = total[rows:]


def last_stage(*values):
    rows, columns = values[0].shape
    out = like(rows // 2, columns)
    return run_kernel(
        last_kernel, 1, whole(*values), whole(*[out] * 4), [out] * 4, "last_stage", *values
    )


def joined(refs):
    left, left_got, right, right_got = (ref[...].astype(FULL) for ref in refs)
    return jnp.concatenate([left + left_got, right + right_got], axis=1)


def output_kernel(*refs):
    tokens_ref, dense_bias_ref, fc2_bias_ref, output_ref = refs[4:]
    total = tokens_ref[...].astype(FULL) + joined(refs[:4])
    output_ref[...] = (total + dense_bias_ref[...] + fc2_bias_ref[...]).astype(LOW)


def input_grad_kernel(*refs):
    tokens_ref, out_grad_ref, gain_ref, grad_ref = refs[4:]
    x_hat, inv_std = normalize_rows(tokens_ref[...])
    scaled = joined(refs[:4]) * gain_ref[...]
    token_grad = inv_std * (
        scaled
        - jnp.mean(scaled, axis=-1, keepdims=True)
        - x_hat * jnp.mean(scaled * x_hat, axis=-1, keepdims=True)
    )
    grad_ref[...] = (out_grad_ref[...].astype(FULL) + token_grad).astype(LOW)


def row_result(kernel, name, *operands):
    out = like(*operands[4].shape)
    return run_kernel(kernel, 1, whole(*operands), resident(*out.shape), out, name, *operands)


def body(
    tokens,
    out_grad,
    segments,
    ln_gain,
    ln_bias,
    qkv_weight,
    qkv_bias,
    dense_weight,
    dense_bias,
    fc1_weight,
    fc1_bias,
    fc2_weight,
    fc2_bias,
):
    low_at, high_at, x_at = lax.axis_index("zl"), lax.axis_index("zh"), lax.axis_index("x")
    t_at = lax.axis_index("t")
    pairwise = lax.axis_size("zh") == 2
    place = jnp.stack([t_at // 2, t_at % 2]).astype(jnp.int32)
    weight_rows = qkv_weight.shape[0]
    pair = 2 * HEAD
    half = dense_weight.shape[1] // 2
    pairs = half // pair
    hidden = fc1_weight.shape[1] // 2

    before = [()]

    def sync(*values):
        before[0] = lax.optimization_barrier((values, before[0]))[0]
        return before[0]

    def to_low(value):
        return swap(value, "zl", 1)

    def to_high(value):
        return swap(value, "zh", 1)

    def to_x(value):
        return swap(value, "x", 1)

    def to_y(value):
        return swap(value, "t", 2)

    def to_core(value):
        return swap(value, "t", 1)

    class Gather:
        def __init__(self, shard):
            self.own = shard
            self.moving = []

        def start(self):
            if pairwise:
                self.moving = [to_high(self.own), to_x(self.own)]
            else:
                rows, columns = self.own.shape
                gathered = lax.all_gather(self.own, ("zh", "x"), axis=0, tiled=True)
                natural = gathered.reshape(-1, 2, 2, rows // 2, columns).transpose(0, 2, 1, 3, 4)
                self.moving = [natural.reshape(-1, columns)]

        def forward(self):
            if pairwise:
                self.high, self.x = self.moving
                self.moving = [to_x(self.high)]

        def whole(self):
            if pairwise:
                return place_pieces(high_at, x_at, self.own, self.x, self.high, self.moving[0])
            return self.moving[0]

    class Sum:
        def __init__(self, given, kept):
            self.given, self.kept = given, kept
            self.moving = []

        def start(self):
            if pairwise:
                self.moving = [to_x(self.given)]
            else:
                rows, columns = self.given.shape
                blocks = self.given.reshape(-1, 2, 2, weight_rows, columns)
                ordered = blocks.transpose(0, 2, 1, 3, 4).reshape(rows, columns)
                self.moving = [
                    lax.psum_scatter(ordered, ("zh", "x"), scatter_dimension=0, tiled=True)
                ]

        def second(self):
            if pairwise:
                self.kept, given = fold(high_at, self.kept, self.moving[0])
                self.moving = [to_high(given)]

        def third(self):
            other = self.kept if pairwise else jnp.zeros_like(self.moving[0])
            self.kept, given = fold(low_at, other, self.moving[0])
            self.moving = [to_low(given)]

        def halves(self):
            return [self.kept, self.moving[0]]

    def segment(values, *transfers):
        tied = sync(*values, *[piece for transfer in transfers for piece in transfer.moving])
        at = len(values)
        for transfer in transfers:
            many = len(transfer.moving)
            transfer.moving = list(tied[at : at + many])
            at += many
        return tied[: len(values)]

    def gathers_of(mine, got):
        return [Gather(shard) for shard in sync(*shards_of(low_at, mine, got))]

    def sums_of(*products):
        if pairwise:
            given_a, given_b, kept_a, kept_b = weight_grad(x_at, *products)
        else:
            given_a, given_b = weight_grad_plain(*products)
            kept_a = kept_b = given_a
        return [given_a, given_b, kept_a, kept_b]

    def as_sums(tied):
        return [Sum(tied[0], tied[2]), Sum(tied[1], tied[3])]

    (fc1_mine,), (fc1_given,) = halves_of(low_at, fc1_weight)
    fc1_given, tokens, out_grad, segments, qkv_weight, dense_weight, fc2_weight = sync(
        fc1_given, tokens, out_grad, segments, qkv_weight, dense_weight, fc2_weight
    )
    got = to_low(fc1_given)
    tokens_core, grad_core = to_core(tokens), to_core(out_grad)
    heads_mine, heads_given = heads_halves(low_at, qkv_weight, dense_weight)
    (fc2_mine,), (fc2_given,) = halves_of(low_at, fc2_weight)
    got, tokens_core, grad_core, heads_given, fc2_given, tokens, out_grad, segments = sync(
        got, tokens_core, grad_core, heads_given, fc2_given, tokens, out_grad, segments
    )
    fc1_a, fc1_b = gathers_of(fc1_mine, got)
    tokens, out_grad, segments, heads_given, fc2_given = sync(
        tokens, out_grad, segments, heads_given, fc2_given
    )
    fc1_a.start()
    tokens_low, tokens_y, segments_low = to_low(tokens), to_y(tokens), to_low(segments)
    tokens_low, tokens_y, segments_low, heads_given, fc1_b.own, fc2_given, out_grad = segment(
        [tokens_low, tokens_y, segments_low, heads_given, fc1_b.own, fc2_given, out_grad], fc1_a
    )
    fc1_a.forward()
    fc1_b.start()
    tokens_both, got = to_y(tokens_low), to_low(heads_given)
    tokens_low_core, tokens_y_core = to_core(tokens_low), to_core(tokens_y)
    all_segments = jnp.concatenate([segments, segments_low])
    starts = jnp.sum(
        (all_segments[:, None, :] < all_segments[:, :, None]).astype(jnp.int32), axis=2
    )
    tokens_both, got, tokens_low_core, tokens_y_core, starts, fc2_given, out_grad = segment(
        [tokens_both, got, tokens_low_core, tokens_y_core, starts, fc2_given, out_grad],
        fc1_a,
        fc1_b,
    )
    tokens_both_core = to_core(tokens_both)
    shards = shards_of(low_at, heads_mine, got)
    tokens_both_core, fc2_given, out_grad, *shards = sync(
        tokens_both_core, fc2_given, out_grad, *shards
    )
    heads_a, heads_b = (Gather(shard) for shard in shards)
    fc1_b.forward()
    heads_a.start()
    grad_low, grad_y = to_low(out_grad), to_y(out_grad)
    token_pieces = [
        tokens,
        tokens_low,
        tokens_y,
        tokens_both,
        tokens_core,
        tokens_low_core,
        tokens_y_core,
        tokens_both_core,
    ]
    all_normed = normalize_all(token_pieces, ln_gain[None], ln_bias[None])
    fc1_full = [fc1_a.whole()]
    all_normed, fc1_full[0], grad_low, grad_y, heads_b.own, fc2_given = segment(
        [all_normed, fc1_full[0], grad_low, grad_y, heads_b.own, fc2_given], fc1_b, heads_a
    )
    heads_a.forward()
    heads_b.start()
    grad_both, got = to_y(grad_low), to_low(fc2_given)
    grad_low_core, grad_y_core = to_core(grad_low), to_core(grad_y)
    fc1_full.append(fc1_b.whole())
    bias = lax.dynamic_slice_in_dim(fc1_bias, low_at * hidden, hidden, 0)[None]
    activated, slope = hidden_forward(all_normed, fc1_full, bias)
    activated, slope, grad_both, got, grad_low_core, grad_y_core = segment(
        [activated, slope, grad_both, got, grad_low_core, grad_y_core], heads_a, heads_b
    )
    grad_both_core = to_core(grad_both)
    grad_both_core, *shards = sync(grad_both_core, *shards_of(low_at, fc2_mine, got))
    fc2_a, fc2_b = (Gather(shard) for shard in shards)
    heads_b.forward()
    fc2_a.start()
    all_grad, grad_sums = stack_pieces(
        [
            out_grad,
            grad_low,
            grad_y,
            grad_both,
            grad_core,
            grad_low_core,
            grad_y_core,
            grad_both_core,
        ]
    )
    heads_full = [heads_a.whole()]
    all_grad, heads_full[0], *partials, fc2_b.own = segment(
        [all_grad, heads_full[0], *sums_of((all_grad, activated)), fc2_b.own], heads_b, fc2_a
    )
    d_fc2_a, d_fc2_b = as_sums(partials)
    fc2_a.forward()
    fc2_b.start()
    heads_full.append(heads_b.whole())
    bias = lax.dynamic_slice_in_dim(qkv_bias, low_at * half, half, 1)
    bias = bias.reshape(3, pairs, pair).transpose(1, 0, 2).reshape(1, 3 * half)
    projected, back = heads_inputs(all_normed, all_grad, heads_full, bias)
    projected, back, d_fc2_a.given, d_fc2_b.given = segment(
        [projected, back, d_fc2_a.given, d_fc2_b.given], fc2_a, fc2_b
    )
    fc2_b.forward()
    d_fc2_a.start()
    attended, qkv_grad, qkv_sums = attention(projected, back, starts, place)
    fc2_full = [fc2_a.whole()]
    attended, qkv_grad, qkv_sums, fc2_full[0], d_fc2_b.given = segment(
        [attended, qkv_grad, qkv_sums, fc2_full[0], d_fc2_b.given], fc2_b, d_fc2_a
    )
    d_fc2_b.start()
    d_fc2_a.second()
    fc2_full.append(fc2_b.whole())
    partials = sums_of((all_normed, qkv_grad), (all_grad, attended))
    fc2_full[1], *partials = segment([fc2_full[1], *partials], d_fc2_a, d_fc2_b)
    d_heads_a, d_heads_b = as_sums(partials)
    d_heads_a.start()
    d_fc2_b.second()
    d_fc2_a.third()
    columns = heads_full[0].shape[1]
    first, second = slice(0, columns), slice(columns, 2 * columns)
    qkv_end = 3 * half - columns
    everything = slice(None)
    given, branch_kept = over_tokens(
        branch_kernel,
        "branch",
        [attended, activated],
        [heads_full[1], *fc2_full],
        [
            (0, everything, 0, slice(qkv_end, columns)),
            (1, first, 1, everything),
            (1, second, 2, everything),
        ],
    )
    given, branch_kept, d_heads_b.given = segment(
        [given, branch_kept, d_heads_b.given], d_heads_a, d_fc2_a, d_fc2_b
    )
    d_heads_b.start()
    d_heads_a.second()
    d_fc2_b.third()
    branch_got = to_core(given)
    pre_grad, pre_sums = hidden_back(all_grad, fc2_full, slope)
    pre_grad, pre_sums, branch_got = segment(
        [pre_grad, pre_sums, branch_got], d_heads_a, d_heads_b, d_fc2_b
    )
    d_heads_b.second()
    d_heads_a.third()
    left, left_given, right, right_given = link_stage(branch_kept, branch_got)
    branch_state = [left, to_y(left_given), right, to_low(right_given)]
    partials = sums_of((all_normed, pre_grad))
    *partials, left, left_got, right, right_got = segment(
        [*partials, *branch_state], d_heads_a, d_heads_b
    )
    d_fc1_a, d_fc1_b = as_sums(partials)
    d_fc1_a.start()
    d_heads_b.third()
    left, left_given, right, right_given = last_stage(left, left_got, right, right_got)
    branch_state = [left, to_low(left_given), right, to_y(right_given)]
    given, kept, norm_sums = over_tokens(
        token_grad_kernel,
        "token_grad",
        [qkv_grad, pre_grad],
        [*heads_full, *fc1_full],
        [
            (0, first, 0, everything),
            (0, slice(columns, 3 * half), 1, slice(0, qkv_end)),
            (1, first, 2, everything),
            (1, second, 3, everything),
        ],
        token_pieces,
    )
    given, kept, norm_sums, d_fc1_b.given, *branch_state = segment(
        [given, kept, norm_sums, d_fc1_b.given, *branch_state], d_fc1_a, d_heads_b
    )
    d_fc1_b.start()
    d_fc1_a.second()
    got, sums = to_core(given), norm_sums.reshape(2 * D)
    sums_got = to_core(sums)
    output = row_result(
        output_kernel, "output", *branch_state, tokens, dense_bias[None], fc2_bias[None]
    )
    fc2_weight_grad = final_grad(low_at, *d_fc2_a.halves(), *d_fc2_b.halves())
    q, k, v, dense_weight_grad = final_heads(low_at, *d_heads_a.halves(), *d_heads_b.halves())
    got, sums, sums_got, output, fc2_weight_grad, q, k, v, dense_weight_grad = segment(
        [got, sums, sums_got, output, fc2_weight_grad, q, k, v, dense_weight_grad],
        d_fc1_a,
        d_fc1_b,
    )
    left, left_given, right, right_given = link_stage(kept, got)
    grad_state = [left, to_y(left_given), right, to_low(right_given)]
    d_fc1_b.second()
    d_fc1_a.third()
    sums = sums + sums_got
    sums_got = to_y(sums)
    sums, sums_got, *grad_state = segment([sums, sums_got, *grad_state], d_fc1_a, d_fc1_b)
    left, left_given, right, right_given = last_stage(*grad_state)
    grad_state = [left, to_low(left_given), right, to_y(right_given)]
    d_fc1_b.third()
    sums = sums + sums_got
    sums_got = to_low(sums)
    sums, sums_got, *grad_state = segment([sums, sums_got, *grad_state], d_fc1_b)
    here = jnp.concatenate([jnp.sum(qkv_sums, axis=(0, 1)), pre_sums[0]])
    sums = jnp.concatenate([sums + sums_got, grad_sums[0], here])
    bias_got = to_low(here)
    sums = sum_over(sum_over(jnp.concatenate([sums, bias_got]), "zh"), "x")
    input_grad = row_result(
        input_grad_kernel, "input_grad", *grad_state, tokens, out_grad, ln_gain[None]
    )
    fc1_weight_grad = final_grad(low_at, *d_fc1_a.halves(), *d_fc1_b.halves())
    both = sums[3 * D :].reshape(2, here.shape[0])
    both = jnp.where(low_at == 0, both, both[::-1])
    qkv_bias_grad = (
        both[:, : 3 * half].reshape(2, pairs, 3, pair).transpose(2, 0, 1, 3).reshape(3, 2 * half)
    )
    return (
        output,
        input_grad,
        sums[:D],
        sums[D : 2 * D],
        jnp.stack([q, k, v], axis=1),
        qkv_bias_grad,
        dense_weight_grad,
        sums[2 * D : 3 * D],
        fc1_weight_grad,
        both[:, 3 * half :].reshape(2 * hidden),
        fc2_weight_grad,
        sums[2 * D : 3 * D],
    )


def solution(mesh):
    dp, tensor = mesh.shape["dp"], mesh.shape["tensor"]
    rows = ("zh", "zl", "x")
    everywhere = (*rows, "t")
    split = Mesh(np.asarray(mesh.devices).reshape(dp // 4, 2, 2, tensor), everywhere)
    return jax.shard_map(
        body,
        mesh=split,
        in_specs=(
            P(everywhere, None),
            P(everywhere, None),
            P(rows, None),
            P(),
            P(),
            P(rows, None, "t"),
            P(None, "t"),
            P(rows, "t"),
            P(),
            P(rows, "t"),
            P("t"),
            P(rows, "t"),
            P(),
        ),
        out_specs=(
            P(everywhere, None),
            P(everywhere, None),
            P(),
            P(),
            P(rows, None, "t"),
            P(None, "t"),
            P(rows, "t"),
            P(),
            P(rows, "t"),
            P("t"),
            P(rows, "t"),
            P(),
        ),
        check_vma=False,
    )
```

time: 834 us -> 574 us (0.69)
  waiting for transfers between devices: 489 us -> 198 us
  Pallas kernels: 20.9 us -> 258 us
  matrix products: 152 us -> 0 us
  local copies, waits for them, and re-layouts: 84.1 us -> 26.2 us
  starting transfers between devices: 22.5 us -> 75.3 us
  other arithmetic: 43.8 us -> 3.88 us
  between operations: 15.4 us -> 1.62 us
    all_gather x5 -> x0, waiting for transfers between devices: 259 us -> none  [the longest x3 154 us: body(): lax.all_gather(share_over_x(halves, x_at), 'z', axis=0, tiled=True)]
    pallas_call x1 -> x44, Pallas kernels: 20.9 us -> 258 us  [the longest x43 236 us: run_kernel(): pl.pallas_call(kernel, grid_spec=pltpu.PrefetchScalarGridSpec(num_scalar_...]
    dot_general x12 -> x0, matrix products: 152 us -> none  [matmul(): lax.dot_general(left, right, (((left_dim,), (right_dim,)), ((), ())), pre...]
    ppermute x21 -> x70, starting transfers between devices: 22 us -> 75.3 us  [swap(): lax.ppermute(value, axis, [(i, i ^ bit) for i in range(lax.axis_size(axis...]
    ppermute x21 -> x70, waiting for transfers between devices: 229 us -> 198 us  [swap(): lax.ppermute(value, axis, [(i, i ^ bit) for i in range(lax.axis_size(axis...]
    unnamed x92 -> x130, local copies, waits for them, and re-layouts: 40.8 us -> 23.4 us
    convert_element_type x8 -> x0, other arithmetic: 16.3 us -> none  [the longest x3 7.71 us: reduce_over_z(): blocks = blocks.astype(LOW)]
    dynamic_slice x11 -> x1, local copies, waits for them, and re-layouts: 12 us -> 0.01 us  [body(): bias = lax.dynamic_slice_in_dim(fc1_bias, low_at * hidden, hidden, 0)[None]]
  transfers between devices with their start and end apart: 28 -> 70, of which waited for: 15 -> 22; matrix products, arithmetic and copies ran while one was open for 28% -> 1% of each run, Pallas kernels for 3% -> 42%
where the time goes in v2:
time: 574 us; the launch traced here: 563 us
  Pallas kernels  258 us (45%)
  waiting for transfers between devices  198 us (34%)
  starting transfers between devices  75.3 us (13%)
  local copies, waits for them, and re-layouts  26.2 us (5%)
    pallas_call x43, Pallas kernels, run_kernel(): pl.pallas_call(kernel, grid_spec=pltpu.PrefetchScalarGridSpec(num_scalar_...  236 us
    ppermute x70, waiting for transfers between devices, swap(): lax.ppermute(value, axis, [(i, i ^ bit) for i in range(lax.axis_size(axis...  198 us
    ppermute x70, starting transfers between devices, swap(): lax.ppermute(value, axis, [(i, i ^ bit) for i in range(lax.axis_size(axis...  75.3 us
    unnamed x130, local copies, waits for them, and re-layouts  23.4 us
    pallas_call x1, Pallas kernels, attention(): pl.pallas_call(attention_kernel, grid_spec=pltpu.PrefetchScalarGridSpec(n...  22 us
  transfers between devices with their start and end apart: 70, of which 22 were waited for; matrix products, arithmetic and copies ran while one was open for 1% of the time, Pallas kernels for 42%

profile of v2, /device:TPU:0, one launch (start us, length us, event | category | flops | bytes accessed | tf_op | source)
XLA Modules:
  0.0 562.9 jit_solution(4345354244890961525)
XLA Ops:
  10.8 7.0 %collective-permute-done.got_ref = bf16[256,1024]{1,0:T(8,128)(2,1)S(1)} collective-permute-done((bf16[256,1024]{1,0:T(8,128)(2,1)S(1)}, bf16[256,1024]{1,0:T(8,128)(2,1)S(1)}, u32[]{:S(2)}, u32[]{:S(2)}) %collective-permute-start) | collective-permute-done | bytes 524320 | tf_op jit(solution)/shard_map/ppermute | solution.py:213
  28.8 27.4 %collective-permute-done.5 = s32[1,1024]{1,0:T(1,128)S(1)} collective-permute-done((s32[1,1024]{1,0:T(1,128)S(1)}, s32[1,1024]{1,0:T(1,128)S(1)}, u32[]{:S(2)}, u32[]{:S(2)}) %collective-permute-start.5) | collective-permute-done | bytes 4128 | tf_op jit(solution)/shard_map/ppermute | solution.py:213
  63.8 6.2 %collective-permute-done.9.got_ref = bf16[256,1024]{1,0:T(8,128)(2,1)S(1)} collective-permute-done((bf16[256,1024]{1,0:T(8,128)(2,1)}, bf16[256,1024]{1,0:T(8,128)(2,1)S(1)}, u32[]{:S(2)}, u32[]{:S(2)}) %collective-permute-start.9) | collective-permute-done | bytes 524320 | tf_op jit(solution)/shard_map/ppermute | solution.py:213
  74.5 19.3 %collective-permute-done.13.refs_2_ = bf16[512,512]{1,0:T(8,128)(2,1)} collective-permute-done((bf16[512,512]{1,0:T(8,128)(2,1)S(1)}, bf16[512,512]{1,0:T(8,128)(2,1)}, u32[]{:S(2)}, u32[]{:S(2)}) %collective-permute-start.13) | collective-permute-done | bytes 524320 | tf_op jit(solution)/shard_map/ppermute | solution.py:213
  100.6 3.3 collective-permute-start.19
  110.8 11.2 %normalize_all.1.normed_ref.refs_0_ = bf16[2048,2048]{1,0:T(8,128)(2,1)} custom-call(bf16[256,2048]{1,0:T(8,128)(2,1)S(1)} %copy-done.2, bf16[256,2048]{1,0:T(8,128)(2,1)} %copy-done.34, bf16[256,2048]{1,0:T(8,128)(2,1)} %copy-done.35, bf16[256,2048]{1,0:T(8,128)(2,1)} %copy-done.36, bf16[256,2048]{1,0:T(8,128)(2,1)} %copy-done.33, ...), custom_call_target="tpu_custom_call" | custom-call | flops 16777216 | bytes 262144 | tf_op jit(solution)/shard_map/normalize_all/pallas_call | solution.py:246
  121.9 9.9 %collective-permute-done.19.refs_2_ = bf16[512,512]{1,0:T(8,128)(2,1)} collective-permute-done((bf16[512,512]{1,0:T(8,128)(2,1)}, bf16[512,512]{1,0:T(8,128)(2,1)}, u32[]{:S(2)}, u32[]{:S(2)}) %collective-permute-start.19) | collective-permute-done | bytes 524320 | tf_op jit(solution)/shard_map/ppermute | solution.py:213
  139.4 7.9 %collective-permute-done.22.got_ref = bf16[256,1024]{1,0:T(8,128)(2,1)S(1)} collective-permute-done((bf16[256,1024]{1,0:T(8,128)(2,1)S(1)}, bf16[256,1024]{1,0:T(8,128)(2,1)S(1)}, u32[]{:S(2)}, u32[]{:S(2)}) %collective-permute-start.22) | collective-permute-done | bytes 524320 | tf_op jit(solution)/shard_map/ppermute | solution.py:213
  154.6 18.5 %hidden_forward.1 = (bf16[2048,1024]{1,0:T(8,128)(2,1)}, bf16[2048,1024]{1,0:T(8,128)(2,1)}) custom-call(bf16[2048,2048]{1,0:T(8,128)(2,1)} %normalize_all.1.normed_ref.refs_0_, bf16[2048,512]{1,0:T(8,128)(2,1)} %place_pieces.6.refs_0_.refs_4_, bf16[2048,512]{1,0:T(8,128)(2,1)} %place_pieces.7.refs_1_.refs_5_, f32[1,1024]{1,0:T(1,128)S(1)} %bitcast.53), custom_call_target="tpu_custom_call" | custom-call | flops 16777216 | bytes 262144 | tf_op jit(solution)/shard_map/hidden_forward/pallas_call | solution.py:246
  181.7 8.7 %stack_pieces.1 = (bf16[2048,2048]{1,0:T(8,128)(2,1)}, f32[1,2048]{1,0:T(1,128)S(1)}) custom-call(bf16[256,2048]{1,0:T(8,128)(2,1)S(1)} %copy-done.5, bf16[256,2048]{1,0:T(8,128)(2,1)} %collective-permute-done.16.refs_1_, bf16[256,2048]{1,0:T(8,128)(2,1)} %collective-permute-done.17.refs_2_, bf16[256,2048]{1,0:T(8,128)(2,1)} %collective-permute-done.21.refs_3_, ...), custom_call_target="tpu_custom_call" | custom-call | flops 16777216 | bytes 262144 | tf_op jit(solution)/shard_map/stack_pieces/pallas_call | solution.py:246
  190.5 14.6 %weight_grad.3 = (bf16[1024,512]{1,0:T(8,128)(2,1)}, bf16[1024,512]{1,0:T(8,128)(2,1)}, bf16[1024,512]{1,0:T(8,128)(2,1)}, bf16[1024,512]{1,0:T(8,128)(2,1)}) custom-call(s32[1]{0:T(128)} %bitcast.9.x_ref, bf16[2048,2048]{1,0:T(8,128)(2,1)} %get-tuple-element.338.refs_0_.grad_ref.refs_1_, bf16[2048,1024]{1,0:T(8,128)(2,1)} %get-tuple-element.325.refs_1_), custom_call_target="tpu_custom_call" | custom-call | flops 16777216 | bytes 262144 | tf_op jit(solution)/shard_map/weight_grad/pallas_call | solution.py:246
  212.7 16.0 %heads_inputs.1 = (f32[2048,768]{1,0:T(8,128)}, bf16[2048,256]{1,0:T(8,128)(2,1)S(1)}) custom-call(bf16[2048,2048]{1,0:T(8,128)(2,1)} %normalize_all.1.normed_ref.refs_0_, bf16[2048,2048]{1,0:T(8,128)(2,1)} %get-tuple-element.338.refs_0_.grad_ref.refs_1_, bf16[2048,512]{1,0:T(8,128)(2,1)} %place_pieces.8.left_ref.refs_2_, ...), custom_call_target="tpu_custom_call" | custom-call | flops 16777216 | bytes 262144 | tf_op jit(solution)/shard_map/heads_inputs/pallas_call | solution.py:246
  228.7 3.7 collective-permute-done.33.refs_2_
  242.4 22.0 %attention_both_ways.1 = (bf16[2,2,2,256,256]{4,3,2,1,0:T(8,128)(2,1)S(1)}, bf16[2,2,2,256,768]{4,3,2,1,0:T(8,128)(2,1)S(1)}, f32[2,1,768]{2,1,0:T(1,128)S(1)}) custom-call(s32[2]{0:T(128)S(1)} %pad_add_fusion.1.place_ref, f32[2,2,2,256,768]{4,3,2,1,0:T(8,128)S(1)} %bitcast.45, bf16[2,2,2,256,256]{4,3,2,1,0:T(8,128)(2,1)S(1)} %bitcast.48, ...), custom_call_target="tpu_custom_call" | custom-call | flops 16777216 | bytes 196608 | tf_op jit(solution)/shard_map/attention_both_ways/pallas_call | solution.py:160
  274.2 16.1 %weight_grad.4 = (bf16[1024,512]{1,0:T(8,128)(2,1)S(1)}, bf16[1024,512]{1,0:T(8,128)(2,1)}, bf16[1024,512]{1,0:T(8,128)(2,1)}, bf16[1024,512]{1,0:T(8,128)(2,1)}) custom-call(s32[1]{0:T(128)} %bitcast.9.x_ref, bf16[2048,2048]{1,0:T(8,128)(2,1)} %normalize_all.1.normed_ref.refs_0_, bf16[2048,2048]{1,0:T(8,128)(2,1)} %get-tuple-element.338.refs_0_.grad_ref.refs_1_, ...), custom_call_target="tpu_custom_call" | custom-call | flops 16777216 | bytes 262144 | tf_op jit(solution)/shard_map/weight_grad/pallas_call | solution.py:246
  290.4 4.4 collective-permute-done.37.got_ref
  299.5 17.9 %branch.1 = (bf16[1024,2048]{1,0:T(8,128)(2,1)}, bf16[1024,2048]{1,0:T(8,128)(2,1)}) custom-call(bf16[2048,256]{1,0:T(8,128)(2,1)S(1)} %bitcast.47, bf16[2048,1024]{1,0:T(8,128)(2,1)} %get-tuple-element.325.refs_1_, bf16[2048,512]{1,0:T(8,128)(2,1)} %place_pieces.9.right_ref.refs_2_.refs_3_, bf16[2048,512]{1,0:T(8,128)(2,1)} %place_pieces.10.refs_0_.refs_3_, ...), custom_call_target="tpu_custom_call" | custom-call | flops 16777216 | bytes 262144 | tf_op jit(solution)/shard_map/branch/pallas_call | solution.py:246
  317.5 4.5 collective-permute-done.41.got_ref
  326.7 14.7 %hidden_back.1 = (bf16[2048,1024]{1,0:T(8,128)(2,1)}, f32[1,1024]{1,0:T(1,128)S(1)}) custom-call(bf16[2048,2048]{1,0:T(8,128)(2,1)} %get-tuple-element.338.refs_0_.grad_ref.refs_1_, bf16[2048,512]{1,0:T(8,128)(2,1)} %place_pieces.10.refs_0_.refs_3_, bf16[2048,512]{1,0:T(8,128)(2,1)} %place_pieces.11.refs_1_.refs_4_, ...), custom_call_target="tpu_custom_call" | custom-call | flops 16777216 | bytes 262144 | tf_op jit(solution)/shard_map/hidden_back/pallas_call | solution.py:246
  342.1 7.2 %collective-permute-done.43.got_ref = bf16[512,512]{1,0:T(8,128)(2,1)S(1)} collective-permute-done((bf16[512,512]{1,0:T(8,128)(2,1)S(1)}, bf16[512,512]{1,0:T(8,128)(2,1)S(1)}, u32[]{:S(2)}, u32[]{:S(2)}) %collective-permute-start.43) | collective-permute-done | bytes 524320 | tf_op jit(solution)/shard_map/ppermute | solution.py:213
  349.4 7.0 %link_stage.2 = (bf16[512,1024]{1,0:T(8,128)(2,1)S(1)}, bf16[512,1024]{1,0:T(8,128)(2,1)}, bf16[512,1024]{1,0:T(8,128)(2,1)}, bf16[512,1024]{1,0:T(8,128)(2,1)}) custom-call(bf16[1024,2048]{1,0:T(8,128)(2,1)} %get-tuple-element.393.kept_ref, bf16[1024,2048]{1,0:T(8,128)(2,1)} %collective-permute-done.42.got_ref), custom_call_target="tpu_custom_call" | custom-call | flops 16777216 | bytes 262144 | tf_op jit(solution)/shard_map/link_stage/pallas_call | solution.py:246
  364.4 14.5 %weight_grad.5 = (bf16[1024,512]{1,0:T(8,128)(2,1)S(1)}, bf16[1024,512]{1,0:T(8,128)(2,1)}, bf16[1024,512]{1,0:T(8,128)(2,1)}, bf16[1024,512]{1,0:T(8,128)(2,1)}) custom-call(s32[1]{0:T(128)} %bitcast.9.x_ref, bf16[2048,2048]{1,0:T(8,128)(2,1)} %normalize_all.1.normed_ref.refs_0_, bf16[2048,1024]{1,0:T(8,128)(2,1)} %get-tuple-element.395.refs_1_), custom_call_target="tpu_custom_call" | custom-call | flops 16777216 | bytes 262144 | tf_op jit(solution)/shard_map/weight_grad/pallas_call | solution.py:246
  378.9 22.1 %collective-permute-done.48.refs_1_ = bf16[256,512]{1,0:T(8,128)(2,1)S(1)} collective-permute-done((bf16[256,512]{1,0:T(8,128)(2,1)S(1)}, bf16[256,512]{1,0:T(8,128)(2,1)S(1)}, u32[]{:S(2)}, u32[]{:S(2)}) %collective-permute-start.48) | collective-permute-done | bytes 262176 | tf_op jit(solution)/shard_map/ppermute | solution.py:213
  408.0 32.3 %token_grad.1 = (bf16[1024,2048]{1,0:T(8,128)(2,1)}, bf16[1024,2048]{1,0:T(8,128)(2,1)}, f32[2,2048]{1,0:T(2,128)S(1)}) custom-call(bf16[2048,768]{1,0:T(8,128)(2,1)} %bitcast.44, bf16[2048,1024]{1,0:T(8,128)(2,1)} %get-tuple-element.395.refs_1_, bf16[2048,512]{1,0:T(8,128)(2,1)} %place_pieces.8.left_ref.refs_2_, ...), custom_call_target="tpu_custom_call" | custom-call | flops 16777216 | bytes 262144 | tf_op jit(solution)/shard_map/token_grad/pallas_call | solution.py:246
  450.8 18.9 %collective-permute-done.56.got_ref = bf16[512,512]{1,0:T(8,128)(2,1)S(1)} collective-permute-done((bf16[512,512]{1,0:T(8,128)(2,1)S(1)}, bf16[512,512]{1,0:T(8,128)(2,1)S(1)}, u32[]{:S(2)}, u32[]{:S(2)}) %collective-permute-start.56) | collective-permute-done | bytes 524320 | tf_op jit(solution)/shard_map/ppermute | solution.py:213
  469.7 7.2 %link_stage.3 = (bf16[512,1024]{1,0:T(8,128)(2,1)S(1)}, bf16[512,1024]{1,0:T(8,128)(2,1)}, bf16[512,1024]{1,0:T(8,128)(2,1)}, bf16[512,1024]{1,0:T(8,128)(2,1)}) custom-call(bf16[1024,2048]{1,0:T(8,128)(2,1)} %get-tuple-element.449.kept_ref, bf16[1024,2048]{1,0:T(8,128)(2,1)} %collective-permute-done.54.got_ref), custom_call_target="tpu_custom_call" | custom-call | flops 16777216 | bytes 262144 | tf_op jit(solution)/shard_map/link_stage/pallas_call | solution.py:246
  485.1 18.6 %collective-permute-done.58 = f32[4096]{0:T(1024)S(1)} collective-permute-done((f32[4096]{0:T(1024)S(1)}, f32[4096]{0:T(1024)S(1)}, u32[]{:S(2)}, u32[]{:S(2)}) %collective-permute-start.58) | collective-permute-done | bytes 16416 | tf_op jit(solution)/shard_map/ppermute | solution.py:213
  503.6 18.0 %collective-permute-done.61.refs_1_ = bf16[256,512]{1,0:T(8,128)(2,1)S(1)} collective-permute-done((bf16[256,512]{1,0:T(8,128)(2,1)S(1)}, bf16[256,512]{1,0:T(8,128)(2,1)S(1)}, u32[]{:S(2)}, u32[]{:S(2)}) %collective-permute-start.61) | collective-permute-done | bytes 262176 | tf_op jit(solution)/shard_map/ppermute | solution.py:213
  522.9 3.3 last_stage.3
  530.8 14.3 %collective-permute-done.63 = f32[4096]{0:T(1024)S(1)} collective-permute-done((f32[4096]{0:T(1024)S(1)}, f32[4096]{0:T(1024)S(1)}, u32[]{:S(2)}, u32[]{:S(2)}) %collective-permute-start.63) | collective-permute-done | bytes 16416 | tf_op jit(solution)/shard_map/ppermute | solution.py:213
  546.8 3.8 collective-permute-done.68
  555.4 4.3 input_grad.1
  (306 shorter events, 156.4 us)
Async XLA Ops:
  20.2 36.8 %collective-permute-start.3 = (bf16[256,2048]{1,0:T(8,128)(2,1)S(1)}, bf16[256,2048]{1,0:T(8,128)(2,1)S(1)}, u32[]{:S(2)}, u32[]{:S(2)}) collective-permute-start(bf16[256,2048]{1,0:T(8,128)(2,1)S(1)} %copy-done.2), channel_id=1, source_target_pairs={{0,8},{8,0},{1,9},{9,1},{2,10},{10,2},{3,11},{11,3},{4,12},{12,4},... | collective-permute-start | bytes 3145736 | tf_op jit(solution)/shard_map/ppermute | solution.py:213
  22.0 35.0 %collective-permute-start.4 = (bf16[256,2048]{1,0:T(8,128)(2,1)S(1)}, bf16[256,2048]{1,0:T(8,128)(2,1)S(1)}, u32[]{:S(2)}, u32[]{:S(2)}) collective-permute-start(bf16[256,2048]{1,0:T(8,128)(2,1)S(1)} %copy-done.2), channel_id=1, source_target_pairs={{0,2},{1,3},{2,0},{3,1},{4,6},{5,7},{6,4},{7,5},{8,10},{9,11},{10,... | collective-permute-start | bytes 3145736 | tf_op jit(solution)/shard_map/ppermute | solution.py:213
  23.5 32.7 %collective-permute-start.6 = (bf16[512,512]{1,0:T(8,128)(2,1)S(1)}, bf16[512,512]{1,0:T(8,128)(2,1)S(1)}, u32[]{:S(2)}, u32[]{:S(2)}) collective-permute-start(bf16[512,512]{1,0:T(8,128)(2,1)S(1)} %get-tuple-element.273.refs_0_), channel_id=1, source_target_pairs={{0,16},{16,0},{1,17},{17,1},{2,18},{18,2},{3,19},{19,3},{4,20},{20... | collective-permute-start | bytes 1572872 | tf_op jit(solution)/shard_map/ppermute | solution.py:213
  26.1 30.1 %collective-permute-start.7 = (bf16[512,512]{1,0:T(8,128)(2,1)S(1)}, bf16[512,512]{1,0:T(8,128)(2,1)S(1)}, u32[]{:S(2)}, u32[]{:S(2)}) collective-permute-start(bf16[512,512]{1,0:T(8,128)(2,1)S(1)} %get-tuple-element.273.refs_0_), channel_id=1, source_target_pairs={{0,4},{4,0},{1,5},{5,1},{2,6},{6,2},{3,7},{7,3},{8,12},{12,8},{9,1... | collective-permute-start | bytes 1572872 | tf_op jit(solution)/shard_map/ppermute | solution.py:213
  61.8 32.9 %collective-permute-start.8 = (bf16[256,2048]{1,0:T(8,128)(2,1)S(1)}, bf16[256,2048]{1,0:T(8,128)(2,1)S(1)}, u32[]{:S(2)}, u32[]{:S(2)}) collective-permute-start(bf16[256,2048]{1,0:T(8,128)(2,1)S(1)} %collective-permute-done.3.refs_1_.refs_7_), channel_id=1, source_target_pairs={{0,2},{1,3},{2,0},{3,1},{4,6},{5,7},{6,4},{7,5},{8,10},{9,11},{10,... | collective-permute-start | bytes 3145736 | tf_op jit(solution)/shard_map/ppermute | solution.py:213
  63.3 31.4 %collective-permute-start.10 = (bf16[256,2048]{1,0:T(8,128)(2,1)S(1)}, bf16[256,2048]{1,0:T(8,128)(2,1)S(1)}, u32[]{:S(2)}, u32[]{:S(2)}) collective-permute-start(bf16[256,2048]{1,0:T(8,128)(2,1)S(1)} %collective-permute-done.3.refs_1_.refs_7_), channel_id=1, source_target_pairs={{0,1},{1,0},{2,3},{3,2},{4,5},{5,4},{6,7},{7,6},{8,9},{9,8},{10,11... | collective-permute-start | bytes 3145736 | tf_op jit(solution)/shard_map/ppermute | solution.py:213
  63.3 31.4 %collective-permute-start.11 = (bf16[256,2048]{1,0:T(8,128)(2,1)S(1)}, bf16[256,2048]{1,0:T(8,128)(2,1)S(1)}, u32[]{:S(2)}, u32[]{:S(2)}) collective-permute-start(bf16[256,2048]{1,0:T(8,128)(2,1)S(1)} %collective-permute-done.4.refs_2_.refs_8_), channel_id=1, source_target_pairs={{0,1},{1,0},{2,3},{3,2},{4,5},{5,4},{6,7},{7,6},{8,9},{9,8},{10,11... | collective-permute-start | bytes 3145736 | tf_op jit(solution)/shard_map/ppermute | solution.py:213
  97.4 36.5 %collective-permute-start.16 = (bf16[256,2048]{1,0:T(8,128)(2,1)S(1)}, bf16[256,2048]{1,0:T(8,128)(2,1)}, u32[]{:S(2)}, u32[]{:S(2)}) collective-permute-start(bf16[256,2048]{1,0:T(8,128)(2,1)S(1)} %copy-done.5), channel_id=1, source_target_pairs={{0,8},{8,0},{1,9},{9,1},{2,10},{10,2},{3,11},{11,3},{4,12},{12,4},... | collective-permute-start | bytes 3145736 | tf_op jit(solution)/shard_map/ppermute | solution.py:213
  97.5 36.5 %collective-permute-start.17 = (bf16[256,2048]{1,0:T(8,128)(2,1)S(1)}, bf16[256,2048]{1,0:T(8,128)(2,1)}, u32[]{:S(2)}, u32[]{:S(2)}) collective-permute-start(bf16[256,2048]{1,0:T(8,128)(2,1)S(1)} %copy-done.5), channel_id=1, source_target_pairs={{0,2},{1,3},{2,0},{3,1},{4,6},{5,7},{6,4},{7,5},{8,10},{9,11},{10,... | collective-permute-start | bytes 3145736 | tf_op jit(solution)/shard_map/ppermute | solution.py:213
  100.6 31.2 %collective-permute-start.19 = (bf16[512,512]{1,0:T(8,128)(2,1)}, bf16[512,512]{1,0:T(8,128)(2,1)}, u32[]{:S(2)}, u32[]{:S(2)}) collective-permute-start(bf16[512,512]{1,0:T(8,128)(2,1)} %get-tuple-element.306.refs_0_), channel_id=1, source_target_pairs={{0,16},{16,0},{1,17},{17,1},{2,18},{18,2},{3,19},{19,3},{4,20},{20... | collective-permute-start | bytes 1572872 | tf_op jit(solution)/shard_map/ppermute | solution.py:213
  103.9 27.9 %collective-permute-start.20 = (bf16[512,512]{1,0:T(8,128)(2,1)}, bf16[512,512]{1,0:T(8,128)(2,1)}, u32[]{:S(2)}, u32[]{:S(2)}) collective-permute-start(bf16[512,512]{1,0:T(8,128)(2,1)} %get-tuple-element.306.refs_0_), channel_id=1, source_target_pairs={{0,4},{4,0},{1,5},{5,1},{2,6},{6,2},{3,7},{7,3},{8,12},{12,8},{9,1... | collective-permute-start | bytes 1572872 | tf_op jit(solution)/shard_map/ppermute | solution.py:213
  137.0 36.1 %collective-permute-start.21 = (bf16[256,2048]{1,0:T(8,128)(2,1)}, bf16[256,2048]{1,0:T(8,128)(2,1)}, u32[]{:S(2)}, u32[]{:S(2)}) collective-permute-start(bf16[256,2048]{1,0:T(8,128)(2,1)} %collective-permute-done.16.refs_1_), channel_id=1, source_target_pairs={{0,2},{1,3},{2,0},{3,1},{4,6},{5,7},{6,4},{7,5},{8,10},{9,11},{10,... | collective-permute-start | bytes 3145736 | tf_op jit(solution)/shard_map/ppermute | solution.py:213
  138.8 34.3 %collective-permute-start.23 = (bf16[256,2048]{1,0:T(8,128)(2,1)}, bf16[256,2048]{1,0:T(8,128)(2,1)}, u32[]{:S(2)}, u32[]{:S(2)}) collective-permute-start(bf16[256,2048]{1,0:T(8,128)(2,1)} %collective-permute-done.16.refs_1_), channel_id=1, source_target_pairs={{0,1},{1,0},{2,3},{3,2},{4,5},{5,4},{6,7},{7,6},{8,9},{9,8},{10,11... | collective-permute-start | bytes 3145736 | tf_op jit(solution)/shard_map/ppermute | solution.py:213
  138.8 34.3 %collective-permute-start.24 = (bf16[256,2048]{1,0:T(8,128)(2,1)}, bf16[256,2048]{1,0:T(8,128)(2,1)}, u32[]{:S(2)}, u32[]{:S(2)}) collective-permute-start(bf16[256,2048]{1,0:T(8,128)(2,1)} %collective-permute-done.17.refs_2_), channel_id=1, source_target_pairs={{0,1},{1,0},{2,3},{3,2},{4,5},{5,4},{6,7},{7,6},{8,9},{9,8},{10,11... | collective-permute-start | bytes 3145736 | tf_op jit(solution)/shard_map/ppermute | solution.py:213
  173.2 31.9 %collective-permute-start.29 = (bf16[512,512]{1,0:T(8,128)(2,1)}, bf16[512,512]{1,0:T(8,128)(2,1)S(1)}, u32[]{:S(2)}, u32[]{:S(2)}) collective-permute-start(bf16[512,512]{1,0:T(8,128)(2,1)} %collective-permute-done.26.refs_2_), channel_id=1, source_target_pairs={{0,4},{4,0},{1,5},{5,1},{2,6},{6,2},{3,7},{7,3},{8,12},{12,8},{9,1... | collective-permute-start | bytes 1572872 | tf_op jit(solution)/shard_map/ppermute | solution.py:213
  176.1 29.0 %collective-permute-start.30 = (bf16[512,512]{1,0:T(8,128)(2,1)S(1)}, bf16[512,512]{1,0:T(8,128)(2,1)}, u32[]{:S(2)}, u32[]{:S(2)}) collective-permute-start(bf16[512,512]{1,0:T(8,128)(2,1)S(1)} %get-tuple-element.337.refs_0_), channel_id=1, source_target_pairs={{0,16},{16,0},{1,17},{17,1},{2,18},{18,2},{3,19},{19,3},{4,20},{20... | collective-permute-start | bytes 1572872 | tf_op jit(solution)/shard_map/ppermute | solution.py:213
  232.4 35.6 %collective-permute-start.36 = (bf16[1024,512]{1,0:T(8,128)(2,1)}, bf16[1024,512]{1,0:T(8,128)(2,1)}, u32[]{:S(2)}, u32[]{:S(2)}) collective-permute-start(bf16[1024,512]{1,0:T(8,128)(2,1)} %get-tuple-element.358), channel_id=1, source_target_pairs={{0,4},{4,0},{1,5},{5,1},{2,6},{6,2},{3,7},{7,3},{8,12},{12,8},{9,1... | collective-permute-start | bytes 3145736 | tf_op jit(solution)/shard_map/ppermute | solution.py:213
  233.6 34.3 %collective-permute-start.35 = (bf16[512,512]{1,0:T(8,128)(2,1)}, bf16[512,512]{1,0:T(8,128)(2,1)}, u32[]{:S(2)}, u32[]{:S(2)}) collective-permute-start(bf16[512,512]{1,0:T(8,128)(2,1)} %collective-permute-done.33.refs_2_), channel_id=1, source_target_pairs={{0,4},{4,0},{1,5},{5,1},{2,6},{6,2},{3,7},{7,3},{8,12},{12,8},{9,1... | collective-permute-start | bytes 1572872 | tf_op jit(solution)/shard_map/ppermute | solution.py:213
  357.4 43.7 %collective-permute-start.46 = (bf16[512,1024]{1,0:T(8,128)(2,1)}, bf16[512,1024]{1,0:T(8,128)(2,1)S(1)}, u32[]{:S(2)}, u32[]{:S(2)}) collective-permute-start(bf16[512,1024]{1,0:T(8,128)(2,1)} %get-tuple-element.405), channel_id=1, source_target_pairs={{0,2},{1,3},{2,0},{3,1},{4,6},{5,7},{6,4},{7,5},{8,10},{9,11},{10,... | collective-permute-start | bytes 3145736 | tf_op jit(solution)/shard_map/ppermute | solution.py:213
  359.2 41.9 %collective-permute-start.47 = (bf16[512,1024]{1,0:T(8,128)(2,1)}, bf16[512,1024]{1,0:T(8,128)(2,1)S(1)}, u32[]{:S(2)}, u32[]{:S(2)}) collective-permute-start(bf16[512,1024]{1,0:T(8,128)(2,1)} %get-tuple-element.407), channel_id=1, source_target_pairs={{0,8},{8,0},{1,9},{9,1},{2,10},{10,2},{3,11},{11,3},{4,12},{12,4},... | collective-permute-start | bytes 3145736 | tf_op jit(solution)/shard_map/ppermute | solution.py:213
  361.0 40.1 %collective-permute-start.49 = (bf16[512,512]{1,0:T(8,128)(2,1)S(1)}, bf16[512,512]{1,0:T(8,128)(2,1)S(1)}, u32[]{:S(2)}, u32[]{:S(2)}) collective-permute-start(bf16[512,512]{1,0:T(8,128)(2,1)S(1)} %get-tuple-element.412), channel_id=1, source_target_pairs={{0,16},{16,0},{1,17},{17,1},{2,18},{18,2},{3,19},{19,3},{4,20},{20... | collective-permute-start | bytes 1572872 | tf_op jit(solution)/shard_map/ppermute | solution.py:213
  364.3 36.7 %collective-permute-start.48 = (bf16[256,512]{1,0:T(8,128)(2,1)S(1)}, bf16[256,512]{1,0:T(8,128)(2,1)S(1)}, u32[]{:S(2)}, u32[]{:S(2)}) collective-permute-start(bf16[256,512]{1,0:T(8,128)(2,1)S(1)} %get-tuple-element.410), channel_id=1, source_target_pairs={{0,8},{8,0},{1,9},{9,1},{2,10},{10,2},{3,11},{11,3},{4,12},{12,4},... | collective-permute-start | bytes 786440 | tf_op jit(solution)/shard_map/ppermute | solution.py:213
  401.1 39.3 %collective-permute-start.52 = (bf16[1024,512]{1,0:T(8,128)(2,1)S(1)}, bf16[1024,512]{1,0:T(8,128)(2,1)S(1)}, u32[]{:S(2)}, u32[]{:S(2)}) collective-permute-start(bf16[1024,512]{1,0:T(8,128)(2,1)S(1)} %get-tuple-element.424), channel_id=1, source_target_pairs={{0,4},{4,0},{1,5},{5,1},{2,6},{6,2},{3,7},{7,3},{8,12},{12,8},{9,1... | collective-permute-start | bytes 3145736 | tf_op jit(solution)/shard_map/ppermute | solution.py:213
  405.5 34.8 %collective-permute-start.50 = (bf16[256,1024]{1,0:T(8,128)(2,1)S(1)}, bf16[256,1024]{1,0:T(8,128)(2,1)S(1)}, u32[]{:S(2)}, u32[]{:S(2)}) collective-permute-start(bf16[256,1024]{1,0:T(8,128)(2,1)S(1)} %get-tuple-element.421), channel_id=1, source_target_pairs={{0,8},{8,0},{1,9},{9,1},{2,10},{10,2},{3,11},{11,3},{4,12},{12,4},... | collective-permute-start | bytes 1572872 | tf_op jit(solution)/shard_map/ppermute | solution.py:213
  405.8 34.5 %collective-permute-start.51 = (bf16[256,1024]{1,0:T(8,128)(2,1)}, bf16[256,1024]{1,0:T(8,128)(2,1)S(1)}, u32[]{:S(2)}, u32[]{:S(2)}) collective-permute-start(bf16[256,1024]{1,0:T(8,128)(2,1)} %get-tuple-element.423), channel_id=1, source_target_pairs={{0,2},{1,3},{2,0},{3,1},{4,6},{5,7},{6,4},{7,5},{8,10},{9,11},{10,... | collective-permute-start | bytes 1572872 | tf_op jit(solution)/shard_map/ppermute | solution.py:213
  406.2 34.1 %collective-permute-start.53 = (bf16[256,512]{1,0:T(8,128)(2,1)S(1)}, bf16[256,512]{1,0:T(8,128)(2,1)S(1)}, u32[]{:S(2)}, u32[]{:S(2)}) collective-permute-start(bf16[256,512]{1,0:T(8,128)(2,1)S(1)} %get-tuple-element.427), channel_id=1, source_target_pairs={{0,8},{8,0},{1,9},{9,1},{2,10},{10,2},{3,11},{11,3},{4,12},{12,4},... | collective-permute-start | bytes 786440 | tf_op jit(solution)/shard_map/ppermute | solution.py:213
  440.4 29.4 %collective-permute-start.54 = (bf16[1024,2048]{1,0:T(8,128)(2,1)}, bf16[1024,2048]{1,0:T(8,128)(2,1)}, u32[]{:S(2)}, u32[]{:S(2)}) collective-permute-start(bf16[1024,2048]{1,0:T(8,128)(2,1)} %get-tuple-element.431), channel_id=1, source_target_pairs={{0,1},{1,0},{2,3},{3,2},{4,5},{5,4},{6,7},{7,6},{8,9},{9,8},{10,11... | collective-permute-start | bytes 12582920 | tf_op jit(solution)/shard_map/ppermute | solution.py:213
  440.5 29.3 %collective-permute-start.57 = (bf16[1024,512]{1,0:T(8,128)(2,1)S(1)}, bf16[1024,512]{1,0:T(8,128)(2,1)S(1)}, u32[]{:S(2)}, u32[]{:S(2)}) collective-permute-start(bf16[1024,512]{1,0:T(8,128)(2,1)S(1)} %copy-done.59), channel_id=1, source_target_pairs={{0,4},{4,0},{1,5},{5,1},{2,6},{6,2},{3,7},{7,3},{8,12},{12,8},{9,1... | collective-permute-start | bytes 3145736 | tf_op jit(solution)/shard_map/ppermute | solution.py:213
  478.0 43.6 %collective-permute-start.59 = (bf16[512,1024]{1,0:T(8,128)(2,1)}, bf16[512,1024]{1,0:T(8,128)(2,1)S(1)}, u32[]{:S(2)}, u32[]{:S(2)}) collective-permute-start(bf16[512,1024]{1,0:T(8,128)(2,1)} %get-tuple-element.455), channel_id=1, source_target_pairs={{0,2},{1,3},{2,0},{3,1},{4,6},{5,7},{6,4},{7,5},{8,10},{9,11},{10,... | collective-permute-start | bytes 3145736 | tf_op jit(solution)/shard_map/ppermute | solution.py:213
  479.7 41.9 %collective-permute-start.60 = (bf16[512,1024]{1,0:T(8,128)(2,1)}, bf16[512,1024]{1,0:T(8,128)(2,1)S(1)}, u32[]{:S(2)}, u32[]{:S(2)}) collective-permute-start(bf16[512,1024]{1,0:T(8,128)(2,1)} %get-tuple-element.457), channel_id=1, source_target_pairs={{0,8},{8,0},{1,9},{9,1},{2,10},{10,2},{3,11},{11,3},{4,12},{12,4},... | collective-permute-start | bytes 3145736 | tf_op jit(solution)/shard_map/ppermute | solution.py:213
  481.5 40.1 %collective-permute-start.62 = (bf16[512,512]{1,0:T(8,128)(2,1)S(1)}, bf16[512,512]{1,0:T(8,128)(2,1)S(1)}, u32[]{:S(2)}, u32[]{:S(2)}) collective-permute-start(bf16[512,512]{1,0:T(8,128)(2,1)S(1)} %get-tuple-element.462), channel_id=1, source_target_pairs={{0,16},{16,0},{1,17},{17,1},{2,18},{18,2},{3,19},{19,3},{4,20},{20... | collective-permute-start | bytes 1572872 | tf_op jit(solution)/shard_map/ppermute | solution.py:213
  484.6 37.0 %collective-permute-start.61 = (bf16[256,512]{1,0:T(8,128)(2,1)S(1)}, bf16[256,512]{1,0:T(8,128)(2,1)S(1)}, u32[]{:S(2)}, u32[]{:S(2)}) collective-permute-start(bf16[256,512]{1,0:T(8,128)(2,1)S(1)} %get-tuple-element.460), channel_id=1, source_target_pairs={{0,8},{8,0},{1,9},{9,1},{2,10},{10,2},{3,11},{11,3},{4,12},{12,4},... | collective-permute-start | bytes 786440 | tf_op jit(solution)/shard_map/ppermute | solution.py:213
  (99 other events, 1762.0 us)

commit v3 on v2

--- a/solution.py
+++ b/solution.py
@@ -191,7 +191,7 @@
             jax.ShapeDtypeStruct(view(width), LOW),
             jax.ShapeDtypeStruct((seqs, 1, width), FULL),
         ],
-        compiler_params=pltpu.CompilerParams(vmem_limit_bytes=40 << 20),
+        compiler_params=pltpu.CompilerParams(vmem_limit_bytes=58 << 20),
         cost_estimate=pl.CostEstimate(
             flops=seqs * LEN * QB * (BACK + 1) * pair // 8,
             transcendentals=0,
@@ -213,12 +213,13 @@
     return lax.ppermute(value, axis, [(i, i ^ bit) for i in range(lax.axis_size(axis))])
 
 
-def sum_over(value, axis):
-    bit = 1
-    while bit < lax.axis_size(axis):
-        value = value + swap(value, axis, bit)
-        bit *= 2
-    return value
+def swap_both(value, axis, bit, other_axis, other_bit):
+    inner = lax.axis_size(other_axis)
+    pairs = [
+        (i, ((i // inner) ^ bit) * inner + ((i % inner) ^ other_bit))
+        for i in range(lax.axis_size(axis) * inner)
+    ]
+    return lax.ppermute(value, (axis, other_axis), pairs)
 
 
 def normalize_rows(token_rows):
@@ -252,7 +253,7 @@
             out_specs=out_specs,
         ),
         out_shape=out_shape,
-        compiler_params=pltpu.CompilerParams(vmem_limit_bytes=52 << 20),
+        compiler_params=pltpu.CompilerParams(vmem_limit_bytes=(52 if steps > 1 else 32) << 20),
         cost_estimate=pl.CostEstimate(flops=1 << 24, transcendentals=0, bytes_accessed=1 << 18),
         name=name,
     )(*scalars, *operands)
@@ -631,63 +632,42 @@
     return total
 
 
-def far_rows_first(i):
-    return jnp.where(i < 4, i + 4, i - 4)
-
-
-def to_given_or_kept(value, given_ref, kept_ref):
-    @pl.when(pl.program_id(0) < 4)
-    def _():
-        given_ref[...] = value
-
-    @pl.when(pl.program_id(0) >= 4)
-    def _():
-        kept_ref[...] = value
-
-
 def branch_kernel(counts, terms, *refs):
     lefts, rights = refs[: counts[0]], refs[counts[0] : sum(counts)]
-    total = sum_of_products(lefts, rights, terms)
-    to_given_or_kept(total.astype(LOW), *refs[sum(counts) :])
+    refs[-1][...] = sum_of_products(lefts, rights, terms).astype(LOW)
 
 
 def token_grad_kernel(counts, terms, *refs):
     lefts, rights = refs[: counts[0]], refs[counts[0] : sum(counts)]
-    pieces, (given_ref, kept_ref, sums_ref) = refs[sum(counts) : -3], refs[-3:]
+    pieces, (out_ref, sums_ref) = refs[sum(counts) : -2], refs[-2:]
 
     @pl.when(pl.program_id(0) == 0)
     def _():
         sums_ref[...] = jnp.zeros_like(sums_ref)
 
     grad = sum_of_products(lefts, rights, terms)
-    to_given_or_kept(grad.astype(LOW), given_ref, kept_ref)
+    out_ref[...] = grad.astype(LOW)
     sums_ref[1:2, :] += jnp.sum(grad, axis=0, keepdims=True)
 
     def use(piece):
         x_hat, _ = normalize_rows(piece[...])
         sums_ref[0:1, :] += jnp.sum(grad * x_hat, axis=0, keepdims=True)
 
-    from_piece([*pieces[4:], *pieces[:4]], use)
-
-
-def over_tokens(kernel, name, lefts, rights, terms, pieces=()):
+    from_piece(pieces, use)
+
+
+def half_rows(kernel, name, far, lefts, rights, terms, pieces=()):
     rows, width = lefts[0].shape[0], rights[0].shape[0]
     step = rows // 8
+    pieces = pieces[4 * far : 4 * far + 4]
     sums = [like(2, width, dtype=FULL)] if pieces else []
     return run_kernel(
         functools.partial(kernel, (len(lefts), len(rights)), terms),
-        8,
-        [
-            pl.BlockSpec((step, left.shape[1]), lambda i, *_: (far_rows_first(i), 0))
-            for left in lefts
-        ]
+        4,
+        [pl.BlockSpec((step, left.shape[1]), lambda i, *_: (i + 4 * far, 0)) for left in lefts]
         + whole(*rights, *pieces),
-        [
-            pl.BlockSpec((step, width), lambda i, *_: (jnp.minimum(i, 3), 0)),
-            pl.BlockSpec((step, width), lambda i, *_: (jnp.maximum(i - 4, 0), 0)),
-            *whole(*sums),
-        ],
-        [like(rows // 2, width)] * 2 + sums,
+        [row_blocks(width, step), *whole(*sums)],
+        [like(4 * step, width)] + sums,
         name,
         *lefts,
         *rights,
@@ -695,31 +675,43 @@
     )
 
 
-def link_kernel(kept_ref, got_ref, left_ref, left_given_ref, right_ref, right_given_ref):
-    quarter, columns = left_ref.shape
-    part = quarter // 2
-    y, low = pl.program_id(0) // 2, pl.program_id(0) % 2
-    held = (kept_ref[...].astype(FULL) + got_ref[...].astype(FULL)).astype(LOW)
+def to_links(held, left_ref, left_given_ref, right_ref, right_given_ref):
+    columns = left_ref.shape[1]
 
     for at in range(4):
 
         @pl.when(pl.program_id(0) == at)
         def _(y=at // 2, low=at % 2):
             left = left_given_ref if y else left_ref
-            left[low * part : (low + 1) * part, :] = held[:, :columns]
+            left[...] = held[:, :columns]
             right = right_given_ref if low else right_ref
-            right[y * part : (y + 1) * part, :] = held[:, columns:]
+            right[...] = held[:, columns:]
+
+
+def links(step, width):
+    columns = width * 5 // 8
+    specs = [
+        pl.BlockSpec((step, columns), lambda i, *_: (jnp.minimum(i, 1), 0)),
+        pl.BlockSpec((step, columns), lambda i, *_: (jnp.maximum(i - 2, 0), 0)),
+        pl.BlockSpec((step, width - columns), lambda i, *_: (i // 2, 0)),
+        pl.BlockSpec((step, width - columns), lambda i, *_: (i // 2, 0)),
+    ]
+    return specs, [like(2 * step, columns)] * 2 + [like(2 * step, width - columns)] * 2
+
+
+def link_kernel(kept_ref, got_ref, *outs):
+    to_links((kept_ref[...].astype(FULL) + got_ref[...].astype(FULL)).astype(LOW), *outs)
 
 
 def link_stage(kept, got):
     rows, width = kept.shape
-    out = like(rows // 2, width // 2)
+    specs, outs = links(rows // 4, width)
     return run_kernel(
         link_kernel,
         4,
         [row_blocks(width, rows // 4)] * 2,
-        whole(*[out] * 4),
-        [out] * 4,
+        specs,
+        outs,
         "link_stage",
         kept,
         got,
@@ -736,11 +728,8 @@
 
 
 def last_stage(*values):
-    rows, columns = values[0].shape
-    out = like(rows // 2, columns)
-    return run_kernel(
-        last_kernel, 1, whole(*values), whole(*[out] * 4), [out] * 4, "last_stage", *values
-    )
+    outs = [like(value.shape[0] // 2, value.shape[1]) for value in values]
+    return run_kernel(last_kernel, 1, whole(*values), whole(*outs), outs, "last_stage", *values)
 
 
 def joined(refs):
@@ -854,7 +843,9 @@
                 blocks = self.given.reshape(-1, 2, 2, weight_rows, columns)
                 ordered = blocks.transpose(0, 2, 1, 3, 4).reshape(rows, columns)
                 self.moving = [
-                    lax.psum_scatter(ordered, ("zh", "x"), scatter_dimension=0, tiled=True)
+                    lax.psum_scatter(
+                        ordered.astype(FULL), ("zh", "x"), scatter_dimension=0, tiled=True
+                    )
                 ]
 
         def second(self):
@@ -916,20 +907,18 @@
     fc1_a.forward()
     fc1_b.start()
     tokens_both, got = to_y(tokens_low), to_low(heads_given)
-    tokens_low_core, tokens_y_core = to_core(tokens_low), to_core(tokens_y)
     all_segments = jnp.concatenate([segments, segments_low])
     starts = jnp.sum(
         (all_segments[:, None, :] < all_segments[:, :, None]).astype(jnp.int32), axis=2
     )
-    tokens_both, got, tokens_low_core, tokens_y_core, starts, fc2_given, out_grad = segment(
-        [tokens_both, got, tokens_low_core, tokens_y_core, starts, fc2_given, out_grad],
-        fc1_a,
-        fc1_b,
-    )
+    tokens_both, got, starts, fc2_given, out_grad, tokens_low, tokens_y = segment(
+        [tokens_both, got, starts, fc2_given, out_grad, tokens_low, tokens_y], fc1_a, fc1_b
+    )
+    tokens_low_core, tokens_y_core = to_core(tokens_low), to_core(tokens_y)
     tokens_both_core = to_core(tokens_both)
     shards = shards_of(low_at, heads_mine, got)
-    tokens_both_core, fc2_given, out_grad, *shards = sync(
-        tokens_both_core, fc2_given, out_grad, *shards
+    tokens_low_core, tokens_y_core, tokens_both_core, fc2_given, out_grad, *shards = sync(
+        tokens_low_core, tokens_y_core, tokens_both_core, fc2_given, out_grad, *shards
     )
     heads_a, heads_b = (Gather(shard) for shard in shards)
     fc1_b.forward()
@@ -953,15 +942,17 @@
     heads_a.forward()
     heads_b.start()
     grad_both, got = to_y(grad_low), to_low(fc2_given)
-    grad_low_core, grad_y_core = to_core(grad_low), to_core(grad_y)
     fc1_full.append(fc1_b.whole())
     bias = lax.dynamic_slice_in_dim(fc1_bias, low_at * hidden, hidden, 0)[None]
     activated, slope = hidden_forward(all_normed, fc1_full, bias)
-    activated, slope, grad_both, got, grad_low_core, grad_y_core = segment(
-        [activated, slope, grad_both, got, grad_low_core, grad_y_core], heads_a, heads_b
-    )
+    activated, slope, grad_both, got, grad_low, grad_y = segment(
+        [activated, slope, grad_both, got, grad_low, grad_y], heads_a, heads_b
+    )
+    grad_low_core, grad_y_core = to_core(grad_low), to_core(grad_y)
     grad_both_core = to_core(grad_both)
-    grad_both_core, *shards = sync(grad_both_core, *shards_of(low_at, fc2_mine, got))
+    grad_low_core, grad_y_core, grad_both_core, *shards = sync(
+        grad_low_core, grad_y_core, grad_both_core, *shards_of(low_at, fc2_mine, got)
+    )
     fc2_a, fc2_b = (Gather(shard) for shard in shards)
     heads_b.forward()
     fc2_a.start()
@@ -1001,19 +992,11 @@
     d_fc2_b.start()
     d_fc2_a.second()
     fc2_full.append(fc2_b.whole())
-    partials = sums_of((all_normed, qkv_grad), (all_grad, attended))
-    fc2_full[1], *partials = segment([fc2_full[1], *partials], d_fc2_a, d_fc2_b)
-    d_heads_a, d_heads_b = as_sums(partials)
-    d_heads_a.start()
-    d_fc2_b.second()
-    d_fc2_a.third()
     columns = heads_full[0].shape[1]
     first, second = slice(0, columns), slice(columns, 2 * columns)
     qkv_end = 3 * half - columns
     everything = slice(None)
-    given, branch_kept = over_tokens(
-        branch_kernel,
-        "branch",
+    branch_products = (
         [attended, activated],
         [heads_full[1], *fc2_full],
         [
@@ -1022,33 +1005,40 @@
             (1, second, 2, everything),
         ],
     )
-    given, branch_kept, d_heads_b.given = segment(
-        [given, branch_kept, d_heads_b.given], d_heads_a, d_fc2_a, d_fc2_b
+    far, *partials = segment(
+        [
+            *half_rows(branch_kernel, "branch", 1, *branch_products),
+            *sums_of((all_normed, qkv_grad), (all_grad, attended)),
+        ],
+        d_fc2_a,
+        d_fc2_b,
+    )
+    d_heads_a, d_heads_b = as_sums(partials)
+    d_heads_a.start()
+    d_fc2_b.second()
+    d_fc2_a.third()
+    branch_got = to_core(far)
+    (branch_kept,) = half_rows(branch_kernel, "branch", 0, *branch_products)
+    pre_grad, pre_sums = hidden_back(all_grad, fc2_full, slope)
+    branch_got, branch_kept, pre_grad, pre_sums, d_heads_b.given = segment(
+        [branch_got, branch_kept, pre_grad, pre_sums, d_heads_b.given],
+        d_heads_a,
+        d_fc2_a,
+        d_fc2_b,
     )
     d_heads_b.start()
     d_heads_a.second()
-    d_fc2_b.third()
-    branch_got = to_core(given)
-    pre_grad, pre_sums = hidden_back(all_grad, fc2_full, slope)
-    pre_grad, pre_sums, branch_got = segment(
-        [pre_grad, pre_sums, branch_got], d_heads_a, d_heads_b, d_fc2_b
-    )
-    d_heads_b.second()
-    d_heads_a.third()
     left, left_given, right, right_given = link_stage(branch_kept, branch_got)
     branch_state = [left, to_y(left_given), right, to_low(right_given)]
-    partials = sums_of((all_normed, pre_grad))
-    *partials, left, left_got, right, right_got = segment(
-        [*partials, *branch_state], d_heads_a, d_heads_b
-    )
-    d_fc1_a, d_fc1_b = as_sums(partials)
+    *branch_state, given_a, given_b, kept_a, kept_b = segment(
+        [*branch_state, *sums_of((all_normed, pre_grad))], d_heads_a, d_heads_b, d_fc2_b
+    )
+    d_fc1_a, d_fc1_b = as_sums([given_a, given_b, kept_a, kept_b])
     d_fc1_a.start()
-    d_heads_b.third()
-    left, left_given, right, right_given = last_stage(left, left_got, right, right_got)
+    d_heads_b.second()
+    left, left_given, right, right_given = last_stage(*branch_state)
     branch_state = [left, to_low(left_given), right, to_y(right_given)]
-    given, kept, norm_sums = over_tokens(
-        token_grad_kernel,
-        "token_grad",
+    grad_products = (
         [qkv_grad, pre_grad],
         [*heads_full, *fc1_full],
         [
@@ -1059,44 +1049,67 @@
         ],
         token_pieces,
     )
-    given, kept, norm_sums, d_fc1_b.given, *branch_state = segment(
-        [given, kept, norm_sums, d_fc1_b.given, *branch_state], d_fc1_a, d_heads_b
+    far, far_sums, d_fc1_b.given, *branch_state = segment(
+        [
+            *half_rows(token_grad_kernel, "token_grad", 1, *grad_products),
+            d_fc1_b.given,
+            *branch_state,
+        ],
+        d_fc1_a,
+        d_heads_a,
+        d_heads_b,
+        d_fc2_b,
     )
     d_fc1_b.start()
     d_fc1_a.second()
-    got, sums = to_core(given), norm_sums.reshape(2 * D)
-    sums_got = to_core(sums)
+    d_heads_a.third()
+    d_fc2_b.third()
+    got = to_core(far)
+    kept, near_sums = half_rows(token_grad_kernel, "token_grad", 0, *grad_products)
     output = row_result(
         output_kernel, "output", *branch_state, tokens, dense_bias[None], fc2_bias[None]
     )
-    fc2_weight_grad = final_grad(low_at, *d_fc2_a.halves(), *d_fc2_b.halves())
-    q, k, v, dense_weight_grad = final_heads(low_at, *d_heads_a.halves(), *d_heads_b.halves())
-    got, sums, sums_got, output, fc2_weight_grad, q, k, v, dense_weight_grad = segment(
-        [got, sums, sums_got, output, fc2_weight_grad, q, k, v, dense_weight_grad],
-        d_fc1_a,
-        d_fc1_b,
-    )
+    got, kept, near_sums, output = segment(
+        [got, kept, near_sums, output], d_fc1_a, d_fc1_b, d_heads_a, d_heads_b, d_fc2_b
+    )
+    d_fc1_b.second()
     left, left_given, right, right_given = link_stage(kept, got)
     grad_state = [left, to_y(left_given), right, to_low(right_given)]
-    d_fc1_b.second()
-    d_fc1_a.third()
-    sums = sums + sums_got
-    sums_got = to_y(sums)
-    sums, sums_got, *grad_state = segment([sums, sums_got, *grad_state], d_fc1_a, d_fc1_b)
+    sums = (near_sums + far_sums).reshape(2 * D)
+    sums_got = to_core(sums)
+    fc2_weight_grad = final_grad(low_at, *d_fc2_a.halves(), *d_fc2_b.halves())
+    here = jnp.concatenate([jnp.sum(qkv_sums, axis=(0, 1)), pre_sums[0]])
+    fc2_weight_grad, here, sums, sums_got, *grad_state = segment(
+        [fc2_weight_grad, here, sums, sums_got, *grad_state], d_fc1_a, d_fc1_b, d_heads_b
+    )
     left, left_given, right, right_given = last_stage(*grad_state)
     grad_state = [left, to_low(left_given), right, to_y(right_given)]
+    d_fc1_a.third()
     d_fc1_b.third()
-    sums = sums + sums_got
-    sums_got = to_low(sums)
-    sums, sums_got, *grad_state = segment([sums, sums_got, *grad_state], d_fc1_b)
-    here = jnp.concatenate([jnp.sum(qkv_sums, axis=(0, 1)), pre_sums[0]])
-    sums = jnp.concatenate([sums + sums_got, grad_sums[0], here])
+    d_heads_b.third()
+    sums, *grad_state = segment(
+        [sums + sums_got, *grad_state], d_fc1_a, d_fc1_b, d_heads_b
+    )
+    sums_got = [to_low(sums), to_y(sums), swap_both(sums, "zl", 1, "t", 2)]
     bias_got = to_low(here)
-    sums = sum_over(sum_over(jnp.concatenate([sums, bias_got]), "zh"), "x")
     input_grad = row_result(
         input_grad_kernel, "input_grad", *grad_state, tokens, out_grad, ln_gain[None]
     )
     fc1_weight_grad = final_grad(low_at, *d_fc1_a.halves(), *d_fc1_b.halves())
+    input_grad, fc1_weight_grad, sums, bias_got, *sums_got = sync(
+        input_grad, fc1_weight_grad, sums, bias_got, *sums_got
+    )
+    sums = jnp.concatenate([sum(sums_got, sums), grad_sums[0], here, bias_got])
+    if pairwise:
+        sums_got = [to_high(sums), to_x(sums), swap_both(sums, "zh", 1, "x", 1)]
+    else:
+        sums_got = [lax.psum(sums, ("zh", "x")) - sums]
+    q, k, v, dense_weight_grad = final_heads(low_at, *d_heads_a.halves(), *d_heads_b.halves())
+    qkv_weight_grad = jnp.stack([q, k, v], axis=1)
+    qkv_weight_grad, dense_weight_grad, sums, *sums_got = sync(
+        qkv_weight_grad, dense_weight_grad, sums, *sums_got
+    )
+    sums = sum(sums_got, sums)
     both = sums[3 * D :].reshape(2, here.shape[0])
     both = jnp.where(low_at == 0, both, both[::-1])
     qkv_bias_grad = (
@@ -1107,7 +1120,7 @@
         input_grad,
         sums[:D],
         sums[D : 2 * D],
-        jnp.stack([q, k, v], axis=1),
+        qkv_weight_grad,
         qkv_bias_grad,
         dense_weight_grad,
         sums[2 * D : 3 * D],

time: 574 us -> 531 us (0.925)
  waiting for transfers between devices: 198 us -> 140 us
  local copies, waits for them, and re-layouts: 26.2 us -> 41.7 us
  Pallas kernels: 258 us -> 246 us
  starting transfers between devices: 75.3 us -> 85.5 us
    ppermute x70, waiting for transfers between devices: 198 us -> 140 us  [swap(): lax.ppermute(value, axis, [(i, i ^ bit) for i in range(lax.axis_size(axis...]
    unnamed x130 -> x235, local copies, waits for them, and re-layouts: 23.4 us -> 40 us
    pallas_call x43 -> x45, Pallas kernels: 236 us -> 222 us  [run_kernel(): pl.pallas_call(kernel, grid_spec=pltpu.PrefetchScalarGridSpec(num_scalar_...]
    ppermute x70, starting transfers between devices: 75.3 us -> 82.5 us  [swap(): lax.ppermute(value, axis, [(i, i ^ bit) for i in range(lax.axis_size(axis...]
  transfers between devices with their start and end apart: 70 -> 72, of which waited for: 22 -> 27; matrix products, arithmetic and copies ran while one was open for 1% -> 1% of each run, Pallas kernels for 42% -> 44%
where the time goes in v3:
time: 531 us; the launch traced here: 521 us
  Pallas kernels  246 us (46%)
  waiting for transfers between devices  140 us (26%)
  starting transfers between devices  85.5 us (16%)
  local copies, waits for them, and re-layouts  41.7 us (8%)
  other arithmetic  5.83 us (1%)
    pallas_call x45, Pallas kernels, run_kernel(): pl.pallas_call(kernel, grid_spec=pltpu.PrefetchScalarGridSpec(num_scalar_...  222 us
    ppermute x70, waiting for transfers between devices, swap(): lax.ppermute(value, axis, [(i, i ^ bit) for i in range(lax.axis_size(axis...  140 us
    ppermute x70, starting transfers between devices, swap(): lax.ppermute(value, axis, [(i, i ^ bit) for i in range(lax.axis_size(axis...  82.5 us
    unnamed x235, local copies, waits for them, and re-layouts  40 us
    pallas_call x1, Pallas kernels, attention(): pl.pallas_call(attention_kernel, grid_spec=pltpu.PrefetchScalarGridSpec(n...  23.9 us
  transfers between devices with their start and end apart: 72, of which 27 were waited for; matrix products, arithmetic and copies ran while one was open for 1% of the time, Pallas kernels for 44%

profile of v3, /device:TPU:0, one launch (start us, length us, event | category | flops | bytes accessed | tf_op | source)
XLA Modules:
  0.0 520.8 jit_solution(12523842603029236523)
XLA Ops:
  8.8 8.9 %collective-permute-done.got_ref = bf16[256,1024]{1,0:T(8,128)(2,1)S(1)} collective-permute-done((bf16[256,1024]{1,0:T(8,128)(2,1)S(1)}, bf16[256,1024]{1,0:T(8,128)(2,1)S(1)}, u32[]{:S(2)}, u32[]{:S(2)}) %collective-permute-start) | collective-permute-done | bytes 524320 | tf_op jit(solution)/shard_map/ppermute | solution.py:213
  27.5 28.4 %collective-permute-done.5 = s32[1,1024]{1,0:T(1,128)S(1)} collective-permute-done((s32[1,1024]{1,0:T(1,128)S(1)}, s32[1,1024]{1,0:T(1,128)S(1)}, u32[]{:S(2)}, u32[]{:S(2)}) %collective-permute-start.5) | collective-permute-done | bytes 4128 | tf_op jit(solution)/shard_map/ppermute | solution.py:213
  66.3 11.7 %collective-permute-done.9.got_ref = bf16[256,1024]{1,0:T(8,128)(2,1)S(1)} collective-permute-done((bf16[256,1024]{1,0:T(8,128)(2,1)S(1)}, bf16[256,1024]{1,0:T(8,128)(2,1)S(1)}, u32[]{:S(2)}, u32[]{:S(2)}) %collective-permute-start.9) | collective-permute-done | bytes 524320 | tf_op jit(solution)/shard_map/ppermute | solution.py:213
  78.0 3.6 collective-permute-done.12.refs_1_
  103.5 11.2 %normalize_all.1.normed_ref.refs_0_ = bf16[2048,2048]{1,0:T(8,128)(2,1)} custom-call(bf16[256,2048]{1,0:T(8,128)(2,1)S(1)} %copy-done.2, bf16[256,2048]{1,0:T(8,128)(2,1)} %copy-done.96, bf16[256,2048]{1,0:T(8,128)(2,1)} %copy-done.95, bf16[256,2048]{1,0:T(8,128)(2,1)} %copy-done.97, bf16[256,2048]{1,0:T(8,128)(2,1)} %copy-done.4, ...), custom_call_target="tpu_custom_call" | custom-call | flops 16777216 | bytes 262144 | tf_op jit(solution)/shard_map/normalize_all/pallas_call | solution.py:247
  117.5 8.7 %collective-permute-done.19.refs_2_ = bf16[512,512]{1,0:T(8,128)(2,1)} collective-permute-done((bf16[512,512]{1,0:T(8,128)(2,1)}, bf16[512,512]{1,0:T(8,128)(2,1)}, u32[]{:S(2)}, u32[]{:S(2)}) %collective-permute-start.19) | collective-permute-done | bytes 524320 | tf_op jit(solution)/shard_map/ppermute | solution.py:213
  135.3 3.0 place_pieces.7.refs_1_.refs_5_
  138.3 18.4 %hidden_forward.1 = (bf16[2048,1024]{1,0:T(8,128)(2,1)}, bf16[2048,1024]{1,0:T(8,128)(2,1)}) custom-call(bf16[2048,2048]{1,0:T(8,128)(2,1)} %normalize_all.1.normed_ref.refs_0_, bf16[2048,512]{1,0:T(8,128)(2,1)} %place_pieces.6.refs_0_.refs_4_, bf16[2048,512]{1,0:T(8,128)(2,1)} %place_pieces.7.refs_1_.refs_5_, f32[1,1024]{1,0:T(1,128)S(1)} %bitcast.53), custom_call_target="tpu_custom_call" | custom-call | flops 16777216 | bytes 262144 | tf_op jit(solution)/shard_map/hidden_forward/pallas_call | solution.py:247
  165.4 3.1 place_pieces.8.left_ref.refs_2_
  168.5 8.9 %stack_pieces.1 = (bf16[2048,2048]{1,0:T(8,128)(2,1)}, f32[1,2048]{1,0:T(1,128)S(1)}) custom-call(bf16[256,2048]{1,0:T(8,128)(2,1)S(1)} %copy-done.6, bf16[256,2048]{1,0:T(8,128)(2,1)} %collective-permute-done.16.refs_1_, bf16[256,2048]{1,0:T(8,128)(2,1)} %collective-permute-done.17.refs_2_, bf16[256,2048]{1,0:T(8,128)(2,1)} %collective-permute-done.21.refs_3_, ...), custom_call_target="tpu_custom_call" | custom-call | flops 16777216 | bytes 262144 | tf_op jit(solution)/shard_map/stack_pieces/pallas_call | solution.py:247
  177.5 14.6 %weight_grad.3 = (bf16[1024,512]{1,0:T(8,128)(2,1)}, bf16[1024,512]{1,0:T(8,128)(2,1)}, bf16[1024,512]{1,0:T(8,128)(2,1)}, bf16[1024,512]{1,0:T(8,128)(2,1)}) custom-call(s32[1]{0:T(128)} %bitcast.9.x_ref, bf16[2048,2048]{1,0:T(8,128)(2,1)} %get-tuple-element.358.refs_0_.grad_ref.refs_1_, bf16[2048,1024]{1,0:T(8,128)(2,1)} %get-tuple-element.343.refs_1_), custom_call_target="tpu_custom_call" | custom-call | flops 16777216 | bytes 262144 | tf_op jit(solution)/shard_map/weight_grad/pallas_call | solution.py:247
  196.7 3.1 place_pieces.9.right_ref.refs_2_.refs_3_
  199.8 15.9 %heads_inputs.1 = (f32[2048,768]{1,0:T(8,128)}, bf16[2048,256]{1,0:T(8,128)(2,1)S(1)}) custom-call(bf16[2048,2048]{1,0:T(8,128)(2,1)} %normalize_all.1.normed_ref.refs_0_, bf16[2048,2048]{1,0:T(8,128)(2,1)} %get-tuple-element.358.refs_0_.grad_ref.refs_1_, bf16[2048,512]{1,0:T(8,128)(2,1)} %place_pieces.8.left_ref.refs_2_, ...), custom_call_target="tpu_custom_call" | custom-call | flops 16777216 | bytes 262144 | tf_op jit(solution)/shard_map/heads_inputs/pallas_call | solution.py:247
  228.6 23.9 %attention_both_ways.1 = (bf16[2,2,2,256,256]{4,3,2,1,0:T(8,128)(2,1)}, bf16[2,2,2,256,768]{4,3,2,1,0:T(8,128)(2,1)}, f32[2,1,768]{2,1,0:T(1,128)}) custom-call(s32[2]{0:T(128)} %pad_add_fusion.1.place_ref, f32[2,2,2,256,768]{4,3,2,1,0:T(8,128)} %bitcast.62, bf16[2,2,2,256,256]{4,3,2,1,0:T(8,128)(2,1)} %bitcast.47, s32[2,8,128]{2,1,0:T(8,128)} %bitcast.65, ...), custom_call_target="tpu_custom_call" | custom-call | flops 16777216 | bytes 196608 | tf_op jit(solution)/shard_map/attention_both_ways/pallas_call | solution.py:160
  252.5 4.1 collective-permute-done.35.refs_3_
  259.0 3.1 place_pieces.11.refs_4_.refs_1_
  262.1 15.7 %weight_grad.4 = (bf16[1024,512]{1,0:T(8,128)(2,1)S(1)}, bf16[1024,512]{1,0:T(8,128)(2,1)}, bf16[1024,512]{1,0:T(8,128)(2,1)}, bf16[1024,512]{1,0:T(8,128)(2,1)}) custom-call(s32[1]{0:T(128)} %bitcast.9.x_ref, bf16[2048,2048]{1,0:T(8,128)(2,1)} %normalize_all.1.normed_ref.refs_0_, bf16[2048,2048]{1,0:T(8,128)(2,1)} %get-tuple-element.358.refs_0_.grad_ref.refs_1_, ...), custom_call_target="tpu_custom_call" | custom-call | flops 16777216 | bytes 262144 | tf_op jit(solution)/shard_map/weight_grad/pallas_call | solution.py:247
  277.8 10.6 %branch.2 = bf16[1024,2048]{1,0:T(8,128)(2,1)} custom-call(bf16[2048,256]{1,0:T(8,128)(2,1)S(1)} %bitcast.45, bf16[2048,1024]{1,0:T(8,128)(2,1)} %get-tuple-element.343.refs_1_, bf16[2048,512]{1,0:T(8,128)(2,1)} %place_pieces.9.right_ref.refs_2_.refs_3_, bf16[2048,512]{1,0:T(8,128)(2,1)} %place_pieces.10.refs_3_.refs_0_, ...), custom_call_target="tpu_custom_call" | custom-call | flops 16777216 | bytes 262144 | tf_op jit(solution)/shard_map/branch/pallas_call | solution.py:247
  293.2 14.7 %hidden_back.1 = (bf16[2048,1024]{1,0:T(8,128)(2,1)}, f32[1,1024]{1,0:T(1,128)S(1)}) custom-call(bf16[2048,2048]{1,0:T(8,128)(2,1)} %get-tuple-element.358.refs_0_.grad_ref.refs_1_, bf16[2048,512]{1,0:T(8,128)(2,1)} %place_pieces.10.refs_3_.refs_0_, bf16[2048,512]{1,0:T(8,128)(2,1)} %place_pieces.11.refs_4_.refs_1_, ...), custom_call_target="tpu_custom_call" | custom-call | flops 16777216 | bytes 262144 | tf_op jit(solution)/shard_map/hidden_back/pallas_call | solution.py:247
  307.9 10.3 %branch.3.kept_ref = bf16[1024,2048]{1,0:T(8,128)(2,1)} custom-call(bf16[2048,256]{1,0:T(8,128)(2,1)S(1)} %bitcast.46, bf16[2048,1024]{1,0:T(8,128)(2,1)} %get-tuple-element.343.refs_1_, bf16[2048,512]{1,0:T(8,128)(2,1)} %place_pieces.9.right_ref.refs_2_.refs_3_, bf16[2048,512]{1,0:T(8,128)(2,1)} %place_pieces.10.refs_3_.refs_0_, ...), custom_call_target="tpu_custom_call" | custom-call | flops 16777216 | bytes 262144 | tf_op jit(solution)/shard_map/branch/pallas_call | solution.py:247
  319.0 6.5 %link_stage.2 = (bf16[512,1280]{1,0:T(8,128)(2,1)}, bf16[512,1280]{1,0:T(8,128)(2,1)}, bf16[512,768]{1,0:T(8,128)(2,1)S(1)}, bf16[512,768]{1,0:T(8,128)(2,1)S(1)}) custom-call(bf16[1024,2048]{1,0:T(8,128)(2,1)} %branch.3.kept_ref, bf16[1024,2048]{1,0:T(8,128)(2,1)} %collective-permute-done.39.got_ref), custom_call_target="tpu_custom_call" | custom-call | flops 16777216 | bytes 262144 | tf_op jit(solution)/shard_map/link_stage/pallas_call | solution.py:247
  330.4 14.7 %weight_grad.5 = (bf16[1024,512]{1,0:T(8,128)(2,1)}, bf16[1024,512]{1,0:T(8,128)(2,1)}, bf16[1024,512]{1,0:T(8,128)(2,1)}, bf16[1024,512]{1,0:T(8,128)(2,1)}) custom-call(s32[1]{0:T(128)} %bitcast.9.x_ref, bf16[2048,2048]{1,0:T(8,128)(2,1)} %normalize_all.1.normed_ref.refs_0_, bf16[2048,1024]{1,0:T(8,128)(2,1)} %get-tuple-element.404.refs_1_), custom_call_target="tpu_custom_call" | custom-call | flops 16777216 | bytes 262144 | tf_op jit(solution)/shard_map/weight_grad/pallas_call | solution.py:247
  345.0 11.5 %collective-permute-done.45.got_ref = bf16[512,512]{1,0:T(8,128)(2,1)S(1)} collective-permute-done((bf16[512,512]{1,0:T(8,128)(2,1)S(1)}, bf16[512,512]{1,0:T(8,128)(2,1)S(1)}, u32[]{:S(2)}, u32[]{:S(2)}) %collective-permute-start.45) | collective-permute-done | bytes 524320 | tf_op jit(solution)/shard_map/ppermute | solution.py:213
  365.5 17.2 %token_grad.2 = (bf16[1024,2048]{1,0:T(8,128)(2,1)}, f32[2,2048]{1,0:T(2,128)S(1)}) custom-call(bf16[2048,768]{1,0:T(8,128)(2,1)} %bitcast.60, bf16[2048,1024]{1,0:T(8,128)(2,1)} %get-tuple-element.404.refs_1_, bf16[2048,512]{1,0:T(8,128)(2,1)} %place_pieces.8.left_ref.refs_2_, bf16[2048,512]{1,0:T(8,128)(2,1)} %place_pieces.9.right_ref.refs_2_.refs_3_, ...), custom_call_target="tpu_custom_call" | custom-call | flops 16777216 | bytes 262144 | tf_op jit(solution)/shard_map/token_grad/pallas_call | solution.py:247
  387.3 3.2 collective-permute-start.52
  393.0 17.0 %token_grad.3 = (bf16[1024,2048]{1,0:T(8,128)(2,1)}, f32[2,2048]{1,0:T(2,128)S(1)}) custom-call(bf16[2048,768]{1,0:T(8,128)(2,1)} %bitcast.61, bf16[2048,1024]{1,0:T(8,128)(2,1)} %get-tuple-element.404.refs_1_, bf16[2048,512]{1,0:T(8,128)(2,1)} %place_pieces.8.left_ref.refs_2_, bf16[2048,512]{1,0:T(8,128)(2,1)} %place_pieces.9.right_ref.refs_2_.refs_3_, ...), custom_call_target="tpu_custom_call" | custom-call | flops 16777216 | bytes 262144 | tf_op jit(solution)/shard_map/token_grad/pallas_call | solution.py:247
  414.9 6.9 %link_stage.3 = (bf16[512,1280]{1,0:T(8,128)(2,1)}, bf16[512,1280]{1,0:T(8,128)(2,1)}, bf16[512,768]{1,0:T(8,128)(2,1)S(1)}, bf16[512,768]{1,0:T(8,128)(2,1)}) custom-call(bf16[1024,2048]{1,0:T(8,128)(2,1)} %get-tuple-element.462.kept_ref, bf16[1024,2048]{1,0:T(8,128)(2,1)} %collective-permute-done.51.got_ref), custom_call_target="tpu_custom_call" | custom-call | flops 16777216 | bytes 262144 | tf_op jit(solution)/shard_map/link_stage/pallas_call | solution.py:247
  427.2 3.5 collective-permute-start.59
  435.8 17.1 %collective-permute-done.59.got_ref = bf16[512,512]{1,0:T(8,128)(2,1)} collective-permute-done((bf16[512,512]{1,0:T(8,128)(2,1)}, bf16[512,512]{1,0:T(8,128)(2,1)}, u32[]{:S(2)}, u32[]{:S(2)}) %collective-permute-start.59) | collective-permute-done | bytes 524320 | tf_op jit(solution)/shard_map/ppermute | solution.py:213
  458.0 3.5 collective-permute-start.60
  468.0 14.7 %collective-permute-done.64.refs_3_ = bf16[256,512]{1,0:T(8,128)(2,1)S(1)} collective-permute-done((bf16[256,512]{1,0:T(8,128)(2,1)S(1)}, bf16[256,512]{1,0:T(8,128)(2,1)S(1)}, u32[]{:S(2)}, u32[]{:S(2)}) %collective-permute-start.64) | collective-permute-done | bytes 262176 | tf_op jit(solution)/shard_map/ppermute | solution.py:213
  483.4 4.9 collective-permute-done.63.refs_3_
  (416 shorter events, 176.0 us)
Async XLA Ops:
  18.8 37.9 %collective-permute-start.4 = (bf16[256,2048]{1,0:T(8,128)(2,1)S(1)}, bf16[256,2048]{1,0:T(8,128)(2,1)S(1)}, u32[]{:S(2)}, u32[]{:S(2)}) collective-permute-start(bf16[256,2048]{1,0:T(8,128)(2,1)S(1)} %copy-done.2), channel_id=1, source_target_pairs={{0,2},{1,3},{2,0},{3,1},{4,6},{5,7},{6,4},{7,5},{8,10},{9,11},{10,... | collective-permute-start | bytes 3145736 | tf_op jit(solution)/shard_map/ppermute | solution.py:213
  20.6 36.2 %collective-permute-start.3 = (bf16[256,2048]{1,0:T(8,128)(2,1)S(1)}, bf16[256,2048]{1,0:T(8,128)(2,1)S(1)}, u32[]{:S(2)}, u32[]{:S(2)}) collective-permute-start(bf16[256,2048]{1,0:T(8,128)(2,1)S(1)} %copy-done.2), channel_id=1, source_target_pairs={{0,8},{8,0},{1,9},{9,1},{2,10},{10,2},{3,11},{11,3},{4,12},{12,4},... | collective-permute-start | bytes 3145736 | tf_op jit(solution)/shard_map/ppermute | solution.py:213
  22.2 33.8 %collective-permute-start.7 = (bf16[512,512]{1,0:T(8,128)(2,1)S(1)}, bf16[512,512]{1,0:T(8,128)(2,1)S(1)}, u32[]{:S(2)}, u32[]{:S(2)}) collective-permute-start(bf16[512,512]{1,0:T(8,128)(2,1)S(1)} %get-tuple-element.289.refs_0_), channel_id=1, source_target_pairs={{0,4},{4,0},{1,5},{5,1},{2,6},{6,2},{3,7},{7,3},{8,12},{12,8},{9,1... | collective-permute-start | bytes 1572872 | tf_op jit(solution)/shard_map/ppermute | solution.py:213
  23.6 33.1 %collective-permute-start.6 = (bf16[512,512]{1,0:T(8,128)(2,1)S(1)}, bf16[512,512]{1,0:T(8,128)(2,1)S(1)}, u32[]{:S(2)}, u32[]{:S(2)}) collective-permute-start(bf16[512,512]{1,0:T(8,128)(2,1)S(1)} %get-tuple-element.289.refs_0_), channel_id=1, source_target_pairs={{0,16},{16,0},{1,17},{17,1},{2,18},{18,2},{3,19},{19,3},{4,20},{20... | collective-permute-start | bytes 1572872 | tf_op jit(solution)/shard_map/ppermute | solution.py:213
  27.0 28.9 %collective-permute-start.5 = (s32[1,1024]{1,0:T(1,128)S(1)}, s32[1,1024]{1,0:T(1,128)S(1)}, u32[]{:S(2)}, u32[]{:S(2)}) collective-permute-start(s32[1,1024]{1,0:T(1,128)S(1)} %copy-done.110), channel_id=1, source_target_pairs={{0,8},{8,0},{1,9},{9,1},{2,10},{10,2},{3,11},{11,3},{4,12},{12,4},... | collective-permute-start | bytes 12296 | tf_op jit(solution)/shard_map/ppermute | solution.py:213
  56.8 28.3 %collective-permute-start.8 = (bf16[256,2048]{1,0:T(8,128)(2,1)S(1)}, bf16[256,2048]{1,0:T(8,128)(2,1)S(1)}, u32[]{:S(2)}, u32[]{:S(2)}) collective-permute-start(bf16[256,2048]{1,0:T(8,128)(2,1)S(1)} %collective-permute-done.3.refs_1_.refs_7_), channel_id=1, source_target_pairs={{0,2},{1,3},{2,0},{3,1},{4,6},{5,7},{6,4},{7,5},{8,10},{9,11},{10,... | collective-permute-start | bytes 3145736 | tf_op jit(solution)/shard_map/ppermute | solution.py:213
  90.7 35.6 %collective-permute-start.17 = (bf16[256,2048]{1,0:T(8,128)(2,1)S(1)}, bf16[256,2048]{1,0:T(8,128)(2,1)}, u32[]{:S(2)}, u32[]{:S(2)}) collective-permute-start(bf16[256,2048]{1,0:T(8,128)(2,1)S(1)} %copy-done.6), channel_id=1, source_target_pairs={{0,2},{1,3},{2,0},{3,1},{4,6},{5,7},{6,4},{7,5},{8,10},{9,11},{10,... | collective-permute-start | bytes 3145736 | tf_op jit(solution)/shard_map/ppermute | solution.py:213
  92.3 36.2 %collective-permute-start.16 = (bf16[256,2048]{1,0:T(8,128)(2,1)S(1)}, bf16[256,2048]{1,0:T(8,128)(2,1)}, u32[]{:S(2)}, u32[]{:S(2)}) collective-permute-start(bf16[256,2048]{1,0:T(8,128)(2,1)S(1)} %copy-done.6), channel_id=1, source_target_pairs={{0,8},{8,0},{1,9},{9,1},{2,10},{10,2},{3,11},{11,3},{4,12},{12,4},... | collective-permute-start | bytes 3145736 | tf_op jit(solution)/shard_map/ppermute | solution.py:213
  94.4 31.9 %collective-permute-start.19 = (bf16[512,512]{1,0:T(8,128)(2,1)}, bf16[512,512]{1,0:T(8,128)(2,1)}, u32[]{:S(2)}, u32[]{:S(2)}) collective-permute-start(bf16[512,512]{1,0:T(8,128)(2,1)} %get-tuple-element.324.refs_0_), channel_id=1, source_target_pairs={{0,16},{16,0},{1,17},{17,1},{2,18},{18,2},{3,19},{19,3},{4,20},{20... | collective-permute-start | bytes 1572872 | tf_op jit(solution)/shard_map/ppermute | solution.py:213
  128.5 28.3 %collective-permute-start.21 = (bf16[256,2048]{1,0:T(8,128)(2,1)}, bf16[256,2048]{1,0:T(8,128)(2,1)}, u32[]{:S(2)}, u32[]{:S(2)}) collective-permute-start(bf16[256,2048]{1,0:T(8,128)(2,1)} %collective-permute-done.16.refs_1_), channel_id=1, source_target_pairs={{0,2},{1,3},{2,0},{3,1},{4,6},{5,7},{6,4},{7,5},{8,10},{9,11},{10,... | collective-permute-start | bytes 3145736 | tf_op jit(solution)/shard_map/ppermute | solution.py:213
  129.0 27.7 %collective-permute-start.22 = (bf16[256,1024]{1,0:T(8,128)(2,1)}, bf16[256,1024]{1,0:T(8,128)(2,1)}, u32[]{:S(2)}, u32[]{:S(2)}) collective-permute-start(bf16[256,1024]{1,0:T(8,128)(2,1)} %get-tuple-element.331), channel_id=1, source_target_pairs={{0,8},{8,0},{1,9},{9,1},{2,10},{10,2},{3,11},{11,3},{4,12},{12,4},... | collective-permute-start | bytes 1572872 | tf_op jit(solution)/shard_map/ppermute | solution.py:213
  157.4 34.6 %collective-permute-start.29 = (bf16[512,512]{1,0:T(8,128)(2,1)}, bf16[512,512]{1,0:T(8,128)(2,1)S(1)}, u32[]{:S(2)}, u32[]{:S(2)}) collective-permute-start(bf16[512,512]{1,0:T(8,128)(2,1)} %collective-permute-done.24.refs_2_), channel_id=1, source_target_pairs={{0,4},{4,0},{1,5},{5,1},{2,6},{6,2},{3,7},{7,3},{8,12},{12,8},{9,1... | collective-permute-start | bytes 1572872 | tf_op jit(solution)/shard_map/ppermute | solution.py:213
  162.7 29.4 %collective-permute-start.31 = (bf16[512,512]{1,0:T(8,128)(2,1)S(1)}, bf16[512,512]{1,0:T(8,128)(2,1)S(1)}, u32[]{:S(2)}, u32[]{:S(2)}) collective-permute-start(bf16[512,512]{1,0:T(8,128)(2,1)S(1)} %get-tuple-element.357.refs_0_), channel_id=1, source_target_pairs={{0,4},{4,0},{1,5},{5,1},{2,6},{6,2},{3,7},{7,3},{8,12},{12,8},{9,1... | collective-permute-start | bytes 1572872 | tf_op jit(solution)/shard_map/ppermute | solution.py:213
  164.2 28.8 %collective-permute-start.30 = (bf16[512,512]{1,0:T(8,128)(2,1)S(1)}, bf16[512,512]{1,0:T(8,128)(2,1)}, u32[]{:S(2)}, u32[]{:S(2)}) collective-permute-start(bf16[512,512]{1,0:T(8,128)(2,1)S(1)} %get-tuple-element.357.refs_0_), channel_id=1, source_target_pairs={{0,16},{16,0},{1,17},{17,1},{2,18},{18,2},{3,19},{19,3},{4,20},{20... | collective-permute-start | bytes 1572872 | tf_op jit(solution)/shard_map/ppermute | solution.py:213
  220.3 36.3 %collective-permute-start.36 = (bf16[1024,512]{1,0:T(8,128)(2,1)}, bf16[1024,512]{1,0:T(8,128)(2,1)}, u32[]{:S(2)}, u32[]{:S(2)}) collective-permute-start(bf16[1024,512]{1,0:T(8,128)(2,1)} %get-tuple-element.378), channel_id=1, source_target_pairs={{0,4},{4,0},{1,5},{5,1},{2,6},{6,2},{3,7},{7,3},{8,12},{12,8},{9,1... | collective-permute-start | bytes 3145736 | tf_op jit(solution)/shard_map/ppermute | solution.py:213
  220.8 35.7 %collective-permute-start.35 = (bf16[512,512]{1,0:T(8,128)(2,1)}, bf16[512,512]{1,0:T(8,128)(2,1)}, u32[]{:S(2)}, u32[]{:S(2)}) collective-permute-start(bf16[512,512]{1,0:T(8,128)(2,1)} %collective-permute-done.33.refs_2_), channel_id=1, source_target_pairs={{0,4},{4,0},{1,5},{5,1},{2,6},{6,2},{3,7},{7,3},{8,12},{12,8},{9,1... | collective-permute-start | bytes 1572872 | tf_op jit(solution)/shard_map/ppermute | solution.py:213
  256.6 31.9 %collective-permute-start.38 = (bf16[1024,512]{1,0:T(8,128)(2,1)S(1)}, bf16[1024,512]{1,0:T(8,128)(2,1)S(1)}, u32[]{:S(2)}, u32[]{:S(2)}) collective-permute-start(bf16[1024,512]{1,0:T(8,128)(2,1)S(1)} %copy-done.112), channel_id=1, source_target_pairs={{0,4},{4,0},{1,5},{5,1},{2,6},{6,2},{3,7},{7,3},{8,12},{12,8},{9,1... | collective-permute-start | bytes 3145736 | tf_op jit(solution)/shard_map/ppermute | solution.py:213
  258.9 29.5 %collective-permute-start.37 = (bf16[512,512]{1,0:T(8,128)(2,1)S(1)}, bf16[512,512]{1,0:T(8,128)(2,1)S(1)}, u32[]{:S(2)}, u32[]{:S(2)}) collective-permute-start(bf16[512,512]{1,0:T(8,128)(2,1)S(1)} %get-tuple-element.389), channel_id=1, source_target_pairs={{0,16},{16,0},{1,17},{17,1},{2,18},{18,2},{3,19},{19,3},{4,20},{20... | collective-permute-start | bytes 1572872 | tf_op jit(solution)/shard_map/ppermute | solution.py:213
  288.4 30.5 %collective-permute-start.39 = (bf16[1024,2048]{1,0:T(8,128)(2,1)}, bf16[1024,2048]{1,0:T(8,128)(2,1)}, u32[]{:S(2)}, u32[]{:S(2)}) collective-permute-start(bf16[1024,2048]{1,0:T(8,128)(2,1)} %branch.2), channel_id=1, source_target_pairs={{0,1},{1,0},{2,3},{3,2},{4,5},{5,4},{6,7},{7,6},{8,9},{9,8},{10,11... | collective-permute-start | bytes 12582920 | tf_op jit(solution)/shard_map/ppermute | solution.py:213
  288.5 30.4 %collective-permute-start.40 = (bf16[1024,512]{1,0:T(8,128)(2,1)S(1)}, bf16[1024,512]{1,0:T(8,128)(2,1)S(1)}, u32[]{:S(2)}, u32[]{:S(2)}) collective-permute-start(bf16[1024,512]{1,0:T(8,128)(2,1)S(1)} %get-tuple-element.396), channel_id=1, source_target_pairs={{0,4},{4,0},{1,5},{5,1},{2,6},{6,2},{3,7},{7,3},{8,12},{12,8},{9,1... | collective-permute-start | bytes 3145736 | tf_op jit(solution)/shard_map/ppermute | solution.py:213
  290.0 28.9 %collective-permute-start.42 = (bf16[512,512]{1,0:T(8,128)(2,1)S(1)}, bf16[512,512]{1,0:T(8,128)(2,1)S(1)}, u32[]{:S(2)}, u32[]{:S(2)}) collective-permute-start(bf16[512,512]{1,0:T(8,128)(2,1)S(1)} %get-tuple-element.401), channel_id=1, source_target_pairs={{0,16},{16,0},{1,17},{17,1},{2,18},{18,2},{3,19},{19,3},{4,20},{20... | collective-permute-start | bytes 1572872 | tf_op jit(solution)/shard_map/ppermute | solution.py:213
  325.5 31.9 %collective-permute-start.43 = (bf16[512,1280]{1,0:T(8,128)(2,1)}, bf16[512,1280]{1,0:T(8,128)(2,1)S(1)}, u32[]{:S(2)}, u32[]{:S(2)}) collective-permute-start(bf16[512,1280]{1,0:T(8,128)(2,1)} %get-tuple-element.410), channel_id=1, source_target_pairs={{0,2},{1,3},{2,0},{3,1},{4,6},{5,7},{6,4},{7,5},{8,10},{9,11},{10,... | collective-permute-start | bytes 3932168 | tf_op jit(solution)/shard_map/ppermute | solution.py:213
  327.0 30.3 %collective-permute-start.46 = (bf16[1024,512]{1,0:T(8,128)(2,1)S(1)}, bf16[1024,512]{1,0:T(8,128)(2,1)S(1)}, u32[]{:S(2)}, u32[]{:S(2)}) collective-permute-start(bf16[1024,512]{1,0:T(8,128)(2,1)S(1)} %copy-done.114), channel_id=1, source_target_pairs={{0,4},{4,0},{1,5},{5,1},{2,6},{6,2},{3,7},{7,3},{8,12},{12,8},{9,1... | collective-permute-start | bytes 3145736 | tf_op jit(solution)/shard_map/ppermute | solution.py:213
  327.3 30.0 %collective-permute-start.44 = (bf16[512,768]{1,0:T(8,128)(2,1)S(1)}, bf16[512,768]{1,0:T(8,128)(2,1)S(1)}, u32[]{:S(2)}, u32[]{:S(2)}) collective-permute-start(bf16[512,768]{1,0:T(8,128)(2,1)S(1)} %get-tuple-element.412), channel_id=1, source_target_pairs={{0,8},{8,0},{1,9},{9,1},{2,10},{10,2},{3,11},{11,3},{4,12},{12,4},... | collective-permute-start | bytes 2359304 | tf_op jit(solution)/shard_map/ppermute | solution.py:213
  357.4 29.3 %collective-permute-start.49 = (bf16[1024,512]{1,0:T(8,128)(2,1)}, bf16[1024,512]{1,0:T(8,128)(2,1)S(1)}, u32[]{:S(2)}, u32[]{:S(2)}) collective-permute-start(bf16[1024,512]{1,0:T(8,128)(2,1)} %get-tuple-element.432), channel_id=1, source_target_pairs={{0,4},{4,0},{1,5},{5,1},{2,6},{6,2},{3,7},{7,3},{8,12},{12,8},{9,1... | collective-permute-start | bytes 3145736 | tf_op jit(solution)/shard_map/ppermute | solution.py:213
  386.7 28.2 %collective-permute-start.51 = (bf16[1024,2048]{1,0:T(8,128)(2,1)}, bf16[1024,2048]{1,0:T(8,128)(2,1)}, u32[]{:S(2)}, u32[]{:S(2)}) collective-permute-start(bf16[1024,2048]{1,0:T(8,128)(2,1)} %get-tuple-element.439), channel_id=1, source_target_pairs={{0,1},{1,0},{2,3},{3,2},{4,5},{5,4},{6,7},{7,6},{8,9},{9,8},{10,11... | collective-permute-start | bytes 12582920 | tf_op jit(solution)/shard_map/ppermute | solution.py:213
  386.7 28.2 %collective-permute-start.53 = (bf16[1024,512]{1,0:T(8,128)(2,1)S(1)}, bf16[1024,512]{1,0:T(8,128)(2,1)S(1)}, u32[]{:S(2)}, u32[]{:S(2)}) collective-permute-start(bf16[1024,512]{1,0:T(8,128)(2,1)S(1)} %copy-done.113), channel_id=1, source_target_pairs={{0,4},{4,0},{1,5},{5,1},{2,6},{6,2},{3,7},{7,3},{8,12},{12,8},{9,1... | collective-permute-start | bytes 3145736 | tf_op jit(solution)/shard_map/ppermute | solution.py:213
  387.3 26.7 %collective-permute-start.52 = (bf16[512,512]{1,0:T(8,128)(2,1)S(1)}, bf16[512,512]{1,0:T(8,128)(2,1)S(1)}, u32[]{:S(2)}, u32[]{:S(2)}) collective-permute-start(bf16[512,512]{1,0:T(8,128)(2,1)S(1)} %get-tuple-element.447), channel_id=1, source_target_pairs={{0,16},{16,0},{1,17},{17,1},{2,18},{18,2},{3,19},{19,3},{4,20},{20... | collective-permute-start | bytes 1572872 | tf_op jit(solution)/shard_map/ppermute | solution.py:213
  421.8 31.9 %collective-permute-start.57 = (bf16[512,1280]{1,0:T(8,128)(2,1)}, bf16[512,1280]{1,0:T(8,128)(2,1)}, u32[]{:S(2)}, u32[]{:S(2)}) collective-permute-start(bf16[512,1280]{1,0:T(8,128)(2,1)} %get-tuple-element.465), channel_id=1, source_target_pairs={{0,2},{1,3},{2,0},{3,1},{4,6},{5,7},{6,4},{7,5},{8,10},{9,11},{10,... | collective-permute-start | bytes 3932168 | tf_op jit(solution)/shard_map/ppermute | solution.py:213
  422.9 30.8 %collective-permute-start.58 = (bf16[512,768]{1,0:T(8,128)(2,1)}, bf16[512,768]{1,0:T(8,128)(2,1)}, u32[]{:S(2)}, u32[]{:S(2)}) collective-permute-start(bf16[512,768]{1,0:T(8,128)(2,1)} %get-tuple-element.467), channel_id=1, source_target_pairs={{0,8},{8,0},{1,9},{9,1},{2,10},{10,2},{3,11},{11,3},{4,12},{12,4},... | collective-permute-start | bytes 2359304 | tf_op jit(solution)/shard_map/ppermute | solution.py:213
  458.0 34.1 %collective-permute-start.60 = (bf16[256,1280]{1,0:T(8,128)(2,1)S(1)}, bf16[256,1280]{1,0:T(8,128)(2,1)S(1)}, u32[]{:S(2)}, u32[]{:S(2)}) collective-permute-start(bf16[256,1280]{1,0:T(8,128)(2,1)S(1)} %get-tuple-element.480), channel_id=1, source_target_pairs={{0,8},{8,0},{1,9},{9,1},{2,10},{10,2},{3,11},{11,3},{4,12},{12,4},... | collective-permute-start | bytes 1966088 | tf_op jit(solution)/shard_map/ppermute | solution.py:213
  461.4 30.6 %collective-permute-start.61 = (bf16[256,768]{1,0:T(8,128)(2,1)S(1)}, bf16[256,768]{1,0:T(8,128)(2,1)S(1)}, u32[]{:S(2)}, u32[]{:S(2)}) collective-permute-start(bf16[256,768]{1,0:T(8,128)(2,1)S(1)} %get-tuple-element.482), channel_id=1, source_target_pairs={{0,2},{1,3},{2,0},{3,1},{4,6},{5,7},{6,4},{7,5},{8,10},{9,11},{10,... | collective-permute-start | bytes 1179656 | tf_op jit(solution)/shard_map/ppermute | solution.py:213
  (155 other events, 1948.9 us)
